TPU v7x, 32 devices: a whole 2x2x4 slice. The times are simulated.
32 devices in a mesh: shard: 8 (over y, x, core), replica: 4 (over z).
Axes of the slice: x: 2, y: 2, z: 4, core: 2. Of those that a mesh axis runs over, the one named last changes fastest.
Arguments:
- hidden: bfloat16 [8192, 768], P(('replica', 'shard')), may hold values from -6 to 6
- segment_ids: int32 [8192], P(('replica', 'shard')), may hold values from 0 to 63, as said below
- w_qkv: bfloat16 [768, 2304], P('shard'), may hold values from -0.21875 to 0.21875
- b_qv: bfloat16 [2, 768], P(None, 'shard'), may hold values from -3 to 3
- w_out: bfloat16 [768, 768], P('shard'), may hold values from -3 to 3
- b_out: bfloat16 [768], P('shard'), may hold values from -3 to 3
- gain1: bfloat16 [768], P('shard'), may hold values from 0.5 to 1.5
- shift1: bfloat16 [768], P('shard'), may hold values from -3 to 3
- w_in: bfloat16 [768, 3072], P('shard'), may hold values from -0.21875 to 0.21875
- b_in: bfloat16 [3072], P('shard'), may hold values from -3 to 3
- w_back: bfloat16 [3072, 768], P('shard'), may hold values from -0.21875 to 0.21875
- b_back: bfloat16 [768], P('shard'), may hold values from -3 to 3
- gain2: bfloat16 [768], P('shard'), may hold values from 0.5 to 1.5
- shift2: bfloat16 [768], P('shard'), may hold values from -3 to 3
- cotangent: float32 [8192, 768], P(('replica', 'shard')), may hold values from -6 to 6
Outputs:
- output: bfloat16 [8192, 768], P(('replica', 'shard'))
- d_hidden: float32 [8192, 768], P(('replica', 'shard'))
- grad_w_qkv: float32 [768, 2304], P('shard')
- grad_b_qv: float32 [2, 768], P(None, 'shard')
- grad_w_out: float32 [768, 768], P('shard')
- grad_b_out: float32 [768], P('shard')
- grad_gain1: float32 [768], P('shard')
- grad_shift1: float32 [768], P('shard')
- grad_w_in: float32 [768, 3072], P('shard')
- grad_b_in: float32 [3072], P('shard')
- grad_w_back: float32 [3072, 768], P('shard')
- grad_b_back: float32 [768], P('shard')
- grad_gain2: float32 [768], P('shard')
- grad_shift2: float32 [768], P('shard')
Inputs may be any that keep to these rules, and one draw needn't show every extreme that they name: `segment_ids`: ids never fall along the tokens. Sequence s (tokens s * 2048 to (s + 1) * 2048 - 1) holds exactly 16 documents with ids s * 16 to s * 16 + 15, one of them 1280 tokens long.
All inputs are finite; a program needn't handle non-finite values.
Results may differ from a plain program's by a relative error of at most 0.023.
Values may be sent and summed in bfloat16 or wider, within the bound.
A program may use at most 192 MiB of HBM per device.

v0:
```python
import math

import jax
import jax.numpy as jnp
from jax import lax
from jax.sharding import PartitionSpec as P

HEADS = 12


scale_factor = 0.125
norm_epsilon = 1e-05
masked_value = -1e30


def normalize(resid, gain, shift):
    mean_value = jnp.mean(resid, axis=-1, keepdims=True)
    centered = resid - mean_value
    variance = jnp.mean(centered * centered, axis=-1, keepdims=True)
    return centered * lax.rsqrt(variance + norm_epsilon) * gain + shift


def gelu_exact(values):
    return jax.nn.gelu(values, approximate=False)


def keep_state(state):
    return state


def block_size(count):
    return math.gcd(count, 512)


def masked_scores(query_heads, key_heads, query_segs, key_segs):
    scores = (
        jnp.einsum("qhd,khd->hqk", query_heads, key_heads, preferred_element_type=jnp.float32)
        * scale_factor
    )
    allowed = query_segs[:, None] == key_segs[None, :]
    return (scores, allowed[None])


def grad_block(
    query_heads, dctx_heads, log_total, delta, query_segs, key_heads, value_heads, key_segs
):
    scores, allowed = masked_scores(query_heads, key_heads, query_segs, key_segs)
    probs = jnp.where(allowed, jnp.exp(scores - log_total[:, :, None]), 0.0)
    d_prob = jnp.einsum("qhd,khd->hqk", dctx_heads, value_heads, preferred_element_type=jnp.float32)
    d_scores = (probs * (d_prob - delta[:, :, None])).astype(jnp.bfloat16)
    return (probs.astype(jnp.bfloat16), d_scores)


def body(
    hidden,
    segment_ids,
    w_qkv,
    b_qv,
    w_out,
    b_out,
    gain1,
    shift1,
    w_in,
    b_in,
    w_back,
    b_back,
    gain2,
    shift2,
    cotangent,
):
    tok_rows, width = hidden.shape
    heads = HEADS
    head_dim = width // heads
    seg_low = segment_ids[0]
    seg_high = segment_ids[-1]
    wq_full, wo_full, bqv_full, bo_full, g1_full, s1_full = (
        lax.all_gather(w_qkv, "shard", axis=0, tiled=True),
        lax.all_gather(w_out, "shard", axis=0, tiled=True),
        lax.all_gather(b_qv, "shard", axis=1, tiled=True),
        lax.all_gather(b_out, "shard", axis=0, tiled=True),
        lax.all_gather(gain1, "shard", axis=0, tiled=True),
        lax.all_gather(shift1, "shard", axis=0, tiled=True),
    )
    qkv = jnp.dot(hidden, wq_full, preferred_element_type=jnp.float32)
    bqv_wide = bqv_full.astype(jnp.float32)
    query = (qkv[:, :width] + bqv_wide[0]).astype(jnp.bfloat16)
    keys = qkv[:, width : 2 * width].astype(jnp.bfloat16)
    values = (qkv[:, 2 * width :] + bqv_wide[1]).astype(jnp.bfloat16)
    query_heads = query.reshape(tok_rows, heads, head_dim)
    key_local = keys.reshape(tok_rows, heads, head_dim)
    value_local = values.reshape(tok_rows, heads, head_dim)
    start_state = (
        jnp.full((heads, tok_rows), masked_value, jnp.float32),
        jnp.zeros((heads, tok_rows), jnp.float32),
        jnp.zeros((tok_rows, heads, head_dim), jnp.float32),
    )
    key_piece = lax.all_gather(keys, "shard", axis=0, tiled=True)
    value_piece = lax.all_gather(values, "shard", axis=0, tiled=True)
    seg_piece = lax.all_gather(segment_ids, "shard", axis=0, tiled=True)
    count = key_piece.shape[0]
    block = block_size(count)

    def forward_step(index, state):
        offset = index * block
        key_heads = lax.dynamic_slice_in_dim(key_piece, offset, block, 0).reshape(
            block, heads, head_dim
        )
        value_heads = lax.dynamic_slice_in_dim(value_piece, offset, block, 0).reshape(
            block, heads, head_dim
        )
        key_segs = lax.dynamic_slice_in_dim(seg_piece, offset, block, 0)

        def forward_update(state):
            running_max, running_sum, accum = state
            scores, allowed = masked_scores(query_heads, key_heads, segment_ids, key_segs)
            new_max = jnp.maximum(
                running_max, jnp.max(jnp.where(allowed, scores, masked_value), axis=-1)
            )
            factor = jnp.exp(running_max - new_max)
            weights = jnp.where(allowed, jnp.exp(scores - new_max[:, :, None]), 0.0)
            running_sum = running_sum * factor + jnp.sum(weights, axis=-1)
            accum = accum * factor.T[:, :, None] + jnp.einsum(
                "hqk,khd->qhd",
                weights.astype(jnp.bfloat16),
                value_heads,
                preferred_element_type=jnp.float32,
            )
            return (new_max, running_sum, accum)

        touches = jnp.logical_and(key_segs[0] <= seg_high, key_segs[-1] >= seg_low)
        return lax.cond(touches, forward_update, keep_state, state)

    running_max, running_sum, accum = lax.fori_loop(0, count // block, forward_step, start_state)
    context32 = accum / running_sum.T[:, :, None]
    log_total = running_max + jnp.log(running_sum)
    context = context32.reshape(tok_rows, width).astype(jnp.bfloat16)
    resid1 = (
        hidden.astype(jnp.float32)
        + jnp.dot(context, wo_full, preferred_element_type=jnp.float32)
        + bo_full.astype(jnp.float32)
    )
    normed1, norm1_pull = jax.vjp(
        normalize, resid1, g1_full.astype(jnp.float32), s1_full.astype(jnp.float32)
    )
    wi_full, bi_full, wb_full, bb_full, g2_full, s2_full = (
        lax.all_gather(w_in, "shard", axis=0, tiled=True),
        lax.all_gather(b_in, "shard", axis=0, tiled=True),
        lax.all_gather(w_back, "shard", axis=0, tiled=True),
        lax.all_gather(b_back, "shard", axis=0, tiled=True),
        lax.all_gather(gain2, "shard", axis=0, tiled=True),
        lax.all_gather(shift2, "shard", axis=0, tiled=True),
    )
    normed1_low = normed1.astype(jnp.bfloat16)
    pre = jnp.dot(normed1_low, wi_full, preferred_element_type=jnp.float32) + bi_full.astype(
        jnp.float32
    )
    act, gelu_pull = jax.vjp(gelu_exact, pre)
    act_low = act.astype(jnp.bfloat16)
    resid2 = (
        normed1
        + jnp.dot(act_low, wb_full, preferred_element_type=jnp.float32)
        + bb_full.astype(jnp.float32)
    )
    out32, norm2_pull = jax.vjp(
        normalize, resid2, g2_full.astype(jnp.float32), s2_full.astype(jnp.float32)
    )
    output = out32.astype(jnp.bfloat16)
    d_resid2, grad_gain2, grad_shift2 = norm2_pull(cotangent)
    d_branch2 = d_resid2.astype(jnp.bfloat16)
    grad_b_back = jnp.sum(d_resid2, axis=0)
    grad_w_back = jnp.einsum("tf,td->fd", act_low, d_branch2, preferred_element_type=jnp.float32)
    d_act = jnp.einsum("td,fd->tf", d_branch2, wb_full, preferred_element_type=jnp.float32)
    (d_pre,) = gelu_pull(d_act)
    grad_b_in = jnp.sum(d_pre, axis=0)
    d_pre_low = d_pre.astype(jnp.bfloat16)
    grad_w_in = jnp.einsum("td,tf->df", normed1_low, d_pre_low, preferred_element_type=jnp.float32)
    d_normed1 = d_resid2 + jnp.einsum(
        "tf,df->td", d_pre_low, wi_full, preferred_element_type=jnp.float32
    )
    d_resid1, grad_gain1, grad_shift1 = norm1_pull(d_normed1)
    grad_b_out = jnp.sum(d_resid1, axis=0)
    d_branch1 = d_resid1.astype(jnp.bfloat16)
    grad_w_out = jnp.einsum("tc,td->cd", context, d_branch1, preferred_element_type=jnp.float32)
    d_context = jnp.einsum(
        "td,cd->tc", d_branch1, wo_full, preferred_element_type=jnp.float32
    ).astype(jnp.bfloat16)
    dctx_heads = d_context.reshape(tok_rows, heads, head_dim)
    delta = jnp.einsum("qhd,qhd->hq", dctx_heads.astype(jnp.float32), context32)
    zero_heads = jnp.zeros((tok_rows, heads, head_dim), jnp.float32)
    query_key_piece = lax.all_gather(keys, "shard", axis=0, tiled=True)
    query_value_piece = lax.all_gather(values, "shard", axis=0, tiled=True)
    query_seg_piece = lax.all_gather(segment_ids, "shard", axis=0, tiled=True)
    count = query_key_piece.shape[0]
    query_block = block_size(count)

    def query_step(index, summed):
        offset = index * query_block
        key_heads = lax.dynamic_slice_in_dim(query_key_piece, offset, query_block, 0).reshape(
            query_block, heads, head_dim
        )
        value_heads = lax.dynamic_slice_in_dim(query_value_piece, offset, query_block, 0).reshape(
            query_block, heads, head_dim
        )
        key_segs = lax.dynamic_slice_in_dim(query_seg_piece, offset, query_block, 0)

        def query_update(summed):
            probs, d_scores = grad_block(
                query_heads,
                dctx_heads,
                log_total,
                delta,
                segment_ids,
                key_heads,
                value_heads,
                key_segs,
            )
            return (
                summed
                + jnp.einsum(
                    "hqk,khd->qhd", d_scores, key_heads, preferred_element_type=jnp.float32
                )
                * scale_factor
            )

        touches = jnp.logical_and(key_segs[0] <= seg_high, key_segs[-1] >= seg_low)
        return lax.cond(touches, query_update, keep_state, summed)

    d_query = lax.fori_loop(0, count // query_block, query_step, zero_heads)
    all_log_total, all_delta = (
        lax.all_gather(log_total, "shard", axis=1, tiled=True),
        lax.all_gather(delta, "shard", axis=1, tiled=True),
    )
    query_piece = lax.all_gather(query, "shard", axis=0, tiled=True)
    dctx_piece = lax.all_gather(d_context, "shard", axis=0, tiled=True)
    key_seg_piece = lax.all_gather(segment_ids, "shard", axis=0, tiled=True)
    count = query_piece.shape[0]
    key_block = block_size(count)

    def key_step(index, state):
        offset = index * key_block
        piece_query = lax.dynamic_slice_in_dim(query_piece, offset, key_block, 0).reshape(
            key_block, heads, head_dim
        )
        piece_dctx = lax.dynamic_slice_in_dim(dctx_piece, offset, key_block, 0).reshape(
            key_block, heads, head_dim
        )
        piece_segs = lax.dynamic_slice_in_dim(key_seg_piece, offset, key_block, 0)
        piece_log = lax.dynamic_slice_in_dim(all_log_total, offset, key_block, 1)
        piece_delta = lax.dynamic_slice_in_dim(all_delta, offset, key_block, 1)

        def key_update(state):
            d_key, d_value = state
            probs, d_scores = grad_block(
                piece_query,
                piece_dctx,
                piece_log,
                piece_delta,
                piece_segs,
                key_local,
                value_local,
                segment_ids,
            )
            d_key = (
                d_key
                + jnp.einsum(
                    "hqk,qhd->khd", d_scores, piece_query, preferred_element_type=jnp.float32
                )
                * scale_factor
            )
            d_value = d_value + jnp.einsum(
                "hqk,qhd->khd", probs, piece_dctx, preferred_element_type=jnp.float32
            )
            return (d_key, d_value)

        touches = jnp.logical_and(piece_segs[0] <= seg_high, piece_segs[-1] >= seg_low)
        return lax.cond(touches, key_update, keep_state, state)

    d_key_heads, d_value_heads = lax.fori_loop(
        0, count // key_block, key_step, (zero_heads, zero_heads)
    )
    d_keys = d_key_heads.reshape(tok_rows, width)
    d_values = d_value_heads.reshape(tok_rows, width)
    d_query = d_query.reshape(tok_rows, width)
    grad_b_qv = jnp.stack([jnp.sum(d_query, axis=0), jnp.sum(d_values, axis=0)], axis=0)
    d_qkv = jnp.concatenate([d_query, d_keys, d_values], axis=1).astype(jnp.bfloat16)
    grad_w_qkv = jnp.einsum("td,te->de", hidden, d_qkv, preferred_element_type=jnp.float32)
    d_hidden = d_resid1 + jnp.einsum(
        "te,de->td", d_qkv, wq_full, preferred_element_type=jnp.float32
    )
    local_grads = (
        grad_w_qkv,
        grad_b_qv,
        grad_w_out,
        grad_b_out,
        grad_gain1,
        grad_shift1,
        grad_w_in,
        grad_b_in,
        grad_w_back,
        grad_b_back,
        grad_gain2,
        grad_shift2,
    )
    shard_grads = (
        lax.psum_scatter(
            local_grads[0].astype(jnp.bfloat16), "shard", scatter_dimension=0, tiled=True
        ).astype(jnp.float32),
        lax.psum_scatter(
            local_grads[1].astype(jnp.bfloat16), "shard", scatter_dimension=1, tiled=True
        ).astype(jnp.float32),
        lax.psum_scatter(
            local_grads[2].astype(jnp.bfloat16), "shard", scatter_dimension=0, tiled=True
        ).astype(jnp.float32),
        lax.psum_scatter(
            local_grads[3].astype(jnp.bfloat16), "shard", scatter_dimension=0, tiled=True
        ).astype(jnp.float32),
        lax.psum_scatter(
            local_grads[4].astype(jnp.bfloat16), "shard", scatter_dimension=0, tiled=True
        ).astype(jnp.float32),
        lax.psum_scatter(
            local_grads[5].astype(jnp.bfloat16), "shard", scatter_dimension=0, tiled=True
        ).astype(jnp.float32),
        lax.psum_scatter(
            local_grads[6].astype(jnp.bfloat16), "shard", scatter_dimension=0, tiled=True
        ).astype(jnp.float32),
        lax.psum_scatter(
            local_grads[7].astype(jnp.bfloat16), "shard", scatter_dimension=0, tiled=True
        ).astype(jnp.float32),
        lax.psum_scatter(
            local_grads[8].astype(jnp.bfloat16), "shard", scatter_dimension=0, tiled=True
        ).astype(jnp.float32),
        lax.psum_scatter(
            local_grads[9].astype(jnp.bfloat16), "shard", scatter_dimension=0, tiled=True
        ).astype(jnp.float32),
        lax.psum_scatter(
            local_grads[10].astype(jnp.bfloat16), "shard", scatter_dimension=0, tiled=True
        ).astype(jnp.float32),
        lax.psum_scatter(
            local_grads[11].astype(jnp.bfloat16), "shard", scatter_dimension=0, tiled=True
        ).astype(jnp.float32),
    )
    total_grads = (
        lax.psum(shard_grads[0].astype(jnp.bfloat16), "replica").astype(jnp.float32),
        lax.psum(shard_grads[1].astype(jnp.bfloat16), "replica").astype(jnp.float32),
        lax.psum(shard_grads[2].astype(jnp.bfloat16), "replica").astype(jnp.float32),
        lax.psum(shard_grads[3].astype(jnp.bfloat16), "replica").astype(jnp.float32),
        lax.psum(shard_grads[4].astype(jnp.bfloat16), "replica").astype(jnp.float32),
        lax.psum(shard_grads[5].astype(jnp.bfloat16), "replica").astype(jnp.float32),
        lax.psum(shard_grads[6].astype(jnp.bfloat16), "replica").astype(jnp.float32),
        lax.psum(shard_grads[7].astype(jnp.bfloat16), "replica").astype(jnp.float32),
        lax.psum(shard_grads[8].astype(jnp.bfloat16), "replica").astype(jnp.float32),
        lax.psum(shard_grads[9].astype(jnp.bfloat16), "replica").astype(jnp.float32),
        lax.psum(shard_grads[10].astype(jnp.bfloat16), "replica").astype(jnp.float32),
        lax.psum(shard_grads[11].astype(jnp.bfloat16), "replica").astype(jnp.float32),
    )
    return (output, d_hidden) + tuple(total_grads)


def solution(mesh):
    in_specs = (
        P(("replica", "shard"), None),
        P(("replica", "shard")),
        P("shard", None),
        P(None, "shard"),
        P("shard", None),
        P("shard"),
        P("shard"),
        P("shard"),
        P("shard", None),
        P("shard"),
        P("shard", None),
        P("shard"),
        P("shard"),
        P("shard"),
        P(("replica", "shard"), None),
    )
    out_specs = (
        P(("replica", "shard"), None),
        P(("replica", "shard"), None),
        P("shard", None),
        P(None, "shard"),
        P("shard", None),
        P("shard"),
        P("shard"),
        P("shard"),
        P("shard", None),
        P("shard"),
        P("shard", None),
        P("shard"),
        P("shard"),
        P("shard"),
    )
    return jax.shard_map(body, mesh=mesh, in_specs=in_specs, out_specs=out_specs, check_vma=False)
```

profile of v0, /device:TPU:0, one launch (start us, length us, event | category | flops | bytes accessed | tf_op | source)
XLA Modules:
  0.0 788.5 jit_solution(2066285224074038387)
XLA Ops:
  8.0 38.5 %all-gather.12.cloned.1.call-done = bf16[768,2304]{1,0:T(8,128)(2,1)} async-done(((bf16[96,2304]{1,0:T(8,128)(2,1)}), bf16[768,2304]{1,0:T(8,128)(2,1)}) %all-gather.12.cloned.1.call-update) | async-done | bytes 3538960 | tf_op jit(solution)/shard_map/all_gather | solution.py:77
  46.5 3.2 fusion.93
  50.7 8.7 %all-gather.1 = bf16[8,96,2]{1,2,0:T(2,128)(2,1)S(1)} all-gather(bf16[1,96,2]{1,2,0:T(2,128)(2,1)S(1)} %bitcast.172), channel_id=1, replica_groups=mesh['shard'=8,'replica'=4] {'shard'}, dimensions={0}, use_global_device_ids=true | all-gather | bytes 3456 | tf_op jit(solution)/shard_map/all_gather | solution.py:79
  64.7 24.2 %all-reduce.14 = (bf16[768]{0:T(1024)(128)(2,1)S(1)}, bf16[768]{0:T(1024)(128)(2,1)S(1)}, bf16[768]{0:T(1024)(128)(2,1)S(1)}, bf16[768]{0:T(1024)(128)(2,1)S(1)}, bf16[768]{0:T(1024)(128)(2,1)S(1)}) all-reduce(bf16[768]{0:T(1024)(128)(2,1)S(1)} %dynamic-update-slice, ...), channel_id=1, replica_groups=mesh['shard'=8,'replica'=4] {'shard'}, use_global_device_ids=true, to_apply=%add | all-reduce | flops 3840 | bytes 15360
  88.8 8.1 %all-gather.2 = bf16[8,1,384]{2,1,0:T(2,128)(2,1)S(1)} all-gather(bf16[1,1,384]{2,1,0:T(2,128)(2,1)S(1)} %reshape.302), channel_id=1, replica_groups=mesh['shard'=8,'replica'=4] {'shard'}, dimensions={0}, use_global_device_ids=true | all-gather | bytes 6912 | tf_op jit(solution)/shard_map/all_gather | solution.py:147
  97.0 8.8 %all-gather = s32[8,1,256]{2,1,0:T(1,128)} all-gather(s32[1,1,256]{2,1,0:T(1,128)S(1)} %bitcast.168), channel_id=1, replica_groups=mesh['shard'=8,'replica'=4] {'shard'}, dimensions={0}, use_global_device_ids=true | all-gather | bytes 9216 | tf_op jit(solution)/shard_map/all_gather | solution.py:99
  107.3 4.6 copy.72
  111.9 5.9 all-gather.16.cloned.1.call-done
  117.8 4.8 copy.73
  122.7 21.6 %while.48 = (s32[]{:T(128)}, f32[12,256]{1,0:T(8,128)S(1)}, f32[12,256]{1,0:T(8,128)S(1)}, f32[256,12,64]{0,2,1:T(8,128)S(1)}, s32[2048]{0:T(1024)}, /*index=5*/...) while((s32[]{:T(128)}, f32[12,256]{1,0:T(8,128)S(1)}, ...), condition=%wide.region_5.6_spmd, body=%wide.region_0.5_spmd.sunk | while | flops 420488192 | bytes 26287476 | solution.py:133
  126.7 5.7 conditional.6
  147.0 37.0 %all-gather.20.cloned.1.call-done = bf16[768,3072]{1,0:T(8,128)(2,1)} async-done(((bf16[96,3072]{1,0:T(8,128)(2,1)}), bf16[768,3072]{1,0:T(8,128)(2,1)}) %all-gather.20.cloned.1.call-update) | async-done | bytes 4718608 | tf_op jit(solution)/shard_map/all_gather | solution.py:146
  184.0 11.8 %multiply_convert_fusion.8 = (bf16[256,3072]{1,0:T(8,128)(2,1)}, f32[256,3072]{1,0:T(8,128)}, f32[256,3072]{1,0:T(8,128)}) fusion(f32[3072]{0:T(1024)S(1)} %bitcast.171, bf16[768,3072]{1,0:T(8,128)(2,1)} %all-gather.20.cloned.1.call-done, f32[256,768]{1,0:T(8,128)S(1)} %get-tuple-element.1246, f32[768]{0:T(1024)S(1)} %convert_element_type.209, ...), kind=kOutput, calls=%fused_computation.63 | convolution fusion | flops 1260847104 | bytes 13389824 | tf_op jit(solution)/shard_map/dot_general | solution.py:154
  195.8 28.8 %all-gather.22.cloned.1.call-done = bf16[3072,768]{1,0:T(8,128)(2,1)} async-done(((bf16[384,768]{1,0:T(8,128)(2,1)}), bf16[3072,768]{1,0:T(8,128)(2,1)}) %all-gather.22.cloned.1.call-update) | async-done | bytes 4718608 | tf_op jit(solution)/shard_map/all_gather | solution.py:148
  224.6 4.5 fusion.89
  231.5 2.8 fusion.90
  234.3 2.3 multiply_reduce_fusion.1
  242.4 16.3 %all-gather.24.cloned.1.call-done = bf16[2048,768]{1,0:T(8,128)(2,1)} async-done(((bf16[256,768]{1,0:T(8,128)(2,1)}), bf16[2048,768]{1,0:T(8,128)(2,1)}) %all-gather.24.cloned.1.call-update) | async-done | bytes 3145744 | tf_op jit(solution)/shard_map/all_gather | solution.py:233
  258.7 4.8 copy.79
  264.1 9.3 %all_gather.77 = f32[12,2048]{1,0:T(8,128)S(1)} all-gather(f32[12,256]{1,0:T(8,128)} %log_add_fusion), channel_id=1, replica_groups=mesh['shard'=8,'replica'=4] {'shard'}, dimensions={1}, use_global_device_ids=true | all-gather | bytes 110592 | tf_op jit(solution)/shard_map/all_gather | solution.py:230
  275.1 8.6 %all_gather.79 = f32[12,2048]{1,0:T(8,128)S(1)} all-gather(f32[12,256]{1,0:T(8,128)} %fusion.66), channel_id=1, replica_groups=mesh['shard'=8,'replica'=4] {'shard'}, dimensions={1}, use_global_device_ids=true | all-gather | bytes 110592 | tf_op jit(solution)/shard_map/all_gather | solution.py:231
  284.6 28.3 %while.49 = (s32[]{:T(128)}, f32[256,12,64]{0,2,1:T(8,128)}, s32[2048]{0:T(1024)}, s32[]{:T(128)}, s32[]{:T(128)}, /*index=5*/s32[256]{0:T(256)}, bf16[2048,768]...) while((s32[]{:T(128)}, f32[256,12,64]{0,2,1:T(8,128)}, ...), condition=%wide.region_17.18_spmd, body=%wide.region_14.17_spmd.sunk | while | flops 613941248 | bytes 20745584 | solution.py:228
  288.9 11.8 %conditional.7 = (f32[256,12,64]{0,2,1:T(8,128)}) conditional(s32[]{:T(128)} %convert_element_type.315, f32[256,12,64]{0,2,1:T(8,128)} %get-tuple-element.1570, (s32[256]{0:T(256)}, s32[512]{0:T(512)S(1)}, bf16[2048,768]{0,1:T(8,128)(2,1)}, s32[]{:T(128)}, bf16[256,12,64]{0,2,1:T(8,128)(2,1)S(1)}, /*index=5*/f32[12,256]{1,0:T(8,128)}, ...), branch_computations={%region_15.15_spmd, %region_16.16_spmd} | conditional | flops 613941248 | bytes 20741160 | solution.py:226
  290.4 3.7 fusion.91
  294.3 6.4 fusion.29
  313.0 4.6 copy.80
  319.6 32.8 %while.50 = (s32[]{:T(128)}, f32[256,12,64]{0,2,1:T(8,128)}, f32[256,12,64]{0,2,1:T(8,128)}, s32[2048]{0:T(1024)}, s32[]{:T(128)}, /*index=5*/s32[]{:T(128)}, s3...) while((s32[]{:T(128)}, f32[256,12,64]{0,2,1:T(8,128)}, ...), condition=%wide.region_21.22_spmd, body=%wide.region_18.21_spmd.sunk | while | flops 821755904 | bytes 29670792 | solution.py:278
  323.5 16.9 %conditional.8 = ((f32[256,12,64]{0,2,1:T(8,128)}, f32[256,12,64]{0,2,1:T(8,128)})) conditional(s32[]{:T(128)} %convert_element_type.316, (f32[256,12,64]{0,2,1:T(8,128)}, f32[256,12,64]{0,2,1:T(8,128)}) %tuple.174, (s32[512]{0:T(512)S(1)}, s32[256]{0:T(256)S(1)}, bf16[2048,768]{0,1:T(8,128)(2,1)}, s32[]{:T(128)}, ...), branch_computations={%region_19.19_spmd, %region_20.20_spmd} | conditional | flops 821755904 | bytes 29666336 | solution.py:276
  325.0 3.7 fusion.92
  328.9 6.7 fusion.50
  335.5 4.9 fusion.45
  353.6 2.9 fusion.84
  356.5 2.8 fusion.55
  359.3 5.8 copy.92
  368.3 5.1 convolution_convert_fusion.1
  374.6 5.1 convolution_convert_fusion
  383.5 115.2 %reduce-scatter.16.cloned.1.call-done = bf16[96,2304]{1,0:T(8,128)(2,1)} async-done(((bf16[768,2304]{1,0:T(8,128)(2,1)}), bf16[96,2304]{1,0:T(8,128)(2,1)}) %reduce-scatter.16.cloned.1.call-update) | async-done | bytes 442384
  498.7 2.1 copy.93
  500.8 38.3 %reduce-scatter.10.cloned.1.call-done = bf16[96,768]{1,0:T(8,128)(2,1)} async-done(((bf16[768,768]{1,0:T(8,128)(2,1)}), bf16[96,768]{1,0:T(8,128)(2,1)}) %reduce-scatter.10.cloned.1.call-update) | async-done | bytes 147472 | tf_op jit(solution)/shard_map/reduce_scatter | solution.py:311
  539.1 57.3 %reduce-scatter.12.cloned.1.call-done = bf16[96,3072]{1,0:T(8,128)(2,1)} async-done(((bf16[768,3072]{1,0:T(8,128)(2,1)}), bf16[96,3072]{1,0:T(8,128)(2,1)}) %reduce-scatter.12.cloned.1.call-update) | async-done | bytes 589840 | tf_op jit(solution)/shard_map/reduce_scatter | solution.py:323
  596.3 57.1 %reduce-scatter.14.cloned.1.call-done = bf16[384,768]{1,0:T(8,128)(2,1)} async-done(((bf16[3072,768]{1,0:T(8,128)(2,1)}), bf16[384,768]{1,0:T(8,128)(2,1)}) %reduce-scatter.14.cloned.1.call-update) | async-done | bytes 589840 | tf_op jit(solution)/shard_map/reduce_scatter | solution.py:329
  658.2 23.6 %all-reduce.13 = (bf16[768]{0:T(1024)(128)(2,1)S(1)}, bf16[768]{0:T(1024)(128)(2,1)S(1)}, bf16[768]{0:T(1024)(128)(2,1)S(1)}, bf16[768]{0:T(1024)(128)(2,1)S(1)}...) all-reduce(bf16[768]{0:T(1024)(128)(2,1)} %dynamic-update-slice.5, ...), channel_id=1, replica_groups=mesh['shard'=8,'replica'=4] {'shard'}, use_global_device_ids=true, to_apply=%add.5 | all-reduce | flops 8448 | bytes 33792
  683.9 4.0 convolution_add_fusion.2
  687.9 2.8 reduce-scatter.18.cloned.1.call-done
  691.6 11.9 %all-reduce.15 = (bf16[2,96]{1,0:T(2,128)(2,1)S(1)}, bf16[96]{0:T(256)(128)(2,1)S(1)}, bf16[96]{0:T(256)(128)(2,1)S(1)}, bf16[96]{0:T(256)(128)(2,1)S(1)}, bf16[...) all-reduce(bf16[2,96]{1,0:T(2,128)(2,1)S(1)} %copy.95, ...), channel_id=1, replica_groups=mesh['shard'=8,'replica'=4] {'replica'}, use_global_device_ids=true, to_apply=%region_27.28 | all-reduce | flops 1152 | bytes 4608 | tf_op jit(solution)/shard_map/psum | solution.py:344
  707.7 66.8 %all-reduce.19.cloned.1.call-done = (bf16[96,2304]{0,1:T(8,128)(2,1)}, bf16[96,768]{1,0:T(8,128)(2,1)}, bf16[96,3072]{1,0:T(8,128)(2,1)}, bf16[384,768]{1,0:T(8,128)(2,1)}) async-done(((bf16[96,2304]{0,1:T(8,128)(2,1)}, bf16[96,768]{1,0:T(8,128)(2,1)}, bf16[96,3072]{1,0:T(8,128)(2,1)}, bf16[384,768]{1,0:T(8,128)(2,1)}), (bf16[96,2304]{0,1:T(8,128)(2,1)}, bf16[96,768]{1,0:T(8,128)(2,1)}, ...) | async-done | bytes 1769488 | tf_op jit(solution)/shard_map/psum | solution.py:343
  774.6 2.3 copy.81
  778.5 2.2 convert_element_type.234
  (269 shorter events, 71.6 us)
Async XLA Ops:
  7.2 39.3 %all-gather.12.cloned.1.call-start = ((), (), s32[]{:S(2)}) async-start(), calls=%async_computation.5 | async-start | bytes 3981312 | tf_op jit(solution)/shard_map/all_gather | solution.py:77
  7.9 42.7 %copy-start.42 = (bf16[2,96]{1,0:T(2,128)(2,1)S(1)}, bf16[2,96]{1,0:T(2,128)(2,1)}, u32[]{:S(2)}) copy-start(bf16[2,96]{1,0:T(2,128)(2,1)} %param.30) | copy-start | bytes 1156
  7.9 99.3 %all-gather.14.cloned.1.call-start = ((), (), s32[]{:S(2)}) async-start(), calls=%async_computation.6 | async-start | bytes 3538944 | tf_op jit(solution)/shard_map/all_gather | solution.py:97
  49.7 12.5 %copy-start.40 = (u32[32]{0:T(128)S(1)}, u32[32]{0:T(128)}, u32[]{:S(2)}) copy-start(u32[32]{0:T(128)} %constant.230) | copy-start | bytes 388
  49.7 13.8 %copy-start.43 = (bf16[96]{0:T(256)(128)(2,1)S(1)}, bf16[96]{0:T(256)(128)(2,1)}, u32[]{:S(2)}) copy-start(bf16[96]{0:T(256)(128)(2,1)} %param.32) | copy-start | bytes 580
  49.7 14.0 %copy-start.44 = (bf16[96]{0:T(256)(128)(2,1)S(1)}, bf16[96]{0:T(256)(128)(2,1)}, u32[]{:S(2)}) copy-start(bf16[96]{0:T(256)(128)(2,1)} %param.34) | copy-start | bytes 580
  49.7 14.2 %copy-start.45 = (bf16[96]{0:T(256)(128)(2,1)S(1)}, bf16[96]{0:T(256)(128)(2,1)}, u32[]{:S(2)}) copy-start(bf16[96]{0:T(256)(128)(2,1)} %param.33) | copy-start | bytes 580
  49.7 14.4 %copy-start.46 = (bf16[96]{0:T(256)(128)(2,1)S(1)}, bf16[96]{0:T(256)(128)(2,1)}, u32[]{:S(2)}) copy-start(bf16[96]{0:T(256)(128)(2,1)} %param.38) | copy-start | bytes 580
  49.8 14.7 %copy-start.47 = (bf16[96]{0:T(256)(128)(2,1)S(1)}, bf16[96]{0:T(256)(128)(2,1)}, u32[]{:S(2)}) copy-start(bf16[96]{0:T(256)(128)(2,1)} %param.39) | copy-start | bytes 580
  49.8 39.1 %copy-start.41 = (bf16[384]{0:T(512)(128)(2,1)S(1)}, bf16[384]{0:T(512)(128)(2,1)}, u32[]{:S(2)}) copy-start(bf16[384]{0:T(512)(128)(2,1)} %param.36) | copy-start | bytes 2308
  49.8 47.2 %copy-start.20 = (s32[256]{0:T(256)S(1)}, s32[256]{0:T(256)}, u32[]{:S(2)}) copy-start(s32[256]{0:T(256)} %param.28) | copy-start | bytes 3076
  50.6 67.2 %all-gather.16.cloned.1.call-start = ((), (), s32[]{:S(2)}) async-start(), calls=%async_computation.7 | async-start | bytes 3538944 | tf_op jit(solution)/shard_map/all_gather | solution.py:98
  60.4 46.3 %copy-start.7 = (bf16[256,768]{1,0:T(8,128)(2,1)}, bf16[256,768]{1,0:T(8,128)(2,1)S(1)}, u32[]{:S(2)}) copy-start(bf16[256,768]{1,0:T(8,128)(2,1)S(1)} %get-tuple-element.1236) | copy-start | bytes 1179652
  60.4 84.0 %all-gather.18.cloned.1.call-start = ((), (), s32[]{:S(2)}) async-start(), calls=%async_computation.8 | async-start | bytes 1327104 | tf_op jit(solution)/shard_map/all_gather | solution.py:78
  61.0 123.0 %all-gather.20.cloned.1.call-start = ((), (), s32[]{:S(2)}) async-start(), calls=%async_computation.9 | async-start | bytes 5308416 | tf_op jit(solution)/shard_map/all_gather | solution.py:146
  61.6 163.0 %all-gather.22.cloned.1.call-start = ((), (), s32[]{:S(2)}) async-start(), calls=%async_computation.10 | async-start | bytes 5308416 | tf_op jit(solution)/shard_map/all_gather | solution.py:148
  62.2 196.5 %all-gather.24.cloned.1.call-start = ((), (), s32[]{:S(2)}) async-start(), calls=%async_computation.11 | async-start | bytes 3538944 | tf_op jit(solution)/shard_map/all_gather | solution.py:233
  97.0 127.6 %copy-start.25 = (f32[768]{0:T(1024)}, f32[768]{0:T(1024)S(1)}, u32[]{:S(2)}) copy-start(f32[768]{0:T(1024)S(1)} %convert_element_type.209) | copy-start | bytes 9220
  97.0 139.6 %copy-start.23 = (f32[768]{0:T(1024)}, f32[768]{0:T(1024)S(1)}, u32[]{:S(2)}) copy-start(f32[768]{0:T(1024)S(1)} %convert_element_type.208) | copy-start | bytes 9220
  97.0 133.3 %copy-start.27 = (f32[768]{0:T(1024)}, f32[768]{0:T(1024)S(1)}, u32[]{:S(2)}) copy-start(f32[768]{0:T(1024)S(1)} %convert_element_type.214) | copy-start | bytes 9220
  106.7 206.3 %all-gather.26.cloned.1.call-start = ((), (), s32[]{:S(2)}) async-start(), calls=%async_computation.12 | async-start | bytes 3538944 | tf_op jit(solution)/shard_map/all_gather | solution.py:234
  122.6 22.3 %copy-start.12 = (bf16[256,768]{1,0:T(8,128)(2,1)S(1)}, bf16[256,768]{1,0:T(8,128)(2,1)}, u32[]{:S(2)}) copy-start(bf16[256,768]{1,0:T(8,128)(2,1)} %param.27) | copy-start | bytes 1179652
  144.4 51.4 %copy-start.9 = (bf16[256,12,64]{0,2,1:T(8,128)(2,1)}, bf16[256,12,64]{0,2,1:T(8,128)(2,1)S(1)}, u32[]{:S(2)}) copy-start(bf16[256,12,64]{0,2,1:T(8,128)(2,1)S(1)} %fusion.70) | copy-start | bytes 1179652
  146.8 89.8 %copy-start.31 = (f32[256]{0:T(256)}, f32[256]{0:T(256)S(1)}, u32[]{:S(2)}) copy-start(f32[256]{0:T(256)S(1)} %broadcast_multiply_fusion.1) | copy-start | bytes 3076
  147.0 89.6 %copy-start.36 = (f32[256]{0:T(256)}, f32[256]{0:T(256)S(1)}, u32[]{:S(2)}) copy-start(f32[256]{0:T(256)S(1)} %fusion.71) | copy-start | bytes 3076
  224.6 6.1 slice-start.2
  224.6 4.7 copy-start.11
  224.6 6.1 slice-start.3
  224.6 6.1 copy-start.49
  229.1 5.2 copy-start
  229.1 5.2 copy-start.29
  229.3 4.9 copy-start.35
  230.3 4.0 slice-start
  237.0 26.5 %copy-start.2 = (f32[256,768]{1,0:T(8,128)}, f32[256,768]{1,0:T(8,128)S(1)}, u32[]{:S(2)}) copy-start(f32[256,768]{1,0:T(8,128)S(1)} %get-tuple-element.1214) | copy-start | bytes 2359300
  238.3 260.4 %reduce-scatter.16.cloned.1.call-start = ((), (), s32[]{:S(2)}) async-start(), calls=%async_computation.16 | async-start | bytes 3981312
  242.4 21.0 %copy-start.16 = (f32[12,256]{1,0:T(8,128)S(1)}, f32[12,256]{1,0:T(8,128)}, u32[]{:S(2)}) copy-start(f32[12,256]{1,0:T(8,128)} %copy-done.15) | copy-start | bytes 36868
  312.9 6.6 copy-start.22
  352.3 4.2 copy-start.13
  365.2 173.9 %reduce-scatter.10.cloned.1.call-start = ((), (), s32[]{:S(2)}) async-start(), calls=%async_computation.13 | async-start | bytes 1327104 | tf_op jit(solution)/shard_map/reduce_scatter | solution.py:311
  368.0 228.4 %reduce-scatter.12.cloned.1.call-start = ((), (), s32[]{:S(2)}) async-start(), calls=%async_computation.14 | async-start | bytes 5308416 | tf_op jit(solution)/shard_map/reduce_scatter | solution.py:323
  373.5 280.0 %reduce-scatter.14.cloned.1.call-start = ((), (), s32[]{:S(2)}) async-start(), calls=%async_computation.15 | async-start | bytes 5308416 | tf_op jit(solution)/shard_map/reduce_scatter | solution.py:329
  379.7 302.7 %copy-start.1 = (f32[256,768]{1,0:T(8,128)S(1)}, f32[256,768]{1,0:T(8,128)}, u32[]{:S(2)}) copy-start(f32[256,768]{1,0:T(8,128)} %copy-done) | copy-start | bytes 2359300
  379.7 302.7 %copy-start.28 = (f32[768]{0:T(1024)S(1)}, f32[768]{0:T(1024)}, u32[]{:S(2)}) copy-start(f32[768]{0:T(1024)} %copy-done.27) | copy-start | bytes 9220
  379.7 302.6 %copy-start.30 = (f32[256]{0:T(256)S(1)}, f32[256]{0:T(256)}, u32[]{:S(2)}) copy-start(f32[256]{0:T(256)} %copy-done.29) | copy-start | bytes 3076
  379.7 304.2 %copy-start.19 = (bf16[256,12,64]{0,2,1:T(8,128)(2,1)S(1)}, bf16[256,12,64]{0,2,1:T(8,128)(2,1)}, u32[]{:S(2)}) copy-start(bf16[256,12,64]{0,2,1:T(8,128)(2,1)} %copy-done.18) | copy-start | bytes 1179652
  379.7 311.0 %reduce-scatter.18.cloned.1.call-start = ((), (), s32[]{:S(2)}) async-start(), calls=%async_computation.17 | async-start | bytes 221184
  383.4 391.1 %all-reduce.19.cloned.1.call-start = ((), (), s32[]{:S(2)}) async-start(), calls=%async_computation.18 | async-start | bytes 3833856 | tf_op jit(solution)/shard_map/psum | solution.py:343
  774.6 6.1 copy-start.17
  (20 other events, 47.5 us)
Sparse Core Ops, SparseCore 0:
  9.9 36.5 all-gather.11
  50.7 32.3 all-gather.13
  85.6 32.1 all-gather.15
  119.5 23.9 all-gather.17
  145.2 38.7 all-gather.19
  185.8 38.7 all-gather.21
  226.5 32.1 all-gather.23
  260.6 32.3 all-gather.25
  365.3 133.3 reduce-scatter.15
  502.4 36.6 reduce-scatter.9
  542.5 53.7 reduce-scatter.11
  599.6 53.7 reduce-scatter.13
  657.1 33.6 reduce-scatter.17
  693.8 80.6 all-reduce.18
where the time goes:
time: 794 us; the launch traced here: 789 us
  waiting for transfers between devices  466 us (59%)
  blocking collectives  103 us (13%)
  matrix products  74.2 us (9%)
  local copies, waits for them, and re-layouts  70.2 us (9%)
  loops' own time  32 us (4%)
  other arithmetic  24.2 us (3%)
  between operations  16.9 us (2%)
    unnamed x16, waiting for transfers between devices  120 us
    psum x1, waiting for transfers between devices, body(): lax.psum(shard_grads[0].astype(jnp.bfloat16), 'replica').astype(jnp.float32)  66.8 us
    reduce_scatter x1, waiting for transfers between devices, body(): lax.psum_scatter(local_grads[6].astype(jnp.bfloat16), 'shard', scatter_di...  57.3 us
    reduce_scatter x1, waiting for transfers between devices, body(): lax.psum_scatter(local_grads[8].astype(jnp.bfloat16), 'shard', scatter_di...  57.1 us
    unnamed x2, blocking collectives  47.7 us
    all_gather x1, waiting for transfers between devices, body(): lax.all_gather(w_qkv, 'shard', axis=0, tiled=True)  38.5 us
    reduce_scatter x1, waiting for transfers between devices, body(): lax.psum_scatter(local_grads[2].astype(jnp.bfloat16), 'shard', scatter_di...  38.3 us
    all_gather x1, waiting for transfers between devices, body(): lax.all_gather(w_in, 'shard', axis=0, tiled=True)  37 us
  transfers between devices with their start and end apart: 14, of which 11 were waited for; matrix products, arithmetic and copies ran while one was open for 14% of the time, Pallas kernels for 0%

commit v1 on v0

--- a/solution.py
+++ b/solution.py
@@ -1,8 +1,11 @@
+import functools
 import math
 
 import jax
 import jax.numpy as jnp
 from jax import lax
+from jax.experimental import pallas as pl
+from jax.experimental.pallas import tpu as pltpu
 from jax.sharding import PartitionSpec as P
 
 HEADS = 12
@@ -51,7 +54,7 @@
     return (probs.astype(jnp.bfloat16), d_scores)
 
 
-def body(
+def plain_body(
     hidden,
     segment_ids,
     w_qkv,
@@ -356,6 +359,837 @@
     return (output, d_hidden) + tuple(total_grads)
 
 
+PLANE = 8
+LINE = 4
+CHIPS = 4
+MESH = pl.DeviceIdType.MESH
+VMEM = pltpu.VMEM
+ANY = pl.ANY
+f32 = jnp.float32
+bf16 = jnp.bfloat16
+
+
+class Wires:
+    def __init__(self, send, recv):
+        self.send, self.recv, self.used = send, recv, 0
+        me = lax.axis_index("shard")
+        self.me = me
+        self.core = me % 2
+        self.chip = me // 2
+        self.mate = me + 1 - 2 * self.core
+        self.xn = me + 2 - 4 * (self.chip % 2)
+        self.yn = me + 4 - 8 * (me // 4)
+        self.dn = self.xn + 4 - 8 * (me // 4)
+        self.cx = self.xn // 2
+        self.cy = self.yn // 2
+        self.cd = self.dn // 2
+
+    def copy(self, src, dst, where):
+        slot = self.used
+        self.used += 1
+        return pltpu.make_async_remote_copy(
+            src_ref=src,
+            dst_ref=dst,
+            send_sem=self.send.at[slot],
+            recv_sem=self.recv.at[slot],
+            device_id=where if isinstance(where, dict) else {"shard": where},
+            device_id_type=MESH,
+        )
+
+    def start(self, src, dst, where):
+        made = self.copy(src, dst, where)
+        made.start()
+        return made
+
+
+def greet(others):
+    barrier = pltpu.get_barrier_semaphore()
+    for other in others:
+        pl.semaphore_signal(barrier, inc=1, device_id=other, device_id_type=MESH)
+    pl.semaphore_wait(barrier, len(others))
+
+
+def plane_others(me):
+    return [{"shard": (me + step) % PLANE} for step in range(1, PLANE)]
+
+
+def call(kernel, ins, outs, scratch, ident, in_spaces, out_spaces, name):
+    return pl.pallas_call(
+        kernel,
+        out_shape=outs,
+        in_specs=[pl.BlockSpec(memory_space=space) for space in in_spaces],
+        out_specs=[pl.BlockSpec(memory_space=space) for space in out_spaces],
+        scratch_shapes=scratch,
+        compiler_params=pltpu.CompilerParams(
+            collective_id=ident, has_side_effects=True, vmem_limit_bytes=60 << 20
+        ),
+        name=name,
+    )(*ins)
+
+
+def dma_sems(count):
+    return [pltpu.SemaphoreType.DMA((count,)), pltpu.SemaphoreType.DMA((count,))]
+
+
+class Gather:
+    def __init__(self, wires, block, out, local_sem):
+        w = self.w = wires
+        self.out = out
+        self.half = block.shape[0] // 2
+        me = w.me
+        self.own = pltpu.make_async_copy(block, out.at[me], local_sem)
+        self.own.start()
+        self.to_x = w.start(block, out.at[me], w.xn)
+        self.to_y = w.start(block, out.at[me], w.yn)
+        self.to_mate = w.start(block, out.at[me], w.mate)
+
+    def relay(self):
+        w, out, half = self.w, self.out, self.half
+        low, high = pl.ds(0, half), pl.ds(half, half)
+        self.to_x.wait_recv()
+        self.x_on = w.start(out.at[w.xn, low], out.at[w.xn, low], w.yn)
+        self.x_mate = w.start(out.at[w.xn], out.at[w.xn], w.mate)
+        self.to_y.wait_recv()
+        self.y_on = w.start(out.at[w.yn, high], out.at[w.yn, high], w.xn)
+        self.y_mate = w.start(out.at[w.yn], out.at[w.yn], w.mate)
+
+    def finish(self):
+        w, out, half = self.w, self.out, self.half
+        low, high = pl.ds(0, half), pl.ds(half, half)
+        self.x_on.wait_recv()
+        self.d_low = w.start(out.at[w.dn, low], out.at[w.dn, low], w.mate)
+        self.y_on.wait_recv()
+        self.d_high = w.start(out.at[w.dn, high], out.at[w.dn, high], w.mate)
+
+    def done(self):
+        for made in (self.to_mate, self.x_mate, self.y_mate, self.d_low, self.d_high):
+            made.wait_recv()
+        for made in (
+            self.to_x,
+            self.to_y,
+            self.to_mate,
+            self.x_on,
+            self.x_mate,
+            self.y_on,
+            self.y_mate,
+            self.d_low,
+            self.d_high,
+        ):
+            made.wait_send()
+        self.own.wait()
+
+
+def gather_kernel(hid, wq, wo, wi, wb, small, hid_o, wq_o, wo_o, wi_o, wb_o, small_o, send, recv, loc):
+    w = Wires(send, recv)
+    greet(plane_others(w.me))
+    me = w.me
+    own_small = pltpu.make_async_copy(small, small_o.at[me], loc.at[0])
+    own_small.start()
+    smalls = [
+        w.start(small, small_o.at[me], (me + step) % PLANE) for step in range(1, PLANE)
+    ]
+    first = Gather(w, hid, hid_o, loc.at[1])
+    own_q = pltpu.make_async_copy(wq.at[w.chip], wq_o.at[me], loc.at[2])
+    own_q.start()
+    q_mate = w.start(wq.at[w.chip], wq_o.at[me], w.mate)
+    q_x = w.start(wq.at[w.cx], wq_o.at[me], w.xn)
+    q_y = w.start(wq.at[w.cy], wq_o.at[me], w.yn)
+    q_d = w.start(wq.at[w.cd], wq_o.at[me], w.dn)
+    rest = [
+        Gather(w, block, out, loc.at[3 + slot])
+        for slot, (block, out) in enumerate(((wo, wo_o), (wi, wi_o), (wb, wb_o)))
+    ]
+    first.relay()
+    q_on = []
+    for came, source in ((q_x, w.xn), (q_y, w.yn), (q_d, w.dn)):
+        came.wait_recv()
+        q_on.append(w.start(wq_o.at[source], wq_o.at[source], w.mate))
+    first.finish()
+    for one in rest:
+        one.relay()
+    for one in rest:
+        one.finish()
+    first.done()
+    for one in rest:
+        one.done()
+    for made in [q_mate] + q_on + smalls:
+        made.wait_recv()
+    for made in [q_mate, q_x, q_y, q_d] + q_on + smalls:
+        made.wait_send()
+    own_small.wait()
+    own_q.wait()
+
+
+def gather_all(hid, wq, wo, wi, wb, small):
+    outs = [
+        jax.ShapeDtypeStruct((PLANE,) + one.shape, one.dtype) for one in (hid, wq, wo, wi, wb, small)
+    ]
+    outs[1] = jax.ShapeDtypeStruct((PLANE,) + wq.shape[1:], wq.dtype)
+    return call(
+        gather_kernel,
+        (hid, wq, wo, wi, wb, small),
+        outs,
+        dma_sems(56) + [pltpu.SemaphoreType.DMA((8,))],
+        1,
+        [VMEM] * 6,
+        [ANY] * 6,
+        "gather_all",
+    )
+
+
+def swap_kernel(block, out, send, recv, loc):
+    w = Wires(send, recv)
+    greet([{"shard": one} for one in (w.xn, w.yn, w.dn)])
+    own = pltpu.make_async_copy(block.at[w.chip], out.at[w.chip], loc.at[0])
+    own.start()
+    made = [
+        w.start(block.at[chip], out.at[w.chip], who)
+        for chip, who in ((w.cd, w.dn), (w.cx, w.xn), (w.cy, w.yn))
+    ]
+    for one in made:
+        one.wait()
+    own.wait()
+
+
+def chip_swap(block, ident, name):
+    return call(
+        swap_kernel,
+        (block,),
+        [jax.ShapeDtypeStruct(block.shape, block.dtype)],
+        dma_sems(4) + [pltpu.SemaphoreType.DMA((1,))],
+        ident,
+        [VMEM],
+        [VMEM],
+        name,
+    )[0]
+
+
+def mate_kernel(block, out, send, recv):
+    w = Wires(send, recv)
+    greet([{"shard": w.mate}])
+    w.start(block.at[:, 1 - w.core], out, w.mate).wait()
+
+
+def mate_swap(block, ident, name):
+    shape = (block.shape[0],) + block.shape[2:]
+    return call(
+        mate_kernel,
+        (block,),
+        [jax.ShapeDtypeStruct(shape, block.dtype)],
+        dma_sems(1),
+        ident,
+        [VMEM],
+        [VMEM],
+        name,
+    )[0]
+
+
+ROWS = 256
+
+
+def attend_kernel(bound, q_ref, k_ref, v_ref, segq_ref, segk_ref, ctx_ref, low_ref, log_ref, *, hd):
+    block = pl.program_id(0)
+    heads = q_ref.shape[2] // hd
+    query = q_ref[0]
+    segq = segq_ref[0][:, 0:1]
+
+    def step(index, state):
+        rows = pl.ds(pl.multiple_of(index * ROWS, ROWS), ROWS)
+        keys = k_ref[rows, :]
+        values = v_ref[rows, :]
+        allowed = segq == segk_ref[index]
+        made = []
+        for head in range(heads):
+            top, total, acc = state[head]
+            cols = slice(head * hd, (head + 1) * hd)
+            scores = (
+                lax.dot_general(
+                    query[:, cols], keys[:, cols], (((1,), (1,)), ((), ())), preferred_element_type=f32
+                )
+                * scale_factor
+            )
+            scores = jnp.where(allowed, scores, masked_value)
+            new = jnp.maximum(top, jnp.max(scores, axis=1, keepdims=True))
+            weights = jnp.where(allowed, jnp.exp(scores - new), 0.0)
+            factor = jnp.exp(top - new)
+            total = total * factor + jnp.sum(weights, axis=1, keepdims=True)
+            acc = acc * factor + lax.dot_general(
+                weights.astype(bf16), values[:, cols], (((1,), (0,)), ((), ())), preferred_element_type=f32
+            )
+            made.append((new, total, acc))
+        return tuple(made)
+
+    zero = tuple(
+        (
+            jnp.full((ROWS, 1), masked_value, f32),
+            jnp.zeros((ROWS, 1), f32),
+            jnp.zeros((ROWS, hd), f32),
+        )
+        for _ in range(heads)
+    )
+    state = lax.fori_loop(bound[0, block], bound[1, block], step, zero)
+    context = jnp.concatenate([acc / total for _, total, acc in state], axis=1)
+    ctx_ref[0] = context
+    low_ref[0] = context.astype(bf16)
+    for head in range(heads):
+        top, total, _ = state[head]
+        log_ref[0, :, head : head + 1] = top + jnp.log(total)
+
+
+def attend(bound, query, keys, values, segq, segk, hd):
+    blocks, rows, wide = query.shape
+    whole = lambda one: pl.BlockSpec(one.shape, lambda i, b: (0,) * one.ndim)
+    per = lambda last: pl.BlockSpec((1, rows, last), lambda i, b: (i, 0, 0))
+    return pl.pallas_call(
+        functools.partial(attend_kernel, hd=hd),
+        grid_spec=pltpu.PrefetchScalarGridSpec(
+            num_scalar_prefetch=1,
+            grid=(blocks,),
+            in_specs=[per(wide), whole(keys), whole(values), per(128), whole(segk)],
+            out_specs=[per(wide), per(wide), per(128)],
+        ),
+        out_shape=[
+            jax.ShapeDtypeStruct((blocks, rows, wide), f32),
+            jax.ShapeDtypeStruct((blocks, rows, wide), bf16),
+            jax.ShapeDtypeStruct((blocks, rows, 128), f32),
+        ],
+        compiler_params=pltpu.CompilerParams(vmem_limit_bytes=48 << 20),
+        name="attend",
+    )(bound, query, keys, values, segq, segk)
+
+
+def attend_back_kernel(
+    bound, q_ref, k_ref, v_ref, segq_ref, segk_ref, ctx_ref, dctx_ref, log_ref, dq_ref, dk_ref, dv_ref, *, hd
+):
+    block = pl.program_id(0)
+    heads = q_ref.shape[2] // hd
+
+    @pl.when(block == 0)
+    def _():
+        dk_ref[...] = jnp.zeros_like(dk_ref)
+        dv_ref[...] = jnp.zeros_like(dv_ref)
+
+    query = q_ref[0]
+    dctx = dctx_ref[0]
+    segq = segq_ref[0][:, 0:1]
+    product = dctx.astype(f32) * ctx_ref[0]
+    delta = [
+        jnp.sum(product[:, head * hd : (head + 1) * hd], axis=1, keepdims=True) for head in range(heads)
+    ]
+
+    def step(index, state):
+        rows = pl.ds(pl.multiple_of(index * ROWS, ROWS), ROWS)
+        keys = k_ref[rows, :]
+        values = v_ref[rows, :]
+        allowed = segq == segk_ref[index]
+        made, dks, dvs = [], [], []
+        for head in range(heads):
+            cols = slice(head * hd, (head + 1) * hd)
+            scores = (
+                lax.dot_general(
+                    query[:, cols], keys[:, cols], (((1,), (1,)), ((), ())), preferred_element_type=f32
+                )
+                * scale_factor
+            )
+            probs = jnp.where(allowed, jnp.exp(scores - log_ref[0, :, head : head + 1]), 0.0)
+            d_prob = lax.dot_general(
+                dctx[:, cols], values[:, cols], (((1,), (1,)), ((), ())), preferred_element_type=f32
+            )
+            d_scores = (probs * (d_prob - delta[head])).astype(bf16)
+            made.append(
+                state[head]
+                + lax.dot_general(
+                    d_scores, keys[:, cols], (((1,), (0,)), ((), ())), preferred_element_type=f32
+                )
+            )
+            dks.append(
+                lax.dot_general(
+                    d_scores, query[:, cols], (((0,), (0,)), ((), ())), preferred_element_type=f32
+                )
+            )
+            dvs.append(
+                lax.dot_general(
+                    probs.astype(bf16), dctx[:, cols], (((0,), (0,)), ((), ())), preferred_element_type=f32
+                )
+            )
+        dk_ref[rows, :] += jnp.concatenate(dks, axis=1) * scale_factor
+        dv_ref[rows, :] += jnp.concatenate(dvs, axis=1)
+        return tuple(made)
+
+    zero = tuple(jnp.zeros((ROWS, hd), f32) for _ in range(heads))
+    state = lax.fori_loop(bound[0, block], bound[1, block], step, zero)
+    dq_ref[0] = jnp.concatenate(state, axis=1) * scale_factor
+
+
+def attend_back(bound, query, keys, values, segq, segk, ctx, dctx, log, hd):
+    blocks, rows, wide = query.shape
+    whole = lambda one: pl.BlockSpec(one.shape, lambda i, b: (0,) * len(one.shape))
+    per = lambda last: pl.BlockSpec((1, rows, last), lambda i, b: (i, 0, 0))
+    total = jax.ShapeDtypeStruct(keys.shape, f32)
+    return pl.pallas_call(
+        functools.partial(attend_back_kernel, hd=hd),
+        grid_spec=pltpu.PrefetchScalarGridSpec(
+            num_scalar_prefetch=1,
+            grid=(blocks,),
+            in_specs=[
+                per(wide),
+                whole(keys),
+                whole(values),
+                per(128),
+                whole(segk),
+                per(wide),
+                per(wide),
+                per(128),
+            ],
+            out_specs=[per(wide), whole(total), whole(total)],
+        ),
+        out_shape=[jax.ShapeDtypeStruct((blocks, rows, wide), f32), total, total],
+        compiler_params=pltpu.CompilerParams(vmem_limit_bytes=48 << 20),
+        name="attend_back",
+    )(bound, query, keys, values, segq, segk, ctx, dctx, log)
+
+
+def add_into(dst, other, out=None):
+    out = dst if out is None else out
+    lead = dst.shape[0] if len(dst.shape) == 3 else 0
+    rows = dst.shape[-2]
+
+    def go(index, carry):
+        if lead:
+            at = (index // (rows // 16), pl.ds(pl.multiple_of((index % (rows // 16)) * 16, 16), 16))
+        else:
+            at = (pl.ds(pl.multiple_of(index * 16, 16), 16),)
+        out[at] = (dst[at].astype(f32) + other[at].astype(f32)).astype(out.dtype)
+        return carry
+
+    lax.fori_loop(0, max(lead, 1) * (rows // 16), go, 0)
+
+
+class Reduce:
+    def __init__(self, wires, full, pair, land, pick):
+        self.w, self.full, self.pair, self.land = wires, full, pair, land
+        self.half = pair.shape[1] // 2
+        self.pick = pick
+        if full is not None:
+            self.meet = wires.start(pick(full, 1 - wires.core), pair, wires.mate)
+
+    def first(self):
+        w, pair, land = self.w, self.pair, self.land
+        low, high = pl.ds(0, self.half), pl.ds(self.half, self.half)
+        if self.full is not None:
+            self.meet.wait_recv()
+            add_into(pair, self.pick(self.full, w.core))
+        self.x0 = w.start(pair.at[w.cd, low], land.at[1], w.xn)
+        self.y0 = w.start(pair.at[w.cd, high], land.at[3], w.yn)
+        self.x1 = w.start(pair.at[w.cx, low], land.at[0], w.xn)
+        self.y1 = w.start(pair.at[w.cy, high], land.at[2], w.yn)
+
+    def second(self):
+        w, pair, land = self.w, self.pair, self.land
+        low, high = pl.ds(0, self.half), pl.ds(self.half, self.half)
+        self.x0.wait_recv()
+        add_into(pair.at[w.cy, low], land.at[1])
+        self.y2 = w.start(pair.at[w.cy, low], land.at[4], w.yn)
+        self.y0.wait_recv()
+        add_into(pair.at[w.cx, high], land.at[3])
+        self.x2 = w.start(pair.at[w.cx, high], land.at[5], w.xn)
+        self.x1.wait_recv()
+        add_into(pair.at[w.chip, low], land.at[0])
+        self.y1.wait_recv()
+        add_into(pair.at[w.chip, high], land.at[2])
+
+    def third(self, out):
+        w, pair, land = self.w, self.pair, self.land
+        low, high = pl.ds(0, self.half), pl.ds(self.half, self.half)
+        self.y2.wait_recv()
+        add_into(pair.at[w.chip, low], land.at[4], out.at[low])
+        self.x2.wait_recv()
+        add_into(pair.at[w.chip, high], land.at[5], out.at[high])
+
+    def done(self):
+        made = [self.x0, self.x1, self.y0, self.y1, self.x2, self.y2]
+        if self.full is not None:
+            made.append(self.meet)
+        for one in made:
+            one.wait_send()
+
+
+class Line:
+    def __init__(self, wires, z, block, land, out):
+        self.w, self.z, self.block, self.land, self.out = wires, z, block, land, out
+        self.edge = (z == 0) | (z == LINE - 1)
+        self.inner = {"replica": 1 + z // 2}
+        self.outer = {"replica": 3 * (z // 2)}
+        self.across = {"replica": 2 - z // 2}
+        self.up = wires.copy(block, land.at[0], self.inner)
+        self.over = wires.copy(block, land.at[1], {"replica": 3 - z})
+        self.back = wires.copy(out, out, self.outer)
+
+    def first(self):
+        @pl.when(self.edge)
+        def _():
+            self.up.start()
+
+    def second(self):
+        @pl.when(jnp.logical_not(self.edge))
+        def _():
+            self.up.wait_recv()
+            add_into(self.block, self.land.at[0])
+            self.over.start()
+
+    def third(self):
+        @pl.when(jnp.logical_not(self.edge))
+        def _():
+            self.over.wait_recv()
+            add_into(self.block, self.land.at[1], self.out)
+            self.back.start()
+
+    def done(self):
+        @pl.when(self.edge)
+        def _():
+            self.up.wait_send()
+            self.back.wait_recv()
+
+        @pl.when(jnp.logical_not(self.edge))
+        def _():
+            self.over.wait_send()
+            self.back.wait_send()
+
+
+def reduce_kernel(
+    gq,
+    gb,
+    gi,
+    go,
+    dh,
+    small,
+    dq_o,
+    db_o,
+    di_o,
+    do_o,
+    dh_o,
+    small_o,
+    q_pair,
+    q_all,
+    pair,
+    land,
+    dh_land,
+    part,
+    s_land,
+    s_sum,
+    zq_land,
+    z_land,
+    zs_land,
+    send,
+    recv,
+    loc,
+):
+    w = Wires(send, recv)
+    z = lax.axis_index("replica")
+    me = w.me
+    barrier = pltpu.get_barrier_semaphore()
+    for other in plane_others(me):
+        pl.semaphore_signal(barrier, inc=1, device_id=other, device_id_type=MESH)
+    edge = (z == 0) | (z == LINE - 1)
+
+    @pl.when(edge)
+    def _():
+        pl.semaphore_signal(barrier, inc=1, device_id={"replica": 1 + z // 2}, device_id_type=MESH)
+        pl.semaphore_wait(barrier, PLANE)
+
+    @pl.when(jnp.logical_not(edge))
+    def _():
+        pl.semaphore_signal(barrier, inc=1, device_id={"replica": 3 * (z // 2)}, device_id_type=MESH)
+        pl.semaphore_signal(barrier, inc=1, device_id={"replica": 3 - z}, device_id_type=MESH)
+        pl.semaphore_wait(barrier, PLANE + 1)
+
+    rows, cols = go.shape[2], go.shape[3]
+    smalls = [
+        w.start(small.at[(me + step) % PLANE], s_land.at[me], (me + step) % PLANE)
+        for step in range(1, PLANE)
+    ]
+    own = pltpu.make_async_copy(small.at[me], s_land.at[me], loc.at[0])
+    own.start()
+    q_meet = w.start(gq.at[:, 1 - w.core], q_pair, w.mate)
+    picks = []
+    for slot in range(gb.shape[2] // rows):
+        at = pl.ds(slot * rows, rows)
+        picks.append((gb, lambda ref, core, at=at: ref.at[:, core, at], db_o.at[at]))
+    for slot in range(gi.shape[3] // cols):
+        at = pl.ds(slot * cols, cols)
+        picks.append((gi, lambda ref, core, at=at: ref.at[:, core, :, at], di_o.at[:, at]))
+    picks.append((go, lambda ref, core: ref.at[:, core], do_o))
+    count = len(picks)
+    chunks = [
+        Reduce(w, full, pair.at[slot], land.at[slot], pick)
+        for slot, (full, pick, _) in enumerate(picks)
+    ]
+    lines = [
+        Line(w, z, part.at[slot], z_land.at[slot], out) for slot, (_, _, out) in enumerate(picks)
+    ]
+    q_meet.wait_recv()
+    add_into(q_pair, gq.at[:, w.core])
+    q_made = [
+        w.start(q_pair.at[chip], q_all.at[w.chip], who)
+        for chip, who in ((w.cd, w.dn), (w.cx, w.xn), (w.cy, w.yn))
+    ]
+    q_own = pltpu.make_async_copy(q_pair.at[w.chip], q_all.at[w.chip], loc.at[1])
+    q_own.start()
+    chunks[0].first()
+    for one in q_made:
+        one.wait_recv()
+    q_own.wait()
+    q_line = Line(w, z, q_all, zq_land, dq_o)
+    q_line.first()
+    hidden = Reduce(w, None, dh, dh_land, None)
+    for one in smalls:
+        one.wait_recv()
+    own.wait()
+    s_sum[...] = jnp.sum(s_land[...], axis=0)
+    s_line = Line(w, z, s_sum, zs_land, small_o)
+    s_line.first()
+    for tick in range(1, count + 5):
+        if tick < count:
+            chunks[tick].first()
+        if tick == count:
+            hidden.first()
+        if 0 <= tick - 1 < count:
+            chunks[tick - 1].second()
+        if tick - 1 == count:
+            hidden.second()
+        if 0 <= tick - 2 < count:
+            chunks[tick - 2].third(part.at[tick - 2])
+            lines[tick - 2].first()
+        if tick - 2 == count:
+            hidden.third(dh_o)
+        if tick == 2:
+            q_line.second()
+            s_line.second()
+        if 0 <= tick - 3 < count:
+            lines[tick - 3].second()
+        if tick == 3:
+            q_line.third()
+            s_line.third()
+        if 0 <= tick - 4 < count:
+            lines[tick - 4].third()
+    for one in smalls + q_made + [q_meet]:
+        one.wait_send()
+    for one in chunks + [hidden]:
+        one.done()
+    for one in lines + [q_line, s_line]:
+        one.done()
+
+
+def reduce_all(gq, gb, gi, go, dh, small):
+    rows, cols = go.shape[2:]
+    count = gb.shape[2] // rows + gi.shape[3] // cols + 1
+    q_block = (CHIPS,) + gq.shape[2:]
+    tail = small.shape[1:]
+    outs = [
+        jax.ShapeDtypeStruct(q_block, bf16),
+        jax.ShapeDtypeStruct(gb.shape[2:], bf16),
+        jax.ShapeDtypeStruct(gi.shape[2:], bf16),
+        jax.ShapeDtypeStruct(go.shape[2:], bf16),
+        jax.ShapeDtypeStruct(dh.shape[1:], bf16),
+        jax.ShapeDtypeStruct(tail, f32),
+    ]
+    scratch = [
+        VMEM(q_block, bf16),
+        VMEM(q_block, bf16),
+        VMEM((count, CHIPS, rows, cols), bf16),
+        VMEM((count, 6, rows // 2, cols), bf16),
+        VMEM((6, dh.shape[1] // 2, dh.shape[2]), bf16),
+        VMEM((count, rows, cols), bf16),
+        VMEM(small.shape, f32),
+        VMEM(tail, f32),
+        VMEM((2,) + q_block, bf16),
+        VMEM((count, 2, rows, cols), bf16),
+        VMEM((2,) + tail, f32),
+    ]
+    wires = 8 + 4 + count * 10 + 6 + 6
+    return call(
+        reduce_kernel,
+        (gq, gb, gi, go, dh, small),
+        outs,
+        scratch + dma_sems(wires) + [pltpu.SemaphoreType.DMA((2,))],
+        7,
+        [VMEM] * 6,
+        [VMEM] * 6,
+        "reduce_all",
+    )
+
+
+def fast_body(
+    hidden,
+    segment_ids,
+    w_qkv,
+    b_qv,
+    w_out,
+    b_out,
+    gain1,
+    shift1,
+    w_in,
+    b_in,
+    w_back,
+    b_back,
+    gain2,
+    shift2,
+    cotangent,
+):
+    tok, width = hidden.shape
+    hd = width // HEADS
+    part = w_qkv.shape[0]
+    wide = width // CHIPS
+    ff = w_in.shape[1]
+    core = lax.axis_index("shard") % 2
+    fold = ff // width
+    pad = lambda rows: jnp.pad(rows, ((0, 0), (0, 128 - rows.shape[1])))
+    small = jnp.concatenate(
+        [
+            pad(
+                jnp.concatenate(
+                    [b_qv]
+                    + [one.reshape(1, part) for one in (b_out, gain1, shift1, b_back, gain2, shift2)]
+                    + [b_in.reshape(fold, part)],
+                    axis=0,
+                )
+            ),
+            segment_ids.astype(bf16).reshape(tok // 128, 128),
+        ],
+        axis=0,
+    )
+    small = jnp.pad(small, ((0, 16 - small.shape[0]), (0, 0)))
+    wq_send = w_qkv.reshape(part, 3, CHIPS, wide).transpose(2, 0, 1, 3).reshape(CHIPS, part, 3 * wide)
+    hid_all, wq_all, wo_all, wi_all, wb_all, small_all = gather_all(
+        hidden, wq_send, w_out, w_in, w_back, small
+    )
+    wq_mine = wq_all.reshape(width, 3 * wide)
+    wo_full = wo_all.reshape(width, width)
+    wi_full = wi_all.reshape(width, ff)
+    wb_full = wb_all.reshape(ff, width)
+    vec = lambda row: small_all[:, row, :part].reshape(width).astype(f32)
+    bo_full, g1_full, s1_full, bb_full, g2_full, s2_full = (vec(row) for row in range(2, 8))
+    bi_full = small_all[:, 8 : 8 + fold, :part].reshape(ff).astype(f32)
+    segs = small_all[:, 8 + fold : 8 + fold + tok // 128, :].astype(jnp.int32).reshape(PLANE, tok)
+    chip = lax.axis_index("shard") // 2
+    bias = lax.dynamic_slice_in_dim(small_all[:, 0:2, :part], 2 * chip, 2, 0)
+    bias_q = bias[:, 0].reshape(wide).astype(f32)
+    bias_v = bias[:, 1].reshape(wide).astype(f32)
+
+    hid_mine = lax.dynamic_index_in_dim(
+        hid_all.reshape(CHIPS, 2, tok, width), core, axis=1, keepdims=False
+    ).reshape(CHIPS * tok, width)
+    query = (
+        (jnp.dot(hid_mine, wq_mine[:, :wide], preferred_element_type=f32) + bias_q)
+        .astype(bf16)
+        .reshape(CHIPS, tok, wide)
+    )
+    kv = jnp.dot(hid_all.reshape(PLANE * tok, width), wq_mine[:, wide:], preferred_element_type=f32)
+    keys = kv[:, :wide].astype(bf16)
+    values = (kv[:, wide:] + bias_v).astype(bf16)
+    seg_mine = lax.dynamic_index_in_dim(segs.reshape(CHIPS, 2, tok), core, axis=1, keepdims=False)
+    touch = jnp.logical_and(
+        segs[None, :, 0] <= seg_mine[:, -1:], segs[None, :, -1] >= seg_mine[:, :1]
+    )
+    place = jnp.arange(PLANE, dtype=jnp.int32)[None]
+    bound = jnp.stack(
+        [
+            jnp.min(jnp.where(touch, place, PLANE), axis=1),
+            jnp.max(jnp.where(touch, place, -1), axis=1) + 1,
+        ]
+    ).astype(jnp.int32)
+    segq = jnp.broadcast_to(seg_mine[:, :, None], (CHIPS, tok, 128))
+    segk = segs.reshape(PLANE, 1, tok)
+    ctx32, ctx_low, log_total = attend(bound, query, keys, values, segq, segk, hd)
+    ctx_parts = chip_swap(ctx_low, 2, "ctx_swap")
+    context = ctx_parts.transpose(1, 0, 2).reshape(tok, width)
+
+    resid1 = hidden.astype(f32) + jnp.dot(context, wo_full, preferred_element_type=f32) + bo_full
+    normed1, norm1_pull = jax.vjp(normalize, resid1, g1_full, s1_full)
+    normed1_low = normed1.astype(bf16)
+    pre = jnp.dot(normed1_low, wi_full, preferred_element_type=f32) + bi_full
+    act, gelu_pull = jax.vjp(gelu_exact, pre)
+    act_low = act.astype(bf16)
+    resid2 = normed1 + jnp.dot(act_low, wb_full, preferred_element_type=f32) + bb_full
+    out32, norm2_pull = jax.vjp(normalize, resid2, g2_full, s2_full)
+    output = out32.astype(bf16)
+    d_resid2, grad_gain2, grad_shift2 = norm2_pull(cotangent)
+    d_branch2 = d_resid2.astype(bf16)
+    grad_b_back = jnp.sum(d_resid2, axis=0)
+    grad_w_back = jnp.einsum("tf,td->fd", act_low, d_branch2, preferred_element_type=f32)
+    d_act = jnp.einsum("td,fd->tf", d_branch2, wb_full, preferred_element_type=f32)
+    (d_pre,) = gelu_pull(d_act)
+    grad_b_in = jnp.sum(d_pre, axis=0)
+    d_pre_low = d_pre.astype(bf16)
+    grad_w_in = jnp.einsum("td,tf->df", normed1_low, d_pre_low, preferred_element_type=f32)
+    d_normed1 = d_resid2 + jnp.einsum("tf,df->td", d_pre_low, wi_full, preferred_element_type=f32)
+    d_resid1, grad_gain1, grad_shift1 = norm1_pull(d_normed1)
+    grad_b_out = jnp.sum(d_resid1, axis=0)
+    d_branch1 = d_resid1.astype(bf16)
+    grad_w_out = jnp.einsum("tc,td->cd", context, d_branch1, preferred_element_type=f32)
+    d_context = jnp.einsum("td,cd->tc", d_branch1, wo_full, preferred_element_type=f32).astype(bf16)
+
+    dctx_mine = chip_swap(d_context.reshape(tok, CHIPS, wide).transpose(1, 0, 2), 3, "dctx_swap")
+    d_query, dk_part, dv_part = attend_back(
+        bound, query, keys, values, segq, segk, ctx32, dctx_mine, log_total, hd
+    )
+    dkv = jnp.concatenate([dk_part, dv_part], axis=1).reshape(CHIPS, 2, tok, 2 * wide)
+    dkv_other = mate_swap(dkv.astype(bf16), 4, "dkv_swap")
+    dkv_mine = lax.dynamic_index_in_dim(dkv, core, axis=1, keepdims=False) + dkv_other.astype(f32)
+    d_qkv = jnp.concatenate([d_query, dkv_mine], axis=2).reshape(CHIPS * tok, 3 * wide)
+    bias_grads = jnp.stack([jnp.sum(d_qkv[:, :wide], axis=0), jnp.sum(d_qkv[:, 2 * wide :], axis=0)])
+    d_qkv_low = d_qkv.astype(bf16)
+    gq = (
+        jnp.einsum("td,te->de", hid_mine, d_qkv_low, preferred_element_type=f32)
+        .astype(bf16)
+        .reshape(CHIPS, 2, part, 3 * wide)
+    )
+    dh = (
+        jnp.einsum("te,de->td", d_qkv_low, wq_mine, preferred_element_type=f32)
+        .astype(bf16)
+        .reshape(CHIPS, tok, width)
+    )
+    mine = (jnp.arange(CHIPS) == chip).astype(f32)[:, None, None, None]
+    bias_pack = (mine * bias_grads.reshape(1, 2, 2, part).transpose(0, 2, 1, 3)).reshape(PLANE, 2, part)
+    stack = jnp.concatenate(
+        [bias_pack]
+        + [
+            one.reshape(PLANE, 1, part)
+            for one in (grad_b_out, grad_gain1, grad_shift1, grad_b_back, grad_gain2, grad_shift2)
+        ]
+        + [grad_b_in.reshape(PLANE, fold, part)],
+        axis=1,
+    )
+    stack = jnp.pad(stack, ((0, 0), (0, 16 - stack.shape[1]), (0, 128 - part)))
+    dq, db, di, do, dh_sum, tiny = reduce_all(
+        gq,
+        grad_w_back.astype(bf16).reshape(CHIPS, 2, ff // PLANE, width),
+        grad_w_in.astype(bf16).reshape(CHIPS, 2, part, ff),
+        grad_w_out.astype(bf16).reshape(CHIPS, 2, part, width),
+        dh,
+        stack,
+    )
+    d_hidden = d_resid1 + dh_sum.astype(f32)
+    g_qkv = dq.astype(f32).reshape(CHIPS, part, 3, wide).transpose(1, 2, 0, 3).reshape(part, 3 * width)
+    tiny = tiny[:, :part]
+    return (
+        output,
+        d_hidden,
+        g_qkv,
+        tiny[0:2],
+        do.astype(f32),
+        tiny[2],
+        tiny[3],
+        tiny[4],
+        di.astype(f32),
+        tiny[8 : 8 + fold].reshape(ff // PLANE),
+        db.astype(f32),
+        tiny[5],
+        tiny[6],
+        tiny[7],
+    )
+
+
 def solution(mesh):
     in_specs = (
         P(("replica", "shard"), None),
@@ -390,4 +1224,6 @@
         P("shard"),
         P("shard"),
     )
+    paired = mesh.shape["shard"] == PLANE and mesh.shape["replica"] == LINE
+    body = fast_body if paired else plain_body
     return jax.shard_map(body, mesh=mesh, in_specs=in_specs, out_specs=out_specs, check_vma=False)

time: 794 us -> 375 us (0.47)
  waiting for transfers between devices: 466 us -> 0 us
  Pallas kernels: 0 us -> 249 us
  blocking collectives: 103 us -> 0 us
  loops' own time: 32 us -> 0 us
  local copies, waits for them, and re-layouts: 70.2 us -> 44.1 us
  matrix products: 74.2 us -> 48.7 us
  between operations: 16.9 us -> 1.46 us
    pallas_call x0 -> x7, Pallas kernels: none -> 249 us  [the longest x5 209 us: call(): pl.pallas_call(kernel, out_shape=outs, in_specs=[pl.BlockSpec(memory_spac...]
    reduce_scatter x3 -> x0, waiting for transfers between devices: 153 us -> none  [the longest x1 57.3 us: body(): lax.psum_scatter(local_grads[6].astype(jnp.bfloat16), 'shard', scatter_di...]
    all_gather x8 -> x0, waiting for transfers between devices: 126 us -> none  [the longest x1 38.5 us: body(): lax.all_gather(w_qkv, 'shard', axis=0, tiled=True)]
    unnamed x16 -> x0, waiting for transfers between devices: 120 us -> none
    psum x1 -> x0, waiting for transfers between devices: 66.8 us -> none  [body(): lax.psum(shard_grads[0].astype(jnp.bfloat16), 'replica').astype(jnp.float32)]
    unnamed x2 -> x0, blocking collectives: 47.7 us -> none
    all_gather x5 -> x0, blocking collectives: 43.6 us -> none  [the longest x1 9.31 us: body(): lax.all_gather(log_total, 'shard', axis=1, tiled=True)]
    another operation x15 -> x0, loops' own time: 32 us -> none  [the longest x1 10.8 us: body(): d_query = lax.fori_loop(0, count // query_block, query_step, zero_heads)]
  transfers between devices with their start and end apart: 14 -> 0, of which waited for: 11 -> 0; matrix products, arithmetic and copies ran while one was open for 14% -> 0% of each run, Pallas kernels for 0% -> 0%
where the time goes in v1:
time: 375 us; the launch traced here: 374 us
  Pallas kernels  249 us (66%)
  matrix products  48.7 us (13%)
  local copies, waits for them, and re-layouts  44.1 us (12%)
  other arithmetic  30.8 us (8%)
    pallas_call x5, Pallas kernels, call(): pl.pallas_call(kernel, out_shape=outs, in_specs=[pl.BlockSpec(memory_spac...  209 us
    pallas_call x1, Pallas kernels, attend_back(): pl.pallas_call(functools.partial(attend_back_kernel, hd=hd), grid_spec=pl...  22.4 us
    pallas_call x1, Pallas kernels, attend(): pl.pallas_call(functools.partial(attend_kernel, hd=hd), grid_spec=pltpu.P...  17.9 us
    dot_general x1, matrix products, fast_body(): pre = jnp.dot(normed1_low, wi_full, preferred_element_type=f32) + bi_full  11.4 us
    unnamed x116, local copies, waits for them, and re-layouts  7.93 us

profile of v1, /device:TPU:0, one launch (start us, length us, event | category | flops | bytes accessed | tf_op | source)
XLA Modules:
  0.0 374.3 jit_solution(6739134530328673218)
XLA Ops:
  4.2 1.6 reshape.307
  7.7 73.4 %gather_all.1 = (bf16[8,256,768]{2,1,0:T(8,128)(2,1)}, bf16[8,96,576]{2,1,0:T(8,128)(2,1)}, bf16[8,96,768]{2,1,0:T(8,128)(2,1)}, bf16[8,96,3072]{2,1,0:T(8,128)(...) custom-call(bf16[256,768]{1,0:T(8,128)(2,1)} %hid.1, bf16[4,96,576]{2,1,0:T(8,128)(2,1)} %copy.69.wq, ...), custom_call_target="tpu_custom_call" | custom-call | tf_op jit(solution)/shard_map/gather_all/pallas_call | solution.py:417
  89.5 1.5 constant_dynamic-slice_fusion.2
  92.2 5.4 %fusion.13 = f32[2048,384]{1,0:T(8,128)} fusion(bf16[2048,768]{1,0:T(8,128)(2,1)} %bitcast.112, bf16[768,576]{1,0:T(8,128)(2,1)S(1)} %bitcast.118), kind=kOutput, calls=%fused_computation.58 | convolution fusion | flops 1207959552 | bytes 6881280 | tf_op jit(solution)/shard_map/dot_general | solution.py:1087
  97.9 2.2 fusion.6.v_ref
  100.1 1.7 slice.164.k_ref
  101.8 17.9 %attend.1 = (f32[4,256,192]{2,1,0:T(8,128)S(1)}, bf16[4,256,192]{2,1,0:T(8,128)(2,1)S(1)}, f32[4,256,128]{2,1,0:T(8,128)S(1)}) custom-call(s32[2,4]{1,0:T(2,128)S(1)} %pad_add_fusion.bound, bf16[4,256,192]{2,1,0:T(8,128)(2,1)S(1)} %bitcast.86, bf16[2048,192]{1,0:T(8,128)(2,1)S(1)} %slice.164.k_ref, bf16[2048,192]{1,0:T(8,128)(2,1)S(1)} %fusion.6.v_ref, ...), custom_call_target="tpu_custom_call" | custom-call | tf_op jit(solution)/shard_map/attend/pallas_call | solution.py:643
  122.3 8.5 %ctx_swap.1 = bf16[4,256,192]{2,1,0:T(8,128)(2,1)} custom-call(bf16[4,256,192]{2,1,0:T(8,128)(2,1)} %copy-done.6), custom_call_target="tpu_custom_call" | custom-call | tf_op jit(solution)/shard_map/ctx_swap/pallas_call | solution.py:417
  130.7 1.2 copy.77
  132.0 2.1 fusion.33
  135.0 11.4 %multiply_convert_fusion = (bf16[256,3072]{1,0:T(8,128)(2,1)S(1)}, f32[256,3072]{1,0:T(8,128)}, f32[256,3072]{1,0:T(8,128)}) fusion(f32[3072]{0:T(1024)S(1)} %copy-done.47, bf16[768,3072]{1,0:T(8,128)(2,1)} %bitcast.128, f32[256,768]{1,0:T(8,128)S(1)} %get-tuple-element.88, f32[768]{0:T(1024)S(1)} %copy-done.28, f32[768]{0:T(1024)S(1)} %reshape.349, ...), kind=kOutput, calls=%fused_computation.7 | convolution fusion | flops 1260847104 | bytes 13389824 | tf_op jit(solution)/shard_map/dot_general | solution.py:1110
  146.5 1.5 fusion.34
  150.6 2.6 fusion.31
  153.3 7.2 %fusion.35 = (f32[3072]{0:T(1024)}, bf16[256,3072]{1,0:T(8,128)(2,1)S(1)}) fusion(f32[256,3072]{1,0:T(8,128)} %get-tuple-element.75, f32[256,3072]{1,0:T(8,128)} %get-tuple-element.89, bf16[3072,768]{1,0:T(8,128)(2,1)} %bitcast.132, f32[256,768]{1,0:T(8,128)S(1)} %get-tuple-element.73, f32[256]{0:T(256)S(1)} %negate_multiply_fusion.2), kind=kOutput, calls=%fused_computation.117 | convolution fusion | flops 1220146176 | bytes 13382656 | tf_op jit(solution)/shard_map/td,fd->tf/dot_general | solution.py:1120
  160.5 3.1 multiply_reduce_fusion.1
  164.3 1.7 fusion.30
  167.5 2.5 convolution_convert_fusion.5
  170.1 1.2 copy.78
  171.2 1.9 add_reduce_fusion
  173.1 1.4 reshape.335
  174.4 1.4 reshape.337
  175.8 1.4 reshape.341
  177.2 1.9 add_reduce_fusion.1
  179.0 1.4 reshape.338
  181.4 9.5 %dctx_swap.1.dctx_ref = bf16[4,256,192]{2,1,0:T(8,128)(2,1)} custom-call(bf16[4,256,192]{2,1,0:T(8,128)(2,1)} %bitcast.106), custom_call_target="tpu_custom_call" | custom-call | tf_op jit(solution)/shard_map/dctx_swap/pallas_call | solution.py:417
  190.9 1.0 copy-done.2
  191.9 1.0 copy-done.5
  192.9 22.4 %attend_back.1 = (f32[4,256,192]{2,1,0:T(8,128)S(1)}, f32[2048,192]{1,0:T(8,128)}, f32[2048,192]{1,0:T(8,128)}) custom-call(s32[2,4]{1,0:T(2,128)S(1)} %pad_add_fusion.bound, bf16[4,256,192]{2,1,0:T(8,128)(2,1)S(1)} %bitcast.87, bf16[2048,192]{1,0:T(8,128)(2,1)S(1)} %slice.164.k_ref, bf16[2048,192]{1,0:T(8,128)(2,1)S(1)} %fusion.6.v_ref, ...), custom_call_target="tpu_custom_call" | custom-call | tf_op jit(solution)/shard_map/attend_back/pallas_call | solution.py:729
  215.4 3.2 pad_maximum_fusion
  219.5 1.6 convolution_convert_fusion.3
  221.0 1.4 convert_element_type.208.block
  222.4 11.7 %dkv_swap.1 = bf16[4,256,384]{2,1,0:T(8,128)(2,1)} custom-call(bf16[4,2,256,384]{3,2,1,0:T(8,128)(2,1)} %convert_element_type.208.block), custom_call_target="tpu_custom_call" | custom-call | tf_op jit(solution)/shard_map/dkv_swap/pallas_call | solution.py:417
  234.2 2.6 fusion.29
  236.8 1.6 convolution_convert_fusion.4
  238.4 2.6 convolution_convert_fusion.2
  241.1 1.3 copy.80
  242.5 2.1 pad_maximum_fusion.1
  245.8 5.3 %convolution_convert_fusion = bf16[768,3072]{1,0:T(8,128)(2,1)} fusion(bf16[256,3072]{1,0:T(8,128)(2,1)} %copy-done.22, f32[256,768]{1,0:T(8,128)S(1)} %copy-done.11, f32[768]{0:T(1024)S(1)} %copy-done.29, f32[768]{0:T(1024)S(1)} %reshape.349, f32[256]{0:T(256)S(1)} %copy-done.46, f32[256]{0:T(256)S(1)} %copy-done.36), kind=kOutput, calls=%fused_computation | convolution fusion | flops 1211301888 | bytes 7086080 | tf_op jit(solution)/shard_map/td,tf->df/dot_general | solution.py:1124
  251.1 3.7 convolution_convert_fusion.1
  254.8 105.8 %reduce_all.1 = (bf16[4,96,576]{2,1,0:T(8,128)(2,1)}, bf16[384,768]{1,0:T(8,128)(2,1)}, bf16[96,3072]{1,0:T(8,128)(2,1)}, bf16[96,768]{1,0:T(8,128)(2,1)}, bf16[256,768]{1,0:T(8,128)(2,1)}, /*index=5*/f32[16,128]{1,0:T(8,128)}) custom-call(bf16[4,2,96,576]{3,2,1,0:T(8,128)(2,1)} %bitcast.101, bf16[4,2,384,768]{3,2,1,0:T(8,128)(2,1)} %bitcast.90, ...), custom_call_target="tpu_custom_call" | custom-call | tf_op jit(solution)/shard_map/reduce_all/pallas_call | solution.py:417
  360.6 2.0 convert_add_fusion
  362.6 1.2 slice.118
  364.5 1.4 slice_bitcast_fusion.4
  366.6 1.6 convert_element_type.217
  368.2 1.3 copy.81
  370.4 1.7 reshape.356
  372.1 1.1 convert_element_type.218
  373.2 1.1 convert_element_type.219
  (179 shorter events, 28.5 us)
Async XLA Ops:
  81.1 10.0 %copy-start.26 = (bf16[8,96,576]{2,1,0:T(8,128)(2,1)S(1)}, bf16[8,96,576]{2,1,0:T(8,128)(2,1)}, u32[]{:S(2)}) copy-start(bf16[8,96,576]{2,1,0:T(8,128)(2,1)} %get-tuple-element.34) | copy-start | bytes 2654212
  132.0 14.4 %copy-start.17 = (bf16[256,4,192]{0,2,1:T(8,128)(2,1)}, bf16[256,4,192]{0,2,1:T(8,128)(2,1)S(1)}, u32[]{:S(2)}) copy-start(bf16[256,4,192]{0,2,1:T(8,128)(2,1)S(1)} %copy.77) | copy-start | bytes 1179652
  132.0 2.9 copy-start.28
  132.0 2.9 copy-start.47
  132.0 14.4 %slice-start.2 = ((s8[4718592]{0:T(1024)(128)(4,1)}), s8[4194304]{0:T(1024)(128)(4,1)S(1)}, s32[]{:S(2)}) async-start(s8[4718592]{0:T(1024)(128)(4,1)} %bitcast.133), calls=%async_computation.2 | async-start | bytes 8388608
  134.2 12.3 %copy-start.9 = (f32[256,768]{1,0:T(8,128)}, f32[256,768]{1,0:T(8,128)S(1)}, u32[]{:S(2)}) copy-start(f32[256,768]{1,0:T(8,128)S(1)} %get-tuple-element.88) | copy-start | bytes 2359300
  134.2 12.2 %copy-start.34 = (f32[256]{0:T(256)}, f32[256]{0:T(256)S(1)}, u32[]{:S(2)}) copy-start(f32[256]{0:T(256)S(1)} %broadcast_multiply_fusion.1) | copy-start | bytes 3076
  134.9 11.5 %copy-start.44 = (f32[256]{0:T(256)}, f32[256]{0:T(256)S(1)}, u32[]{:S(2)}) copy-start(f32[256]{0:T(256)S(1)} %fusion.22) | copy-start | bytes 3076
  135.0 11.5 %copy-start.52 = (f32[768]{0:T(1024)S(1)}, f32[768]{0:T(1024)}, u32[]{:S(2)}) copy-start(f32[768]{0:T(1024)} %reshape.352) | copy-start | bytes 9220
  135.0 11.5 %slice-start.3 = ((s8[4718592]{0:T(1024)(128)(4,1)}), s8[524288]{0:T(1024)(128)(4,1)S(1)}, s32[]{:S(2)}) async-start(s8[4718592]{0:T(1024)(128)(4,1)} %bitcast.133), calls=%async_computation.3 | async-start | bytes 1048576
  146.4 1.6 copy-start.19
  146.5 2.4 copy-start.21
  146.5 2.4 copy-start.31
  146.5 4.1 %copy-start.37 = (f32[768]{0:T(1024)S(1)}, f32[768]{0:T(1024)}, u32[]{:S(2)}) copy-start(f32[768]{0:T(1024)} %reshape.354) | copy-start | bytes 9220
  150.6 9.8 %slice-start = ((s8[4718592]{0:T(1024)(128)(4,1)}), s8[4194304]{0:T(1024)(128)(4,1)S(1)}, s32[]{:S(2)}) async-start(s8[4718592]{0:T(1024)(128)(4,1)} %bitcast.129), calls=%async_computation | async-start | bytes 8388608
  153.3 10.4 %copy-start.13 = (f32[256,768]{1,0:T(8,128)}, f32[256,768]{1,0:T(8,128)S(1)}, u32[]{:S(2)}) copy-start(f32[256,768]{1,0:T(8,128)S(1)} %get-tuple-element.73) | copy-start | bytes 2359300
  153.3 7.2 %copy-start.50 = (f32[256]{0:T(256)}, f32[256]{0:T(256)S(1)}, u32[]{:S(2)}) copy-start(f32[256]{0:T(256)S(1)} %negate_multiply_fusion.2) | copy-start | bytes 3076
  153.3 7.2 %copy-start.10 = (f32[256,768]{1,0:T(8,128)S(1)}, f32[256,768]{1,0:T(8,128)}, u32[]{:S(2)}) copy-start(f32[256,768]{1,0:T(8,128)} %copy-done.9) | copy-start | bytes 2359300
  153.3 7.2 %copy-start.35 = (f32[256]{0:T(256)S(1)}, f32[256]{0:T(256)}, u32[]{:S(2)}) copy-start(f32[256]{0:T(256)} %copy-done.34) | copy-start | bytes 3076
  153.3 7.2 %copy-start.45 = (f32[256]{0:T(256)S(1)}, f32[256]{0:T(256)}, u32[]{:S(2)}) copy-start(f32[256]{0:T(256)} %copy-done.44) | copy-start | bytes 3076
  153.3 7.2 %slice-start.1 = ((s8[4718592]{0:T(1024)(128)(4,1)}), s8[524288]{0:T(1024)(128)(4,1)S(1)}, s32[]{:S(2)}) async-start(s8[4718592]{0:T(1024)(128)(4,1)} %bitcast.129), calls=%async_computation.1 | async-start | bytes 1048576
  160.5 3.2 copy-start.22
  160.5 3.8 %copy-start.49 = (f32[256]{0:T(256)S(1)}, f32[256]{0:T(256)}, u32[]{:S(2)}) copy-start(f32[256]{0:T(256)} %copy-done.48) | copy-start | bytes 3076
  215.3 3.3 copy-start
  215.3 4.1 %copy-start.8 = (f32[256,768]{1,0:T(8,128)S(1)}, f32[256,768]{1,0:T(8,128)}, u32[]{:S(2)}) copy-start(f32[256,768]{1,0:T(8,128)} %copy-done.7) | copy-start | bytes 2359300
  215.3 4.1 %copy-start.18 = (bf16[256,4,192]{0,2,1:T(8,128)(2,1)S(1)}, bf16[256,4,192]{0,2,1:T(8,128)(2,1)}, u32[]{:S(2)}) copy-start(bf16[256,4,192]{0,2,1:T(8,128)(2,1)} %copy-done.17) | copy-start | bytes 1179652
  215.4 4.1 %copy-start.33 = (f32[256]{0:T(256)S(1)}, f32[256]{0:T(256)}, u32[]{:S(2)}) copy-start(f32[256]{0:T(256)} %copy-done.32) | copy-start | bytes 3076
  234.1 2.7 copy-start.16
  234.2 2.7 copy-start.25
  236.8 1.6 copy-start.27
  238.4 3.9 %copy-start.1 = (f32[4,256,192]{2,1,0:T(8,128)S(1)}, f32[4,256,192]{2,1,0:T(8,128)}, u32[]{:S(2)}) copy-start(f32[4,256,192]{2,1,0:T(8,128)} %copy-done) | copy-start | bytes 2359300
  242.4 2.5 copy-start.53
  242.4 2.6 copy-start.30
  242.4 2.6 copy-start.38
  242.4 2.6 copy-start.39
  242.4 2.6 copy-start.40
  242.4 2.6 copy-start.41
  242.4 2.6 copy-start.42
  242.4 2.6 copy-start.43
  242.4 3.3 copy-start.11
  242.4 3.3 copy-start.29
  242.5 3.3 copy-start.36
  242.5 3.3 copy-start.46
  245.8 5.3 %copy-start.14 = (f32[256,768]{1,0:T(8,128)S(1)}, f32[256,768]{1,0:T(8,128)}, u32[]{:S(2)}) copy-start(f32[256,768]{1,0:T(8,128)} %copy-done.13) | copy-start | bytes 2359300
  245.8 5.3 %copy-start.20 = (bf16[256,3072]{1,0:T(8,128)(2,1)S(1)}, bf16[256,3072]{1,0:T(8,128)(2,1)}, u32[]{:S(2)}) copy-start(bf16[256,3072]{1,0:T(8,128)(2,1)} %copy-done.19) | copy-start | bytes 4718596
  245.8 5.3 %copy-start.51 = (f32[256]{0:T(256)S(1)}, f32[256]{0:T(256)}, u32[]{:S(2)}) copy-start(f32[256]{0:T(256)} %copy-done.50) | copy-start | bytes 3076
  368.2 3.9 %copy-start.24 = (bf16[96,3072]{1,0:T(8,128)(2,1)S(1)}, bf16[96,3072]{1,0:T(8,128)(2,1)}, u32[]{:S(2)}) copy-start(bf16[96,3072]{1,0:T(8,128)(2,1)} %get-tuple-element.48) | copy-start | bytes 1769476
  369.6 3.6 copy-start.23
  (10 other events, 8.7 us)

commit v2 on v0

--- a/solution.py
+++ b/solution.py
@@ -1,8 +1,11 @@
+import functools
 import math
 
 import jax
 import jax.numpy as jnp
 from jax import lax
+from jax.experimental import pallas as pl
+from jax.experimental.pallas import tpu as pltpu
 from jax.sharding import PartitionSpec as P
 
 HEADS = 12
@@ -51,7 +54,7 @@
     return (probs.astype(jnp.bfloat16), d_scores)
 
 
-def body(
+def plain_body(
     hidden,
     segment_ids,
     w_qkv,
@@ -356,6 +359,968 @@
     return (output, d_hidden) + tuple(total_grads)
 
 
+PLANE = 8
+LINE = 4
+CHIPS = 4
+MESH = pl.DeviceIdType.MESH
+VMEM = pltpu.VMEM
+ANY = pl.ANY
+f32 = jnp.float32
+bf16 = jnp.bfloat16
+
+
+class Wires:
+    def __init__(self, send, recv):
+        self.send, self.recv, self.used = send, recv, 0
+        me = lax.axis_index("shard")
+        self.me = me
+        self.core = me % 2
+        self.chip = me // 2
+        self.mate = me + 1 - 2 * self.core
+        self.xn = me + 2 - 4 * (self.chip % 2)
+        self.yn = me + 4 - 8 * (me // 4)
+        self.dn = self.xn + 4 - 8 * (me // 4)
+        self.cx = self.xn // 2
+        self.cy = self.yn // 2
+        self.cd = self.dn // 2
+
+    def copy(self, src, dst, where):
+        slot = self.used
+        self.used += 1
+        return pltpu.make_async_remote_copy(
+            src_ref=src,
+            dst_ref=dst,
+            send_sem=self.send.at[slot],
+            recv_sem=self.recv.at[slot],
+            device_id=where if isinstance(where, dict) else {"shard": where},
+            device_id_type=MESH,
+        )
+
+    def start(self, src, dst, where):
+        made = self.copy(src, dst, where)
+        made.start()
+        return made
+
+
+def plane_others(me):
+    return [{"shard": (me + step) % PLANE} for step in range(1, PLANE)]
+
+
+def dma_sems(count):
+    return [pltpu.SemaphoreType.DMA((count,)), pltpu.SemaphoreType.DMA((count,))]
+
+
+class Gather:
+    def __init__(self, wires, block, out, local_sem):
+        w = self.w = wires
+        self.out = out
+        self.half = block.shape[0] // 2
+        mine = self.at(w.me)
+        self.own = pltpu.make_async_copy(block, mine, local_sem)
+        self.own.start()
+        self.to_x = w.start(block, mine, w.xn)
+        self.to_y = w.start(block, mine, w.yn)
+        self.to_mate = w.start(block, mine, w.mate)
+
+    def at(self, who, *rows):
+        if rows:
+            return self.out.at[who // 2, who % 2, rows[0]]
+        return self.out.at[who // 2, who % 2]
+
+    def relay(self):
+        w, at, half = self.w, self.at, self.half
+        low, high = pl.ds(0, half), pl.ds(half, half)
+        self.to_x.wait_recv()
+        self.x_on = w.start(at(w.xn, low), at(w.xn, low), w.yn)
+        self.x_mate = w.start(at(w.xn), at(w.xn), w.mate)
+        self.to_y.wait_recv()
+        self.y_on = w.start(at(w.yn, high), at(w.yn, high), w.xn)
+        self.y_mate = w.start(at(w.yn), at(w.yn), w.mate)
+
+    def finish(self):
+        w, at, half = self.w, self.at, self.half
+        low, high = pl.ds(0, half), pl.ds(half, half)
+        self.x_on.wait_recv()
+        self.d_low = w.start(at(w.dn, low), at(w.dn, low), w.mate)
+        self.y_on.wait_recv()
+        self.d_high = w.start(at(w.dn, high), at(w.dn, high), w.mate)
+
+    def done(self):
+        for made in (self.to_mate, self.x_mate, self.y_mate, self.d_low, self.d_high):
+            made.wait_recv()
+        for made in (
+            self.to_x,
+            self.to_y,
+            self.to_mate,
+            self.x_on,
+            self.x_mate,
+            self.y_on,
+            self.y_mate,
+            self.d_low,
+            self.d_high,
+        ):
+            made.wait_send()
+        self.own.wait()
+
+
+SPAN = 512
+AHEAD = 3
+BAND = 32
+
+
+def dot(left, right, left_dim, right_dim):
+    return lax.dot_general(
+        left, right, (((left_dim,), (right_dim,)), ((), ())), preferred_element_type=f32
+    )
+
+
+def turn(block):
+    return block.astype(f32).T
+
+
+def allowed_pairs(segk, segq):
+    return jnp.concatenate([segk] * (segq.shape[1] // 128), axis=1) == segq
+
+
+def upper(block):
+    return jnp.concatenate([block, jnp.zeros_like(block)], axis=0)
+
+
+def lower(block):
+    return jnp.concatenate([jnp.zeros_like(block), block], axis=0)
+
+
+def attend(query, kv_ref, vt_ref, segk_ref, segq, hd):
+    heads, keys = kv_ref.shape[:2]
+    rows = query.shape[1]
+    wide = [upper(query[head * hd : (head + 1) * hd]) for head in range(heads)]
+
+    def step(index, state):
+        at = pl.ds(pl.multiple_of(index * SPAN, SPAN), SPAN)
+        allowed = allowed_pairs(segk_ref[at, :], segq)
+        scores = [
+            jnp.where(allowed, dot(kv_ref[head, at, :], wide[head], 1, 0), masked_value)
+            for head in range(heads)
+        ]
+        made = []
+        for head in range(heads):
+            top, total, acc = state[head]
+            new = jnp.maximum(top, jnp.max(scores[head], axis=0, keepdims=True))
+            weights = jnp.exp(scores[head] - new)
+            factor = jnp.exp(top - new)
+            made.append(
+                (
+                    new,
+                    total * factor + jnp.sum(weights, axis=0, keepdims=True),
+                    acc * factor + dot(vt_ref[head * hd : (head + 1) * hd, at], weights.astype(bf16), 1, 0),
+                )
+            )
+        return tuple(made)
+
+    zero = tuple(
+        (
+            jnp.full((1, rows), 0.5 * masked_value, f32),
+            jnp.zeros((1, rows), f32),
+            jnp.zeros((hd, rows), f32),
+        )
+        for _ in range(heads)
+    )
+    state = lax.fori_loop(0, keys // SPAN, step, zero)
+    return (
+        jnp.concatenate([acc / total for _, total, acc in state], axis=0),
+        jnp.concatenate([top + jnp.log(total) for top, total, _ in state], axis=0),
+    )
+
+
+def attend_back(qt, dt, log, delta, kv_ref, kt_ref, segk_ref, segq, dkv_ref, start, stop, hd):
+    heads = kv_ref.shape[0]
+    rows = qt.shape[1]
+    part = [slice(head * hd, (head + 1) * hd) for head in range(heads)]
+    wide_q = [upper(qt[one]) for one in part]
+    wide_d = [lower(dt[one]) for one in part]
+
+    def step(index, state):
+        at = pl.ds(pl.multiple_of(index * SPAN, SPAN), SPAN)
+        allowed = allowed_pairs(segk_ref[at, :], segq)
+        low = []
+        for head in range(heads):
+            both = kv_ref[head, at, :]
+            scores = dot(both, wide_q[head], 1, 0)
+            d_prob = dot(both, wide_d[head], 1, 0)
+            probs = jnp.where(allowed, jnp.exp(scores - log[head : head + 1]), 0.0)
+            low.append((probs.astype(bf16), (probs * (d_prob - delta[head])).astype(bf16)))
+        made = [
+            state[head] + dot(kt_ref[part[head], at], low[head][1], 1, 0) for head in range(heads)
+        ]
+        dkv_ref[at, :] += jnp.concatenate(
+            [dot(low[head][1], qt[part[head]], 1, 1) for head in range(heads)]
+            + [dot(low[head][0], dt[part[head]], 1, 1) for head in range(heads)],
+            axis=1,
+        )
+        return tuple(made)
+
+    zero = tuple(jnp.zeros((hd, rows), f32) for _ in range(heads))
+    return jnp.concatenate(lax.fori_loop(start, stop, step, zero), axis=0)
+
+
+def add_into(dst, other, out=None):
+    out = dst if out is None else out
+    lead = dst.shape[0] if len(dst.shape) == 3 else 0
+    rows = dst.shape[-2]
+
+    def go(index, carry):
+        if lead:
+            at = (index // (rows // 16), pl.ds(pl.multiple_of((index % (rows // 16)) * 16, 16), 16))
+        else:
+            at = (pl.ds(pl.multiple_of(index * 16, 16), 16),)
+        out[at] = (dst[at].astype(f32) + other[at].astype(f32)).astype(out.dtype)
+        return carry
+
+    lax.fori_loop(0, max(lead, 1) * (rows // 16), go, 0)
+
+
+class Reduce:
+    def __init__(self, wires, full, pair, land, pick):
+        self.w, self.full, self.pair, self.land = wires, full, pair, land
+        self.half = pair.shape[1] // 2
+        self.pick = pick
+        if full is not None:
+            self.meet = wires.copy(pick(full, 1 - wires.core), pair, wires.mate)
+
+    def first(self):
+        w, pair, land = self.w, self.pair, self.land
+        low, high = pl.ds(0, self.half), pl.ds(self.half, self.half)
+        if self.full is not None:
+            self.meet.wait_recv()
+            add_into(pair, self.pick(self.full, w.core))
+        self.x0 = w.start(pair.at[w.cd, low], land.at[1], w.xn)
+        self.y0 = w.start(pair.at[w.cd, high], land.at[3], w.yn)
+        self.x1 = w.start(pair.at[w.cx, low], land.at[0], w.xn)
+        self.y1 = w.start(pair.at[w.cy, high], land.at[2], w.yn)
+
+    def second(self):
+        w, pair, land = self.w, self.pair, self.land
+        low, high = pl.ds(0, self.half), pl.ds(self.half, self.half)
+        self.x0.wait_recv()
+        add_into(pair.at[w.cy, low], land.at[1])
+        self.y2 = w.start(pair.at[w.cy, low], land.at[4], w.yn)
+        self.y0.wait_recv()
+        add_into(pair.at[w.cx, high], land.at[3])
+        self.x2 = w.start(pair.at[w.cx, high], land.at[5], w.xn)
+        self.x1.wait_recv()
+        add_into(pair.at[w.chip, low], land.at[0])
+        self.y1.wait_recv()
+        add_into(pair.at[w.chip, high], land.at[2])
+
+    def third(self, out):
+        w, pair, land = self.w, self.pair, self.land
+        low, high = pl.ds(0, self.half), pl.ds(self.half, self.half)
+        self.y2.wait_recv()
+        add_into(pair.at[w.chip, low], land.at[4], out.at[low])
+        self.x2.wait_recv()
+        add_into(pair.at[w.chip, high], land.at[5], out.at[high])
+
+    def done(self):
+        made = [self.x0, self.x1, self.y0, self.y1, self.x2, self.y2]
+        if self.full is not None:
+            made.append(self.meet)
+        for one in made:
+            one.wait_send()
+
+
+class Line:
+    def __init__(self, wires, z, block, land, out):
+        self.w, self.z, self.block, self.land, self.out = wires, z, block, land, out
+        self.edge = (z == 0) | (z == LINE - 1)
+        self.inner = {"replica": 1 + z // 2}
+        self.outer = {"replica": 3 * (z // 2)}
+        self.across = {"replica": 2 - z // 2}
+        self.up = wires.copy(block, land.at[0], self.inner)
+        self.over = wires.copy(block, land.at[1], {"replica": 3 - z})
+        self.back = wires.copy(out, out, self.outer)
+
+    def first(self):
+        @pl.when(self.edge)
+        def _():
+            self.up.start()
+
+    def second(self):
+        @pl.when(jnp.logical_not(self.edge))
+        def _():
+            self.up.wait_recv()
+            add_into(self.block, self.land.at[0])
+            self.over.start()
+
+    def third(self):
+        @pl.when(jnp.logical_not(self.edge))
+        def _():
+            self.over.wait_recv()
+            add_into(self.block, self.land.at[1], self.out)
+            self.back.start()
+
+    def done(self):
+        @pl.when(self.edge)
+        def _():
+            self.up.wait_send()
+            self.back.wait_recv()
+
+        @pl.when(jnp.logical_not(self.edge))
+        def _():
+            self.over.wait_send()
+            self.back.wait_send()
+
+
+def each(rows, block, step, init):
+    def go(index, carry):
+        return step(pl.ds(pl.multiple_of(index * block, block), block), carry)
+
+    return lax.fori_loop(0, rows // block, go, init)
+
+
+def fold_rows(block):
+    return jnp.sum(block.reshape(block.shape[0] // 8, 8, block.shape[1]), axis=0)
+
+
+def settle(block):
+    return jnp.sum(block, axis=0, keepdims=True)
+
+
+def vector(small, row, part):
+    return jnp.concatenate(
+        [small[source, row : row + 1, :part].astype(f32) for source in range(PLANE)], axis=1
+    )
+
+
+def put_vector(stack, row, value, part):
+    for source in range(PLANE):
+        stack[source, row : row + 1, :part] = value[:, source * part : (source + 1) * part]
+
+
+def moments(block):
+    mean_value = jnp.mean(block, axis=-1, keepdims=True)
+    centered = block - mean_value
+    scale = lax.rsqrt(jnp.mean(centered * centered, axis=-1, keepdims=True) + norm_epsilon)
+    return centered * scale, scale
+
+
+def norm_back(grad, gain, unit, scale):
+    scaled = grad * gain
+    return (
+        scaled
+        - jnp.mean(scaled, axis=-1, keepdims=True)
+        - unit * jnp.mean(scaled * unit, axis=-1, keepdims=True)
+    ) * scale
+
+
+def layer_kernel(
+    hid,
+    wq,
+    small,
+    wo,
+    wi,
+    wb,
+    cot,
+    out_o,
+    dq_o,
+    db_o,
+    di_o,
+    do_o,
+    dh_o,
+    small_o,
+    wo_s,
+    wi_s,
+    wb_s,
+    names_s,
+    wq_s,
+    wq_a,
+    hid_s,
+    hidt,
+    qt,
+    kv_s,
+    kt,
+    vt,
+    segk,
+    segq,
+    ctx32,
+    log,
+    ctx_s,
+    ctxt,
+    acc_s,
+    unit_s,
+    scale_s,
+    low_s,
+    lowt_s,
+    act_s,
+    slope_s,
+    wide_s,
+    grad_s,
+    resid_s,
+    dctx_s,
+    dkv_a,
+    dqkv_s,
+    gq_s,
+    tiny_s,
+    q_pair,
+    q_all,
+    pair,
+    land,
+    dh_land,
+    part_s,
+    s_land,
+    s_sum,
+    zq_land,
+    z_land,
+    zs_land,
+    send,
+    recv,
+    loc,
+    *,
+    hd,
+):
+    w = Wires(send, recv)
+    z = lax.axis_index("replica")
+    me, core = w.me, w.core
+    tok, width = hid.shape
+    wide = width // CHIPS
+    heads = wide // hd
+    ff = wi.shape[1]
+    part = width // PLANE
+    fold = ff // width
+    rows_in = ff // PLANE // 128
+    seg_row = 8 + rows_in
+
+    barrier = pltpu.get_barrier_semaphore()
+    for other in plane_others(me):
+        pl.semaphore_signal(barrier, inc=1, device_id=other, device_id_type=MESH)
+    edge = (z == 0) | (z == LINE - 1)
+
+    @pl.when(edge)
+    def _():
+        pl.semaphore_signal(barrier, inc=1, device_id={"replica": 1 + z // 2}, device_id_type=MESH)
+
+    @pl.when(jnp.logical_not(edge))
+    def _():
+        pl.semaphore_signal(barrier, inc=1, device_id={"replica": 3 * (z // 2)}, device_id_type=MESH)
+        pl.semaphore_signal(barrier, inc=1, device_id={"replica": 3 - z}, device_id_type=MESH)
+
+    for chip in range(CHIPS):
+        for place, section in enumerate((1, 2, 0)):
+            start = section * width + chip * wide
+            wq_s[chip, :, place * wide : (place + 1) * wide] = wq[:, start : start + wide]
+
+    @pl.when(edge)
+    def _():
+        pl.semaphore_wait(barrier, PLANE)
+
+    @pl.when(jnp.logical_not(edge))
+    def _():
+        pl.semaphore_wait(barrier, PLANE + 1)
+
+    names_s[me] = small[...]
+    first = Gather(w, hid, hid_s, loc.at[0])
+    wq_a[me] = wq_s[w.chip]
+    q_mate = w.start(wq_s.at[w.chip], wq_a.at[me], w.mate)
+    q_d = w.start(wq_s.at[w.cd], wq_a.at[me], w.dn)
+    q_x = w.start(wq_s.at[w.cx], wq_a.at[me], w.xn)
+    q_y = w.start(wq_s.at[w.cy], wq_a.at[me], w.yn)
+    smalls = [w.start(small, names_s.at[me], (me + step) % PLANE) for step in range(1, PLANE)]
+    first.relay()
+    q_on = []
+    for came, source in ((q_x, w.xn), (q_y, w.yn), (q_d, w.dn)):
+        came.wait_recv()
+        q_on.append(w.start(wq_a.at[source], wq_a.at[source], w.mate))
+    rest = [
+        Gather(w, block, out, loc.at[1 + slot])
+        for slot, (block, out) in enumerate(((wo, wo_s), (wi, wi_s), (wb, wb_s)))
+    ]
+    for made in smalls:
+        made.wait_recv()
+    for source in range(PLANE):
+        ids = names_s[source].astype(f32)[seg_row : seg_row + tok // 128]
+        segq[source] = jnp.concatenate([ids[one : one + 1] for one in range(tok // 128)], axis=1)
+        for one in range(tok // 128):
+            at = source * tok + one * 128
+            segk[at : at + 128, :] = jnp.broadcast_to(ids[one : one + 1], (128, 128)).T
+    first.finish()
+    for made in [q_mate] + q_on:
+        made.wait_recv()
+    first.done()
+
+    names = [names_s[2 * w.chip + side].astype(f32).T for side in range(2)]
+    bias_q = jnp.concatenate([one[:part, 0:1] for one in names], axis=0)
+    bias_v = jnp.concatenate([one[:part, 1:2] for one in names], axis=0)
+
+    def project(index, carry):
+        for mine in (True, False):
+            side = core if mine else 1 - core
+            block = hid_s[index, side]
+            weight = wq_a[...].reshape(width, 3 * wide)
+            rows = pl.ds(pl.multiple_of((2 * index + side) * tok, tok), tok)
+            kv = dot(block, weight if mine else weight[:, : 2 * wide], 1, 0)
+            kvt = kv.T
+            low_v = (kvt[wide : 2 * wide] + bias_v).astype(bf16)
+            kt[:, rows] = kvt[:wide].astype(bf16)
+            vt[:, rows] = low_v
+            back = turn(low_v)
+            for head in range(heads):
+                cols = slice(head * hd, (head + 1) * hd)
+                kv_s[head, rows, :] = jnp.concatenate([kv[:, cols], back[:, cols]], axis=1).astype(bf16)
+            if mine:
+                query = kvt[2 * wide :] + bias_q
+                qt[index] = (query.astype(bf16).astype(f32) * scale_factor).astype(bf16)
+                hidt[index] = turn(block).astype(bf16)
+        return carry
+
+    lax.fori_loop(0, CHIPS, project, 0)
+    rest[0].relay()
+
+    def one_block(turn_no, carry):
+        index = (
+            (turn_no == 0) * w.cd + (turn_no == 1) * w.cx + (turn_no == 2) * w.cy + (turn_no == 3) * w.chip
+        )
+        context, logs = attend(qt[index], kv_s, vt, segk, segq[2 * index + core], hd)
+        ctx32[index] = context
+        ctx_s[index] = context.astype(bf16)
+        log[index] = logs
+        return carry
+
+    lax.fori_loop(0, 2, one_block, 0)
+    c_d = w.start(ctx_s.at[w.cd], ctxt.at[w.chip], w.dn)
+    c_x = w.start(ctx_s.at[w.cx], ctxt.at[w.chip], w.xn)
+    rest[1].relay()
+    rest[0].finish()
+    lax.fori_loop(2, 4, one_block, 0)
+    c_y = w.start(ctx_s.at[w.cy], ctxt.at[w.chip], w.yn)
+    ctxt[w.chip] = ctx_s[w.chip]
+    rest[1].finish()
+    rest[2].relay()
+    rest[0].done()
+    for made in (c_d, c_x, c_y):
+        made.wait()
+
+    wo_v = wo_s[...].reshape(width, width)
+    bo, g1, s1, bb, g2, s2 = (vector(names_s, row, part) for row in range(2, 8))
+    tiny_s[...] = jnp.zeros_like(tiny_s)
+    acc_s[...] = dot(turn(ctxt[...].reshape(width, tok)).astype(bf16), wo_v, 1, 0)
+
+    def open_one(at, carry):
+        unit, scale = moments(hid[at, :].astype(f32) + acc_s[at, :] + bo)
+        unit_s[at, :] = unit
+        scale_s[at, :] = jnp.broadcast_to(scale, (BAND, 128))
+        normed = unit * g1 + s1
+        low_s[at, :] = normed.astype(bf16)
+        acc_s[at, :] = normed + bb
+        return carry
+
+    each(tok, BAND, open_one, 0)
+    lowt_s[...] = turn(low_s[...]).astype(bf16)
+    rest[1].done()
+
+    def up(chunk, carry):
+        cols = pl.ds(pl.multiple_of(chunk * width, width), width)
+        bias = jnp.concatenate(
+            [
+                names_s[2 * chunk + side, 8 + row : 9 + row, :].astype(f32)
+                for side in range(2)
+                for row in range(rows_in)
+            ],
+            axis=1,
+        )
+        wide_s[...] = dot(low_s[...], wi_s[:, :, :, cols].reshape(width, width), 1, 0)
+
+        def gelu(at, carry):
+            pre = wide_s[at, :] + bias
+            phi = 0.5 * (1.0 + lax.erf(pre * math.sqrt(0.5)))
+            act_s[chunk, at, :] = (pre * phi).astype(bf16)
+            slope_s[chunk, at, :] = phi + pre * (
+                jnp.exp(-0.5 * pre * pre) * (1.0 / math.sqrt(2.0 * math.pi))
+            )
+            return carry
+
+        each(tok, BAND, gelu, 0)
+        return carry
+
+    lax.fori_loop(0, fold, up, 0)
+    rest[2].finish()
+    rest[2].done()
+
+    def join_back(chunk, carry):
+        acc_s[...] += dot(act_s[chunk], wb_s[chunk].reshape(width, width), 1, 0)
+        return carry
+
+    lax.fori_loop(0, fold, join_back, 0)
+
+    zero = jnp.zeros((8, width), f32)
+
+    def close(at, sums):
+        unit, scale = moments(acc_s[at, :])
+        out_o[at, :] = (unit * g2 + s2).astype(bf16)
+        grad = cot[at, :]
+        d_resid = norm_back(grad, g2, unit, scale)
+        acc_s[at, :] = d_resid
+        grad_s[at, :] = d_resid.astype(bf16)
+        return (sums[0] + fold_rows(d_resid), sums[1] + fold_rows(grad * unit), sums[2] + fold_rows(grad))
+
+    sums = each(tok, BAND, close, (zero, zero, zero))
+    for row, value in zip((5, 6, 7), sums):
+        put_vector(tiny_s, row, settle(value), part)
+
+    def down(chunk, carry):
+        grad = grad_s[...]
+        wide_s[...] = dot(grad, wb_s[chunk].reshape(width, width), 1, 1)
+        wb_s[chunk] = (
+            dot(turn(act_s[chunk]).astype(bf16), grad, 1, 0).astype(bf16).reshape(2, ff // PLANE, width)
+        )
+
+        def through(at, sums):
+            d_pre = wide_s[at, :] * slope_s[chunk, at, :]
+            act_s[chunk, at, :] = d_pre.astype(bf16)
+            return sums + fold_rows(d_pre)
+
+        total = settle(each(tok, BAND, through, zero))
+        for side in range(2):
+            for row in range(rows_in):
+                start = (side * rows_in + row) * 128
+                tiny_s[2 * chunk + side, 8 + row : 9 + row, :] = total[:, start : start + 128]
+        return carry
+
+    lax.fori_loop(0, fold, down, 0)
+
+    picks = []
+    for slot in range(wb.shape[0] // part):
+        at = pl.ds(slot * part, part)
+        picks.append((wb_s, lambda ref, core, at=at: ref.at[:, core, at], db_o.at[at]))
+    for slot in range(fold):
+        at = pl.ds(slot * width, width)
+        picks.append((wi_s, lambda ref, core, at=at: ref.at[:, core, :, at], di_o.at[:, at]))
+    picks.append((wo_s, lambda ref, core: ref.at[:, core], do_o))
+    count = len(picks)
+    chunks = [
+        Reduce(w, full, pair.at[slot], land.at[slot], pick)
+        for slot, (full, pick, _) in enumerate(picks)
+    ]
+    lines = [
+        Line(w, z, part_s.at[slot], z_land.at[slot], out) for slot, (_, _, out) in enumerate(picks)
+    ]
+    for one in chunks[:AHEAD]:
+        one.meet.start()
+    ticks = 0
+
+    def tick():
+        nonlocal ticks
+        now = ticks
+        ticks += 1
+        if now + AHEAD < count:
+            chunks[now + AHEAD].meet.start()
+        if now < count:
+            chunks[now].first()
+        if 0 <= now - 1 < count:
+            chunks[now - 1].second()
+        if 0 <= now - 2 < count:
+            chunks[now - 2].third(part_s.at[now - 2])
+            lines[now - 2].first()
+        if 0 <= now - 3 < count:
+            lines[now - 3].second()
+        if 0 <= now - 4 < count:
+            lines[now - 4].third()
+
+    for chunk in range(fold):
+        cols = slice(chunk * width, (chunk + 1) * width)
+        d_low = act_s[chunk]
+        acc_s[...] += dot(d_low, wi_s[:, :, :, cols].reshape(width, width), 1, 1)
+        wi_s[:, :, :, cols] = dot(lowt_s[...], d_low, 1, 0).astype(bf16).reshape(CHIPS, 2, part, width)
+        tick()
+
+    def finish(at, sums):
+        unit = unit_s[at, :]
+        grad = acc_s[at, :]
+        d_resid = norm_back(grad, g1, unit, scale_s[at, 0:1])
+        resid_s[at, :] = d_resid
+        grad_s[at, :] = d_resid.astype(bf16)
+        return (sums[0] + fold_rows(d_resid), sums[1] + fold_rows(grad * unit), sums[2] + fold_rows(grad))
+
+    sums = each(tok, BAND, finish, (zero, zero, zero))
+    grad = grad_s[...]
+    ctx_s[...] = dot(wo_s[...].reshape(width, width), grad, 1, 1).astype(bf16).reshape(CHIPS, wide, tok)
+    dctx_made = [
+        w.start(ctx_s.at[chip], dctx_s.at[w.chip], who)
+        for chip, who in ((w.cx, w.xn), (w.cy, w.yn), (w.cd, w.dn))
+    ]
+    dctx_s[w.chip] = ctx_s[w.chip]
+    wo_s[...] = dot(ctxt[...].reshape(width, tok), grad, 1, 0).astype(bf16).reshape(CHIPS, 2, part, width)
+    for row, value in zip((2, 3, 4), sums):
+        put_vector(tiny_s, row, settle(value), part)
+    tick()
+
+    dq_s = slope_s.at[:, 0:wide, 0:tok]
+    dkv_a[...] = jnp.zeros_like(dkv_a)
+    steps = PLANE * tok // SPAN
+    for turn_no, index in enumerate((w.chip, w.cx, w.cy, w.cd)):
+        if turn_no:
+            dctx_made[turn_no - 1].wait_recv()
+        dt = dctx_s[index]
+        product = dt.astype(f32) * ctx32[index]
+        delta = [
+            jnp.sum(product[head * hd : (head + 1) * hd], axis=0, keepdims=True) for head in range(heads)
+        ]
+        dq_s[index] = attend_back(
+            qt[index], dt, log[index], delta, kv_s, kt, segk, segq[2 * index + core], dkv_a, 0, steps, hd
+        )
+        tick()
+
+    dkv_s = hid_s.at[:, 0, :, 0 : 2 * wide]
+    dkv_land = hid_s.at[:, 1, :, 0 : 2 * wide]
+
+    def away(index, carry):
+        at = pl.ds(pl.multiple_of((2 * index + 1 - core) * tok, tok), tok)
+        dkv_s[index] = dkv_a[at, :].astype(bf16)
+        return carry
+
+    lax.fori_loop(0, CHIPS, away, 0)
+    meet = w.start(dkv_s, dkv_land, w.mate)
+    tick()
+    meet.wait_recv()
+
+    def join(index, sums):
+        at = pl.ds(pl.multiple_of((2 * index + core) * tok, tok), tok)
+        dkv = dkv_a[at, :] + dkv_land[index].astype(f32)
+        dqkv = jnp.concatenate([dkv, (dq_s[index] * scale_factor).T], axis=1)
+        dqkv_s[index] = dqkv.astype(bf16)
+        return sums + jnp.sum(dqkv, axis=0, keepdims=True)
+
+    sums = lax.fori_loop(0, CHIPS, join, jnp.zeros((1, 3 * wide), f32))
+    for half in range(2):
+        at = slice(half * width // 2, (half + 1) * width // 2)
+        total = sum(dot(hidt[index, at, :], dqkv_s[index], 1, 0) for index in range(CHIPS))
+        gq_s[2 * half : 2 * half + 2] = total.astype(bf16).reshape(2, 2, part, 3 * wide)
+    q_meet = w.start(gq_s.at[:, 1 - core], q_pair, w.mate)
+    for side in range(2):
+        slot = 2 * w.chip + side
+        tiny_s[slot, 0:1, :part] = sums[:, 2 * wide + side * part : 2 * wide + (side + 1) * part]
+        tiny_s[slot, 1:2, :part] = sums[:, wide + side * part : wide + (side + 1) * part]
+    tinies = [
+        w.start(tiny_s.at[(me + step) % PLANE], s_land.at[me], (me + step) % PLANE)
+        for step in range(1, PLANE)
+    ]
+    s_land[me] = tiny_s[me]
+    dh_s = act_s
+    hidden = Reduce(w, None, dh_s, dh_land, None)
+
+    q_meet.wait_recv()
+    add_into(q_pair, gq_s.at[:, core])
+    q_made = [
+        w.start(q_pair.at[chip], q_all.at[w.chip], who)
+        for chip, who in ((w.cx, w.xn), (w.cy, w.yn), (w.cd, w.dn))
+    ]
+    q_all[w.chip] = q_pair[w.chip]
+    q_lines = [
+        Line(w, z, q_all.at[chip], zq_land.at[chip], dq_o.at[chip]) for chip in (w.chip, w.cx, w.cy, w.cd)
+    ]
+    q_lines[0].first()
+
+    def input_grad(index, carry):
+        dh_s[index] = dot(dqkv_s[index], wq_a[...].reshape(width, 3 * wide), 1, 1).astype(bf16)
+        return carry
+
+    lax.fori_loop(0, CHIPS, input_grad, 0)
+    hidden.first()
+    tick()
+    for one in tinies:
+        one.wait_recv()
+    s_sum[...] = jnp.sum(s_land[...], axis=0)
+    s_line = Line(w, z, s_sum, zs_land, small_o)
+    s_line.first()
+    for slot in (1, 2, 3):
+        q_made[slot - 1].wait_recv()
+        q_lines[slot].first()
+        q_lines[slot - 1].second()
+        if slot > 1:
+            q_lines[slot - 2].third()
+    tick()
+    s_line.second()
+    q_lines[3].second()
+    q_lines[2].third()
+    hidden.second()
+    while ticks < count + 4:
+        tick()
+    s_line.third()
+    q_lines[3].third()
+    hidden.third(dh_o)
+    for one in [q_mate, q_x, q_y, q_d] + q_on + smalls + tinies + q_made + [q_meet, meet] + dctx_made:
+        one.wait_send()
+    for one in chunks + [hidden]:
+        one.done()
+    for one in lines + q_lines + [s_line]:
+        one.done()
+    dh_o[...] = (resid_s[...] + dh_o[...].astype(f32)).astype(dh_o.dtype)
+
+
+def layer_all(hid, wq, small, wo, wi, wb, cot, hd):
+    tok, width = hid.shape
+    wide = width // CHIPS
+    part = wq.shape[0]
+    ff = wi.shape[1]
+    fold = ff // width
+    seq = PLANE * tok
+    rows, cols = wo.shape
+    count = wb.shape[0] // rows + fold + 1
+    q_block = (CHIPS, part, 3 * wide)
+    shape = jax.ShapeDtypeStruct
+    outs = [
+        shape((tok, width), bf16),
+        shape(q_block, bf16),
+        shape(wb.shape, bf16),
+        shape(wi.shape, bf16),
+        shape(wo.shape, bf16),
+        shape((tok, width), f32),
+        shape((16, 128), f32),
+    ]
+    pairs = (CHIPS, 2)
+    heads_block = (CHIPS, wide, tok)
+    scratch = [
+        VMEM(pairs + wo.shape, bf16),
+        VMEM(pairs + wi.shape, bf16),
+        VMEM(pairs + wb.shape, bf16),
+        VMEM((PLANE, 16, 128), bf16),
+        VMEM(q_block, bf16),
+        VMEM((PLANE, part, 3 * wide), bf16),
+        VMEM(pairs + (tok, width), bf16),
+        VMEM((CHIPS, width, tok), bf16),
+        VMEM(heads_block, bf16),
+        VMEM((wide // hd, seq, 2 * hd), bf16),
+        VMEM((wide, seq), bf16),
+        VMEM((wide, seq), bf16),
+        VMEM((seq, 128), f32),
+        VMEM((PLANE, 1, tok), f32),
+        VMEM(heads_block, f32),
+        VMEM((CHIPS, wide // hd, tok), f32),
+        VMEM(heads_block, bf16),
+        VMEM(heads_block, bf16),
+        VMEM((tok, width), f32),
+        VMEM((tok, width), f32),
+        VMEM((tok, 128), f32),
+        VMEM((tok, width), bf16),
+        VMEM((width, tok), bf16),
+        VMEM((fold, tok, width), bf16),
+        VMEM((fold, tok, width), f32),
+        VMEM((tok, width), f32),
+        VMEM((tok, width), bf16),
+        VMEM((tok, width), f32),
+        VMEM(heads_block, bf16),
+        VMEM((seq, 2 * wide), f32),
+        VMEM((CHIPS, tok, 3 * wide), bf16),
+        VMEM(pairs + (part, 3 * wide), bf16),
+        VMEM((PLANE, 16, 128), f32),
+        VMEM(q_block, bf16),
+        VMEM(q_block, bf16),
+        VMEM((count, CHIPS, rows, cols), bf16),
+        VMEM((count, 6, rows // 2, cols), bf16),
+        VMEM((6, tok // 2, width), bf16),
+        VMEM((count, rows, cols), bf16),
+        VMEM((PLANE, 16, 128), f32),
+        VMEM((16, 128), f32),
+        VMEM((CHIPS, 2) + q_block[1:], bf16),
+        VMEM((count, 2, rows, cols), bf16),
+        VMEM((2, 16, 128), f32),
+    ]
+    return pl.pallas_call(
+        functools.partial(layer_kernel, hd=hd),
+        out_shape=outs,
+        in_specs=[pl.BlockSpec(memory_space=VMEM)] * 7,
+        out_specs=[pl.BlockSpec(memory_space=VMEM)] * 7,
+        scratch_shapes=scratch + dma_sems(count * 10 + 100) + [pltpu.SemaphoreType.DMA((4,))],
+        compiler_params=pltpu.CompilerParams(
+            collective_id=1, has_side_effects=True, vmem_limit_bytes=67043328
+        ),
+        name="layer_all",
+    )(hid, wq, small, wo, wi, wb, cot)
+
+
+def finish_kernel(dq, db, di, do, dh, out, q_o, b_o, i_o, o_o, h_o, out_o):
+    wide = dq.shape[2] // 3
+    width = dh.shape[1]
+    for chip in range(CHIPS):
+        for place, section in enumerate((1, 2, 0)):
+            start = section * width + chip * wide
+            q_o[:, start : start + wide] = dq[chip, :, place * wide : (place + 1) * wide].astype(f32)
+    b_o[...] = db[...].astype(f32)
+    i_o[...] = di[...].astype(f32)
+    o_o[...] = do[...].astype(f32)
+    h_o[...] = dh[...]
+    out_o[...] = out[...]
+
+
+def finish_all(dq, db, di, do, dh, out):
+    part, wide = dq.shape[1:]
+    shape = jax.ShapeDtypeStruct
+    outs = [shape((part, CHIPS * wide), f32)] + [shape(one.shape, f32) for one in (db, di, do, dh)]
+    outs.append(shape(out.shape, out.dtype))
+    return pl.pallas_call(
+        finish_kernel,
+        out_shape=outs,
+        in_specs=[pl.BlockSpec(memory_space=VMEM)] * 6,
+        out_specs=[pl.BlockSpec(memory_space=VMEM)] * 6,
+        compiler_params=pltpu.CompilerParams(vmem_limit_bytes=32 << 20),
+        name="finish_all",
+    )(dq, db, di, do, dh, out)
+
+
+def fast_body(
+    hidden,
+    segment_ids,
+    w_qkv,
+    b_qv,
+    w_out,
+    b_out,
+    gain1,
+    shift1,
+    w_in,
+    b_in,
+    w_back,
+    b_back,
+    gain2,
+    shift2,
+    cotangent,
+):
+    tok, width = hidden.shape
+    hd = width // HEADS
+    part = w_qkv.shape[0]
+    ff = w_in.shape[1]
+    lines = b_in.shape[0] // 128
+    narrow = jnp.concatenate(
+        [b_qv] + [one[None] for one in (b_out, gain1, shift1, b_back, gain2, shift2)], axis=0
+    )
+    small = jnp.concatenate(
+        [
+            jnp.pad(narrow, ((0, 0), (0, 128 - part))),
+            b_in.reshape(lines, 128),
+            segment_ids.astype(bf16).reshape(tok // 128, 128),
+            jnp.zeros((8 - lines - tok // 128, 128), bf16),
+        ],
+        axis=0,
+    )
+    output, dq, db, di, do, dh, tiny = layer_all(
+        hidden, w_qkv, small, w_out, w_in, w_back, cotangent, hd
+    )
+    g_qkv, g_back, g_in, g_out, d_hidden, output = finish_all(dq, db, di, do, dh, output)
+    return (
+        output,
+        d_hidden,
+        g_qkv,
+        tiny[0:2, :part],
+        g_out,
+        tiny[2, :part],
+        tiny[3, :part],
+        tiny[4, :part],
+        g_in,
+        tiny[8 : 8 + lines].reshape(ff // PLANE),
+        g_back,
+        tiny[5, :part],
+        tiny[6, :part],
+        tiny[7, :part],
+    )
+
+
 def solution(mesh):
     in_specs = (
         P(("replica", "shard"), None),
@@ -390,4 +1355,6 @@
         P("shard"),
         P("shard"),
     )
+    paired = mesh.shape["shard"] == PLANE and mesh.shape["replica"] == LINE
+    body = fast_body if paired else plain_body
     return jax.shard_map(body, mesh=mesh, in_specs=in_specs, out_specs=out_specs, check_vma=False)

time: 794 us -> 199 us (0.25)
  waiting for transfers between devices: 466 us -> 0 us
  Pallas kernels: 0 us -> 185 us
  blocking collectives: 103 us -> 0 us
  matrix products: 74.2 us -> 0 us
  local copies, waits for them, and re-layouts: 70.2 us -> 11 us
  loops' own time: 32 us -> 0 us
  other arithmetic: 24.2 us -> 2.03 us
  between operations: 16.9 us -> 0.67 us
    pallas_call x0 -> x2, Pallas kernels: none -> 185 us  [the longest x1 183 us: layer_all(): pl.pallas_call(functools.partial(layer_kernel, hd=hd), out_shape=outs, in...]
    reduce_scatter x3 -> x0, waiting for transfers between devices: 153 us -> none  [the longest x1 57.3 us: body(): lax.psum_scatter(local_grads[6].astype(jnp.bfloat16), 'shard', scatter_di...]
    all_gather x8 -> x0, waiting for transfers between devices: 126 us -> none  [the longest x1 38.5 us: body(): lax.all_gather(w_qkv, 'shard', axis=0, tiled=True)]
    unnamed x16 -> x0, waiting for transfers between devices: 120 us -> none
    dot_general x19 -> x0, matrix products: 74.2 us -> none  [the longest x1 11.8 us: body(): jnp.dot(normed1_low, wi_full, preferred_element_type=jnp.float32)]
    psum x1 -> x0, waiting for transfers between devices: 66.8 us -> none  [body(): lax.psum(shard_grads[0].astype(jnp.bfloat16), 'replica').astype(jnp.float32)]
    unnamed x2 -> x0, blocking collectives: 47.7 us -> none
    all_gather x5 -> x0, blocking collectives: 43.6 us -> none  [the longest x1 9.31 us: body(): lax.all_gather(log_total, 'shard', axis=1, tiled=True)]
  transfers between devices with their start and end apart: 14 -> 0, of which waited for: 11 -> 0; matrix products, arithmetic and copies ran while one was open for 14% -> 0% of each run, Pallas kernels for 0% -> 0%
where the time goes in v2:
time: 199 us
  Pallas kernels  185 us (93%)
  local copies, waits for them, and re-layouts  11 us (6%)
  other arithmetic  2.03 us (1%)
    pallas_call x1, Pallas kernels, layer_all(): pl.pallas_call(functools.partial(layer_kernel, hd=hd), out_shape=outs, in...  183 us
    unnamed x12, local copies, waits for them, and re-layouts  6.19 us

profile of v2, /device:TPU:0, one launch (start us, length us, event | category | flops | bytes accessed | tf_op | source)
XLA Modules:
  0.0 198.7 jit_solution(9513671184375092604)
XLA Ops:
  0.6 0.7 convert_bitcast_fusion
  1.3 0.1 pad.8.clone
  1.4 0.8 concatenate.6
  2.2 1.3 fusion.3.small
  3.5 182.6 %layer_all.1 = (bf16[256,768]{1,0:T(8,128)(2,1)}, bf16[4,96,576]{2,1,0:T(8,128)(2,1)}, bf16[384,768]{1,0:T(8,128)(2,1)}, bf16[96,3072]{1,0:T(8,128)(2,1)}, bf16[...) custom-call(bf16[256,768]{1,0:T(8,128)(2,1)} %hid.1, bf16[96,2304]{1,0:T(8,128)(2,1)} %wq.1, ...), custom_call_target="tpu_custom_call" | custom-call | tf_op jit(solution)/shard_map/layer_all/pallas_call | solution.py:1226
  186.2 1.2 slice.24
  187.4 1.3 slice_bitcast_fusion
  188.7 1.4 slice_bitcast_fusion.1
  190.1 0.0 copy-start
  190.1 1.1 copy-done
  191.3 0.0 copy-start.1
  191.3 1.1 copy-done.1
  192.3 0.0 copy-start.2
  192.3 1.1 copy-done.2
  193.4 0.0 copy-start.3
  193.4 1.0 copy-done.3
  194.4 0.0 copy-start.4
  194.4 1.0 copy-done.4
  195.4 0.0 copy-start.5
  195.4 0.9 copy-done.5
  196.3 2.4 %finish_all.1 = (f32[96,2304]{1,0:T(8,128)}, f32[384,768]{1,0:T(8,128)}, f32[96,3072]{1,0:T(8,128)}, f32[96,768]{1,0:T(8,128)}, f32[256,768]{1,0:T(8,128)}, /*index=5*/bf16[256,768]{1,0:T(8,128)(2,1)}) custom-call(bf16[4,96,576]{2,1,0:T(8,128)(2,1)S(1)} %copy-done.3, bf16[384,768]{1,0:T(8,128)(2,1)S(1)} %copy-done.1, bf16[96,3072]{1,0:T(8,128)(2,1)S(1)} %copy-done.2, ...), custom_call_target="tpu_custom_call" | custom-call | tf_op jit(solution)/shard_map/finish_all/pallas_call | solution.py:1258
  (1 shorter events, 0.0 us)
Async XLA Ops:
  190.1 1.1 copy-start
  191.3 1.1 copy-start.1
  192.3 1.1 copy-start.2
  193.4 1.0 copy-start.3
  194.4 1.0 copy-start.4
  195.4 0.9 copy-start.5

commit v3 on v2

--- a/solution.py
+++ b/solution.py
@@ -411,60 +411,94 @@
 
 
 class Gather:
-    def __init__(self, wires, block, out, local_sem):
-        w = self.w = wires
-        self.out = out
-        self.half = block.shape[0] // 2
-        mine = self.at(w.me)
-        self.own = pltpu.make_async_copy(block, mine, local_sem)
-        self.own.start()
-        self.to_x = w.start(block, mine, w.xn)
-        self.to_y = w.start(block, mine, w.yn)
-        self.to_mate = w.start(block, mine, w.mate)
+    def __init__(self, wires, out, block=None, far=None):
+        self.w, self.out, self.far = wires, out, far
+        self.half = out.shape[2] // 2
+        self.block = self.at(wires.me) if block is None else block
+        self.made = []
 
     def at(self, who, *rows):
         if rows:
             return self.out.at[who // 2, who % 2, rows[0]]
         return self.out.at[who // 2, who % 2]
 
+    def start(self, where, who, *rows):
+        one = self.w.start(self.at(who, *rows), self.at(who, *rows), where)
+        self.made.append(one)
+        return one
+
+    def pass_on(self, who):
+        one = self.start(self.far, who)
+        return one
+
+    def begin(self):
+        w, mine = self.w, self.at(self.w.me)
+        self.to_x = w.start(self.block, mine, w.xn)
+        self.to_y = w.start(self.block, mine, w.yn)
+        self.to_mate = w.start(self.block, mine, w.mate)
+        self.made += [self.to_x, self.to_y, self.to_mate]
+
     def relay(self):
-        w, at, half = self.w, self.at, self.half
-        low, high = pl.ds(0, half), pl.ds(half, half)
+        w, half = self.w, self.half
         self.to_x.wait_recv()
-        self.x_on = w.start(at(w.xn, low), at(w.xn, low), w.yn)
-        self.x_mate = w.start(at(w.xn), at(w.xn), w.mate)
+        self.x_on = self.start(w.yn, w.xn, pl.ds(0, half))
+        if self.far is not None:
+            self.x_far = self.pass_on(w.xn)
+        self.x_mate = self.start(w.mate, w.xn)
         self.to_y.wait_recv()
-        self.y_on = w.start(at(w.yn, high), at(w.yn, high), w.xn)
-        self.y_mate = w.start(at(w.yn), at(w.yn), w.mate)
+        self.y_on = self.start(w.xn, w.yn, pl.ds(half, half))
+        if self.far is not None:
+            self.y_far = self.pass_on(w.yn)
+        self.y_mate = self.start(w.mate, w.yn)
 
     def finish(self):
-        w, at, half = self.w, self.at, self.half
-        low, high = pl.ds(0, half), pl.ds(half, half)
+        w, half = self.w, self.half
         self.x_on.wait_recv()
-        self.d_low = w.start(at(w.dn, low), at(w.dn, low), w.mate)
+        self.d_low = self.start(w.mate, w.dn, pl.ds(0, half))
         self.y_on.wait_recv()
-        self.d_high = w.start(at(w.dn, high), at(w.dn, high), w.mate)
+        self.d_high = self.start(w.mate, w.dn, pl.ds(half, half))
+        if self.far is not None:
+            self.d_far = self.pass_on(w.dn)
 
     def done(self):
         for made in (self.to_mate, self.x_mate, self.y_mate, self.d_low, self.d_high):
             made.wait_recv()
-        for made in (
-            self.to_x,
-            self.to_y,
-            self.to_mate,
-            self.x_on,
-            self.x_mate,
-            self.y_on,
-            self.y_mate,
-            self.d_low,
-            self.d_high,
-        ):
+        for made in self.made:
             made.wait_send()
-        self.own.wait()
+
+
+class Passed:
+    def __init__(self, wires, out, source):
+        self.w, self.source = wires, source
+        self.near = Gather(wires, out)
+        self.relays = []
+
+    def begin(self):
+        w = self.w
+        self.to_mate = self.near.start(w.mate, w.me)
+
+    def relay(self):
+        self.source.x_far.wait_recv()
+        self.relays.append(self.near.start(self.w.mate, self.w.xn))
+        self.source.y_far.wait_recv()
+        self.relays.append(self.near.start(self.w.mate, self.w.yn))
+
+    def finish(self):
+        self.source.d_far.wait_recv()
+        self.relays.append(self.near.start(self.w.mate, self.w.dn))
+
+    def done(self):
+        for made in [self.to_mate] + self.relays:
+            made.wait_recv()
+        for made in self.near.made:
+            made.wait_send()
 
 
 SPAN = 512
 AHEAD = 3
+LATE = 4
+PAIRED = ((0, 2), (1, 3), (5, 6))
+COMMON = (4, 7, 8)
 BAND = 32
 
 
@@ -567,32 +601,33 @@
     out = dst if out is None else out
     lead = dst.shape[0] if len(dst.shape) == 3 else 0
     rows = dst.shape[-2]
+    band = 48 if rows % 48 == 0 else 32 if rows % 32 == 0 else 16
+    steps = rows // band
 
     def go(index, carry):
         if lead:
-            at = (index // (rows // 16), pl.ds(pl.multiple_of((index % (rows // 16)) * 16, 16), 16))
+            at = (index // steps, pl.ds(pl.multiple_of((index % steps) * band, band), band))
         else:
-            at = (pl.ds(pl.multiple_of(index * 16, 16), 16),)
-        out[at] = (dst[at].astype(f32) + other[at].astype(f32)).astype(out.dtype)
+            at = (pl.ds(pl.multiple_of(index * band, band), band),)
+        out[at] = (dst[at] + other[at]).astype(out.dtype)
         return carry
 
-    lax.fori_loop(0, max(lead, 1) * (rows // 16), go, 0)
+    lax.fori_loop(0, max(lead, 1) * steps, go, 0)
 
 
 class Reduce:
-    def __init__(self, wires, full, pair, land, pick):
+    def __init__(self, wires, full, pair, land):
         self.w, self.full, self.pair, self.land = wires, full, pair, land
         self.half = pair.shape[1] // 2
-        self.pick = pick
         if full is not None:
-            self.meet = wires.copy(pick(full, 1 - wires.core), pair, wires.mate)
+            self.meet = wires.copy(full.at[:, 1 - wires.core], pair, wires.mate)
 
     def first(self):
         w, pair, land = self.w, self.pair, self.land
         low, high = pl.ds(0, self.half), pl.ds(self.half, self.half)
         if self.full is not None:
             self.meet.wait_recv()
-            add_into(pair, self.pick(self.full, w.core))
+            add_into(pair, self.full.at[:, w.core])
         self.x0 = w.start(pair.at[w.cd, low], land.at[1], w.xn)
         self.y0 = w.start(pair.at[w.cd, high], land.at[3], w.yn)
         self.x1 = w.start(pair.at[w.cx, low], land.at[0], w.xn)
@@ -727,9 +762,7 @@
     do_o,
     dh_o,
     small_o,
-    wo_s,
-    wi_s,
-    wb_s,
+    weights,
     names_s,
     wq_s,
     wq_a,
@@ -789,6 +822,24 @@
     rows_in = ff // PLANE // 128
     seg_row = 8 + rows_in
 
+    loads = [pltpu.make_async_copy(wo, weights.at[0, w.chip, core], loc.at[0])]
+    for slot in range(fold):
+        loads.append(
+            pltpu.make_async_copy(
+                wi.at[:, pl.ds(slot * width, width)], weights.at[1 + slot, w.chip, core], loc.at[1 + slot]
+            )
+        )
+    for slot in range(fold):
+        loads.append(
+            pltpu.make_async_copy(
+                wb.at[pl.ds(slot * part, part)],
+                weights.at[1 + fold + slot, w.chip, core],
+                loc.at[1 + fold + slot],
+            )
+        )
+    for one in loads:
+        one.start()
+
     barrier = pltpu.get_barrier_semaphore()
     for other in plane_others(me):
         pl.semaphore_signal(barrier, inc=1, device_id=other, device_id_type=MESH)
@@ -803,6 +854,8 @@
         pl.semaphore_signal(barrier, inc=1, device_id={"replica": 3 * (z // 2)}, device_id_type=MESH)
         pl.semaphore_signal(barrier, inc=1, device_id={"replica": 3 - z}, device_id_type=MESH)
 
+    odd = z % 2
+    far = {"replica": z + 1 - 2 * odd}
     for chip in range(CHIPS):
         for place, section in enumerate((1, 2, 0)):
             start = section * width + chip * wide
@@ -817,7 +870,9 @@
         pl.semaphore_wait(barrier, PLANE + 1)
 
     names_s[me] = small[...]
-    first = Gather(w, hid, hid_s, loc.at[0])
+    hid_s[w.chip, core] = hid[...]
+    first = Gather(w, hid_s, hid)
+    first.begin()
     wq_a[me] = wq_s[w.chip]
     q_mate = w.start(wq_s.at[w.chip], wq_a.at[me], w.mate)
     q_d = w.start(wq_s.at[w.cd], wq_a.at[me], w.dn)
@@ -829,10 +884,15 @@
     for came, source in ((q_x, w.xn), (q_y, w.yn), (q_d, w.dn)):
         came.wait_recv()
         q_on.append(w.start(wq_a.at[source], wq_a.at[source], w.mate))
-    rest = [
-        Gather(w, block, out, loc.at[1 + slot])
-        for slot, (block, out) in enumerate(((wo, wo_s), (wi, wi_s), (wb, wb_s)))
-    ]
+    for one in loads:
+        one.wait()
+    own_ids = [even + odd * (uneven - even) for even, uneven in PAIRED]
+    far_ids = [uneven + odd * (even - uneven) for even, uneven in PAIRED]
+    mine = [Gather(w, weights.at[one], far=far) for one in own_ids]
+    theirs = [Passed(w, weights.at[one], source) for one, source in zip(far_ids, mine)]
+    both = [Gather(w, weights.at[one]) for one in COMMON]
+    for one in mine + theirs:
+        one.begin()
     for made in smalls:
         made.wait_recv()
     for source in range(PLANE):
@@ -872,33 +932,43 @@
         return carry
 
     lax.fori_loop(0, CHIPS, project, 0)
-    rest[0].relay()
-
-    def one_block(turn_no, carry):
-        index = (
-            (turn_no == 0) * w.cd + (turn_no == 1) * w.cx + (turn_no == 2) * w.cy + (turn_no == 3) * w.chip
-        )
+    mine[0].relay()
+    ctx_made = []
+    for turn_no, (index, who) in enumerate(
+        ((w.cd, w.dn), (w.cx, w.xn), (w.cy, w.yn), (w.chip, None))
+    ):
         context, logs = attend(qt[index], kv_s, vt, segk, segq[2 * index + core], hd)
         ctx32[index] = context
-        ctx_s[index] = context.astype(bf16)
         log[index] = logs
-        return carry
-
-    lax.fori_loop(0, 2, one_block, 0)
-    c_d = w.start(ctx_s.at[w.cd], ctxt.at[w.chip], w.dn)
-    c_x = w.start(ctx_s.at[w.cx], ctxt.at[w.chip], w.xn)
-    rest[1].relay()
-    rest[0].finish()
-    lax.fori_loop(2, 4, one_block, 0)
-    c_y = w.start(ctx_s.at[w.cy], ctxt.at[w.chip], w.yn)
-    ctxt[w.chip] = ctx_s[w.chip]
-    rest[1].finish()
-    rest[2].relay()
-    rest[0].done()
-    for made in (c_d, c_x, c_y):
+        if who is None:
+            ctxt[w.chip] = context.astype(bf16)
+        else:
+            ctx_s[index] = context.astype(bf16)
+            ctx_made.append(w.start(ctx_s.at[index], ctxt.at[w.chip], who))
+        if turn_no == 0:
+            mine[1].relay()
+            mine[0].finish()
+            mine[2].relay()
+            for one in both:
+                one.begin()
+        if turn_no == 1:
+            mine[1].finish()
+            theirs[0].relay()
+            mine[2].finish()
+        if turn_no == 2:
+            theirs[0].finish()
+            both[0].relay()
+    both[1].relay()
+    theirs[1].relay()
+    both[0].finish()
+    both[2].relay()
+    theirs[1].finish()
+    for made in ctx_made:
         made.wait()
-
-    wo_v = wo_s[...].reshape(width, width)
+    theirs[0].done()
+    mine[0].done()
+
+    wo_v = weights[0].reshape(width, width)
     bo, g1, s1, bb, g2, s2 = (vector(names_s, row, part) for row in range(2, 8))
     tiny_s[...] = jnp.zeros_like(tiny_s)
     acc_s[...] = dot(turn(ctxt[...].reshape(width, tok)).astype(bf16), wo_v, 1, 0)
@@ -914,10 +984,12 @@
 
     each(tok, BAND, open_one, 0)
     lowt_s[...] = turn(low_s[...]).astype(bf16)
-    rest[1].done()
+    both[1].finish()
+    theirs[1].done()
+    mine[1].done()
+    both[0].done()
 
     def up(chunk, carry):
-        cols = pl.ds(pl.multiple_of(chunk * width, width), width)
         bias = jnp.concatenate(
             [
                 names_s[2 * chunk + side, 8 + row : 9 + row, :].astype(f32)
@@ -926,7 +998,7 @@
             ],
             axis=1,
         )
-        wide_s[...] = dot(low_s[...], wi_s[:, :, :, cols].reshape(width, width), 1, 0)
+        wide_s[...] = dot(low_s[...], weights[1 + chunk].reshape(width, width), 1, 0)
 
         def gelu(at, carry):
             pre = wide_s[at, :] + bias
@@ -941,11 +1013,19 @@
         return carry
 
     lax.fori_loop(0, fold, up, 0)
-    rest[2].finish()
-    rest[2].done()
+    both[2].finish()
+    theirs[2].relay()
+    theirs[2].finish()
+    for one in (mine[2], theirs[2], both[1], both[2]):
+        one.done()
+
+    def back_rows(chunk):
+        return jnp.concatenate(
+            [weights[1 + fold + row, chunk, side] for side in range(2) for row in range(fold)], axis=0
+        )
 
     def join_back(chunk, carry):
-        acc_s[...] += dot(act_s[chunk], wb_s[chunk].reshape(width, width), 1, 0)
+        acc_s[...] += dot(act_s[chunk], back_rows(chunk), 1, 0)
         return carry
 
     lax.fori_loop(0, fold, join_back, 0)
@@ -967,10 +1047,12 @@
 
     def down(chunk, carry):
         grad = grad_s[...]
-        wide_s[...] = dot(grad, wb_s[chunk].reshape(width, width), 1, 1)
-        wb_s[chunk] = (
-            dot(turn(act_s[chunk]).astype(bf16), grad, 1, 0).astype(bf16).reshape(2, ff // PLANE, width)
-        )
+        wide_s[...] = dot(grad, back_rows(chunk), 1, 1)
+        made = dot(turn(act_s[chunk]).astype(bf16), grad, 1, 0).astype(bf16)
+        for side in range(2):
+            for row in range(fold):
+                start = (side * fold + row) * part
+                weights[1 + fold + row, chunk, side] = made[start : start + part]
 
         def through(at, sums):
             d_pre = wide_s[at, :] * slope_s[chunk, at, :]
@@ -986,21 +1068,15 @@
 
     lax.fori_loop(0, fold, down, 0)
 
-    picks = []
-    for slot in range(wb.shape[0] // part):
-        at = pl.ds(slot * part, part)
-        picks.append((wb_s, lambda ref, core, at=at: ref.at[:, core, at], db_o.at[at]))
-    for slot in range(fold):
-        at = pl.ds(slot * width, width)
-        picks.append((wi_s, lambda ref, core, at=at: ref.at[:, core, :, at], di_o.at[:, at]))
-    picks.append((wo_s, lambda ref, core: ref.at[:, core], do_o))
+    picks = [(1 + fold + slot, db_o.at[pl.ds(slot * part, part)]) for slot in range(fold)]
+    picks += [(1 + slot, di_o.at[:, pl.ds(slot * width, width)]) for slot in range(fold)]
+    picks.append((0, do_o))
     count = len(picks)
     chunks = [
-        Reduce(w, full, pair.at[slot], land.at[slot], pick)
-        for slot, (full, pick, _) in enumerate(picks)
+        Reduce(w, weights.at[which], pair.at[slot], land.at[slot]) for slot, (which, _) in enumerate(picks)
     ]
     lines = [
-        Line(w, z, part_s.at[slot], z_land.at[slot], out) for slot, (_, _, out) in enumerate(picks)
+        Line(w, z, part_s.at[slot], z_land.at[slot], out) for slot, (_, out) in enumerate(picks)
     ]
     for one in chunks[:AHEAD]:
         one.meet.start()
@@ -1019,16 +1095,15 @@
         if 0 <= now - 2 < count:
             chunks[now - 2].third(part_s.at[now - 2])
             lines[now - 2].first()
-        if 0 <= now - 3 < count:
-            lines[now - 3].second()
-        if 0 <= now - 4 < count:
-            lines[now - 4].third()
+        if 0 <= now - LATE < count:
+            lines[now - LATE].second()
+        if 0 <= now - 2 * LATE + 2 < count:
+            lines[now - 2 * LATE + 2].third()
 
     for chunk in range(fold):
-        cols = slice(chunk * width, (chunk + 1) * width)
         d_low = act_s[chunk]
-        acc_s[...] += dot(d_low, wi_s[:, :, :, cols].reshape(width, width), 1, 1)
-        wi_s[:, :, :, cols] = dot(lowt_s[...], d_low, 1, 0).astype(bf16).reshape(CHIPS, 2, part, width)
+        acc_s[...] += dot(d_low, weights[1 + chunk].reshape(width, width), 1, 1)
+        weights[1 + chunk] = dot(lowt_s[...], d_low, 1, 0).astype(bf16).reshape(CHIPS, 2, part, width)
         tick()
 
     def finish(at, sums):
@@ -1041,13 +1116,13 @@
 
     sums = each(tok, BAND, finish, (zero, zero, zero))
     grad = grad_s[...]
-    ctx_s[...] = dot(wo_s[...].reshape(width, width), grad, 1, 1).astype(bf16).reshape(CHIPS, wide, tok)
+    ctx_s[...] = dot(weights[0].reshape(width, width), grad, 1, 1).astype(bf16).reshape(CHIPS, wide, tok)
     dctx_made = [
         w.start(ctx_s.at[chip], dctx_s.at[w.chip], who)
         for chip, who in ((w.cx, w.xn), (w.cy, w.yn), (w.cd, w.dn))
     ]
     dctx_s[w.chip] = ctx_s[w.chip]
-    wo_s[...] = dot(ctxt[...].reshape(width, tok), grad, 1, 0).astype(bf16).reshape(CHIPS, 2, part, width)
+    weights[0] = dot(ctxt[...].reshape(width, tok), grad, 1, 0).astype(bf16).reshape(CHIPS, 2, part, width)
     for row, value in zip((2, 3, 4), sums):
         put_vector(tiny_s, row, settle(value), part)
     tick()
@@ -1104,7 +1179,7 @@
     ]
     s_land[me] = tiny_s[me]
     dh_s = act_s
-    hidden = Reduce(w, None, dh_s, dh_land, None)
+    hidden = Reduce(w, None, dh_s, dh_land)
 
     q_meet.wait_recv()
     add_into(q_pair, gq_s.at[:, core])
@@ -1141,7 +1216,7 @@
     q_lines[3].second()
     q_lines[2].third()
     hidden.second()
-    while ticks < count + 4:
+    while ticks < count + 2 * LATE - 2:
         tick()
     s_line.third()
     q_lines[3].third()
@@ -1178,9 +1253,7 @@
     pairs = (CHIPS, 2)
     heads_block = (CHIPS, wide, tok)
     scratch = [
-        VMEM(pairs + wo.shape, bf16),
-        VMEM(pairs + wi.shape, bf16),
-        VMEM(pairs + wb.shape, bf16),
+        VMEM((count,) + pairs + wo.shape, bf16),
         VMEM((PLANE, 16, 128), bf16),
         VMEM(q_block, bf16),
         VMEM((PLANE, part, 3 * wide), bf16),
@@ -1226,9 +1299,9 @@
     return pl.pallas_call(
         functools.partial(layer_kernel, hd=hd),
         out_shape=outs,
-        in_specs=[pl.BlockSpec(memory_space=VMEM)] * 7,
+        in_specs=[pl.BlockSpec(memory_space=space) for space in (VMEM, VMEM, VMEM, ANY, ANY, ANY, VMEM)],
         out_specs=[pl.BlockSpec(memory_space=VMEM)] * 7,
-        scratch_shapes=scratch + dma_sems(count * 10 + 100) + [pltpu.SemaphoreType.DMA((4,))],
+        scratch_shapes=scratch + dma_sems(count * 10 + 170) + [pltpu.SemaphoreType.DMA((count,))],
         compiler_params=pltpu.CompilerParams(
             collective_id=1, has_side_effects=True, vmem_limit_bytes=67043328
         ),
@@ -1236,33 +1309,54 @@
     )(hid, wq, small, wo, wi, wb, cot)
 
 
-def finish_kernel(dq, db, di, do, dh, out, q_o, b_o, i_o, o_o, h_o, out_o):
+def finish_kernel(*refs):
+    ins, rest = refs[:7], refs[7:]
+    dq_o, db_o, di_o, do_o, dh_o, out_o, qv_o, bi_o = rest[:8]
+    vectors, copies, sems = rest[8:14], rest[14:21], rest[21]
+    made = [
+        pltpu.make_async_copy(one, copy, sems.at[slot]) for slot, (one, copy) in enumerate(zip(ins, copies))
+    ]
+    for one in made:
+        one.start()
+    dq, db, di, do, dh, out, tiny = copies
     wide = dq.shape[2] // 3
     width = dh.shape[1]
+    part = do.shape[0]
+    made[0].wait()
     for chip in range(CHIPS):
         for place, section in enumerate((1, 2, 0)):
             start = section * width + chip * wide
-            q_o[:, start : start + wide] = dq[chip, :, place * wide : (place + 1) * wide].astype(f32)
-    b_o[...] = db[...].astype(f32)
-    i_o[...] = di[...].astype(f32)
-    o_o[...] = do[...].astype(f32)
-    h_o[...] = dh[...]
+            dq_o[:, start : start + wide] = dq[chip, :, place * wide : (place + 1) * wide].astype(f32)
+    for one in made[1:]:
+        one.wait()
+    db_o[...] = db[...].astype(f32)
+    di_o[...] = di[...].astype(f32)
+    do_o[...] = do[...].astype(f32)
+    dh_o[...] = dh[...]
     out_o[...] = out[...]
-
-
-def finish_all(dq, db, di, do, dh, out):
+    qv_o[...] = tiny[0:2, :part]
+    for row, one in enumerate(vectors):
+        one[...] = tiny[2 + row : 3 + row, :part]
+    lines = bi_o.shape[1] // 128
+    bi_o[...] = jnp.concatenate([tiny[8 + row : 9 + row, :] for row in range(lines)], axis=1)
+
+
+def finish_all(dq, db, di, do, dh, out, tiny):
     part, wide = dq.shape[1:]
     shape = jax.ShapeDtypeStruct
+    ins = (dq, db, di, do, dh, out, tiny)
     outs = [shape((part, CHIPS * wide), f32)] + [shape(one.shape, f32) for one in (db, di, do, dh)]
-    outs.append(shape(out.shape, out.dtype))
+    outs += [shape(out.shape, out.dtype), shape((2, part), f32), shape((1, db.shape[0]), f32)]
+    outs += [shape((1, part), f32)] * 6
     return pl.pallas_call(
         finish_kernel,
         out_shape=outs,
-        in_specs=[pl.BlockSpec(memory_space=VMEM)] * 6,
-        out_specs=[pl.BlockSpec(memory_space=VMEM)] * 6,
-        compiler_params=pltpu.CompilerParams(vmem_limit_bytes=32 << 20),
+        in_specs=[pl.BlockSpec(memory_space=ANY)] * 7,
+        out_specs=[pl.BlockSpec(memory_space=VMEM)] * 14,
+        scratch_shapes=[VMEM(one.shape, one.dtype) for one in ins] + [pltpu.SemaphoreType.DMA((7,))],
+        compiler_params=pltpu.CompilerParams(vmem_limit_bytes=60 << 20),
         name="finish_all",
-    )(dq, db, di, do, dh, out)
+    )(*ins)
 
 
 def fast_body(
@@ -1302,22 +1396,25 @@
     output, dq, db, di, do, dh, tiny = layer_all(
         hidden, w_qkv, small, w_out, w_in, w_back, cotangent, hd
     )
-    g_qkv, g_back, g_in, g_out, d_hidden, output = finish_all(dq, db, di, do, dh, output)
+    g_qkv, g_back, g_in, g_out, d_hidden, output, g_qv, g_bin, *vectors = finish_all(
+        dq, db, di, do, dh, output, tiny
+    )
+    g_bout, g_gain1, g_shift1, g_bback, g_gain2, g_shift2 = (one.reshape(part) for one in vectors)
     return (
         output,
         d_hidden,
         g_qkv,
-        tiny[0:2, :part],
+        g_qv,
         g_out,
-        tiny[2, :part],
-        tiny[3, :part],
-        tiny[4, :part],
+        g_bout,
+        g_gain1,
+        g_shift1,
         g_in,
-        tiny[8 : 8 + lines].reshape(ff // PLANE),
+        g_bin.reshape(ff // PLANE),
         g_back,
-        tiny[5, :part],
-        tiny[6, :part],
-        tiny[7, :part],
+        g_bback,
+        g_gain2,
+        g_shift2,
     )
 
 

time: 199 us -> 187 us (0.940)
  local copies, waits for them, and re-layouts: 11 us -> 0.86 us
  Pallas kernels: 185 us -> 182 us
    unnamed x12 -> x0, local copies, waits for them, and re-layouts: 6.19 us -> none
    pallas_call x1, Pallas kernels: 183 us -> 177 us  [layer_all(): pl.pallas_call(functools.partial(layer_kernel, hd=hd), out_shape=outs, in...]
where the time goes in v3:
time: 187 us; the launch traced here: 186 us
  Pallas kernels  182 us (97%)
  other arithmetic  3.28 us (2%)
    pallas_call x1, Pallas kernels, layer_all(): pl.pallas_call(functools.partial(layer_kernel, hd=hd), out_shape=outs, in...  177 us
    pallas_call x1, Pallas kernels, finish_all(): pl.pallas_call(finish_kernel, out_shape=outs, in_specs=[pl.BlockSpec(memo...  4.14 us

profile of v3, /device:TPU:0, one launch (start us, length us, event | category | flops | bytes accessed | tf_op | source)
XLA Modules:
  0.0 186.4 jit_solution(12544614525449942822)
XLA Ops:
  0.6 0.7 convert_bitcast_fusion
  1.3 0.1 pad.8.clone
  1.4 0.8 concatenate.6
  2.2 1.3 fusion.3.small
  3.5 177.4 %layer_all.1 = (bf16[256,768]{1,0:T(8,128)(2,1)}, bf16[4,96,576]{2,1,0:T(8,128)(2,1)}, bf16[384,768]{1,0:T(8,128)(2,1)}, bf16[96,3072]{1,0:T(8,128)(2,1)}, bf16[...) custom-call(bf16[256,768]{1,0:T(8,128)(2,1)} %hid.1, bf16[96,2304]{1,0:T(8,128)(2,1)} %wq.1, ...), custom_call_target="tpu_custom_call" | custom-call | tf_op jit(solution)/shard_map/layer_all/pallas_call | solution.py:1299
  181.0 4.1 %finish_all.1 = (f32[96,2304]{1,0:T(8,128)}, f32[384,768]{1,0:T(8,128)}, f32[96,3072]{1,0:T(8,128)}, f32[96,768]{1,0:T(8,128)}, f32[256,768]{1,0:T(8,128)}, /*in...) custom-call(bf16[4,96,576]{2,1,0:T(8,128)(2,1)} %get-tuple-element.3, ...), custom_call_target="tpu_custom_call" | custom-call | tf_op jit(solution)/shard_map/finish_all/pallas_call | solution.py:1351
  185.1 1.3 reduce
  (1 shorter events, 0.0 us)

commit v4 on v3

--- a/solution.py
+++ b/solution.py
@@ -416,6 +416,7 @@
         self.half = out.shape[2] // 2
         self.block = self.at(wires.me) if block is None else block
         self.made = []
+        self.came = set()
 
     def at(self, who, *rows):
         if rows:
@@ -460,9 +461,14 @@
         if self.far is not None:
             self.d_far = self.pass_on(w.dn)
 
+    def took(self, *names):
+        for name in names:
+            if name not in self.came:
+                self.came.add(name)
+                getattr(self, name).wait_recv()
+
     def done(self):
-        for made in (self.to_mate, self.x_mate, self.y_mate, self.d_low, self.d_high):
-            made.wait_recv()
+        self.took("to_mate", "x_mate", "y_mate", "d_low", "d_high")
         for made in self.made:
             made.wait_send()
 
@@ -495,10 +501,21 @@
 
 
 SPAN = 512
-AHEAD = 3
-LATE = 4
-PAIRED = ((0, 2), (1, 3), (5, 6))
-COMMON = (4, 7, 8)
+PLAN_DOWN = ((), ("F0",), ("F1",), ("S0", "F2"))
+PLAN_OPEN = ("S1", "T0")
+PLAN_IN = (("M4",), ("M5", "F3"), ("M6", "S2", "T1"), ("M7",), ("M8", "Y0"))
+PLAN_BACK = (
+    ("F4", "S3", "T2", "Y1", "Z0"),
+    ("F5", "S4", "T3", "Y2", "Z1"),
+    ("F6", "S5", "T4", "Y3", "Z2"),
+    ("F7", "S6", "T5", "Y4", "Z3"),
+)
+PLAN_MEET = ("F8", "S7", "T6", "Y5", "Z4")
+PLAN_GRAD = ("S8", "T7", "Y6", "Z5")
+PLAN_SENT = ("Z6",)
+PLAN_END = (("T8", "Y7"), ("Z7",), ("Y8",), ("Z8",))
+PAIRED = ((0, 2), (1, 3))
+COMMON = (4, 5, 6, 7, 8)
 BAND = 32
 
 
@@ -779,6 +796,7 @@
     ctx_s,
     ctxt,
     acc_s,
+    bias_s,
     unit_s,
     scale_s,
     low_s,
@@ -826,7 +844,7 @@
     for slot in range(fold):
         loads.append(
             pltpu.make_async_copy(
-                wi.at[:, pl.ds(slot * width, width)], weights.at[1 + slot, w.chip, core], loc.at[1 + slot]
+                wi.at[:, pl.ds(slot * width, width)], pair.at[0, slot], loc.at[1 + slot]
             )
         )
     for slot in range(fold):
@@ -870,29 +888,36 @@
         pl.semaphore_wait(barrier, PLANE + 1)
 
     names_s[me] = small[...]
-    hid_s[w.chip, core] = hid[...]
-    first = Gather(w, hid_s, hid)
-    first.begin()
+    smalls = [w.start(small, names_s.at[me], (me + step) % PLANE) for step in range(1, PLANE)]
     wq_a[me] = wq_s[w.chip]
     q_mate = w.start(wq_s.at[w.chip], wq_a.at[me], w.mate)
     q_d = w.start(wq_s.at[w.cd], wq_a.at[me], w.dn)
     q_x = w.start(wq_s.at[w.cx], wq_a.at[me], w.xn)
     q_y = w.start(wq_s.at[w.cy], wq_a.at[me], w.yn)
-    smalls = [w.start(small, names_s.at[me], (me + step) % PLANE) for step in range(1, PLANE)]
-    first.relay()
-    q_on = []
-    for came, source in ((q_x, w.xn), (q_y, w.yn), (q_d, w.dn)):
-        came.wait_recv()
-        q_on.append(w.start(wq_a.at[source], wq_a.at[source], w.mate))
+    hid_s[w.chip, core] = hid[...]
+    first = Gather(w, hid_s, hid)
+    first.begin()
     for one in loads:
         one.wait()
+    per = PLANE // fold
+    for chunk in range(fold):
+        weights[1 + chunk, w.chip, core] = jnp.concatenate(
+            [
+                pair[0, shard // per, :, start : start + part]
+                for shard in range(PLANE)
+                for start in [(shard % per) * fold * part + chunk * part]
+            ],
+            axis=1,
+        )
     own_ids = [even + odd * (uneven - even) for even, uneven in PAIRED]
     far_ids = [uneven + odd * (even - uneven) for even, uneven in PAIRED]
     mine = [Gather(w, weights.at[one], far=far) for one in own_ids]
     theirs = [Passed(w, weights.at[one], source) for one, source in zip(far_ids, mine)]
     both = [Gather(w, weights.at[one]) for one in COMMON]
-    for one in mine + theirs:
-        one.begin()
+    q_on = []
+    for came, source in ((q_x, w.xn), (q_y, w.yn), (q_d, w.dn)):
+        came.wait_recv()
+        q_on.append(w.start(wq_a.at[source], wq_a.at[source], w.mate))
     for made in smalls:
         made.wait_recv()
     for source in range(PLANE):
@@ -901,22 +926,30 @@
         for one in range(tok // 128):
             at = source * tok + one * 128
             segk[at : at + 128, :] = jnp.broadcast_to(ids[one : one + 1], (128, 128)).T
-    first.finish()
-    for made in [q_mate] + q_on:
-        made.wait_recv()
-    first.done()
-
     names = [names_s[2 * w.chip + side].astype(f32).T for side in range(2)]
     bias_q = jnp.concatenate([one[:part, 0:1] for one in names], axis=0)
     bias_v = jnp.concatenate([one[:part, 1:2] for one in names], axis=0)
-
-    def project(index, carry):
-        for mine in (True, False):
-            side = core if mine else 1 - core
+    spread = [
+        jnp.concatenate(
+            [names_s[source, 8 + row : 9 + row, :].astype(f32) for row in range(rows_in)], axis=1
+        )
+        for source in range(PLANE)
+    ]
+    for chunk in range(fold):
+        bias_s[chunk] = jnp.concatenate(
+            [one[:, chunk * part : (chunk + 1) * part] for one in spread], axis=1
+        )
+    for made in [q_mate] + q_on:
+        made.wait_recv()
+
+    def project(turn_no, carry):
+        index = pick_turn(turn_no)
+        for own in (True, False):
+            side = core if own else 1 - core
             block = hid_s[index, side]
             weight = wq_a[...].reshape(width, 3 * wide)
             rows = pl.ds(pl.multiple_of((2 * index + side) * tok, tok), tok)
-            kv = dot(block, weight if mine else weight[:, : 2 * wide], 1, 0)
+            kv = dot(block, weight if own else weight[:, : 2 * wide], 1, 0)
             kvt = kv.T
             low_v = (kvt[wide : 2 * wide] + bias_v).astype(bf16)
             kt[:, rows] = kvt[:wide].astype(bf16)
@@ -925,14 +958,32 @@
             for head in range(heads):
                 cols = slice(head * hd, (head + 1) * hd)
                 kv_s[head, rows, :] = jnp.concatenate([kv[:, cols], back[:, cols]], axis=1).astype(bf16)
-            if mine:
+            if own:
                 query = kvt[2 * wide :] + bias_q
                 qt[index] = (query.astype(bf16).astype(f32) * scale_factor).astype(bf16)
                 hidt[index] = turn(block).astype(bf16)
         return carry
 
-    lax.fori_loop(0, CHIPS, project, 0)
+    def pick_turn(turn_no):
+        return (
+            (turn_no == 0) * w.chip + (turn_no == 1) * w.cx + (turn_no == 2) * w.cy + (turn_no == 3) * w.cd
+        )
+
+    first.took("to_mate")
+    lax.fori_loop(0, 1, project, 0)
+    first.relay()
+    for one in mine + theirs:
+        one.begin()
+    both[0].begin()
+    first.took("x_mate", "y_mate")
+    lax.fori_loop(1, 3, project, 0)
+    first.finish()
     mine[0].relay()
+    first.took("d_low", "d_high")
+    lax.fori_loop(3, 4, project, 0)
+    first.done()
+    both[1].begin()
+    mine[1].relay()
     ctx_made = []
     for turn_no, (index, who) in enumerate(
         ((w.cd, w.dn), (w.cx, w.xn), (w.cy, w.yn), (w.chip, None))
@@ -946,23 +997,22 @@
             ctx_s[index] = context.astype(bf16)
             ctx_made.append(w.start(ctx_s.at[index], ctxt.at[w.chip], who))
         if turn_no == 0:
-            mine[1].relay()
+            both[2].begin()
+        if turn_no == 1:
+            both[0].relay()
+            both[3].begin()
             mine[0].finish()
-            mine[2].relay()
-            for one in both:
-                one.begin()
-        if turn_no == 1:
+        if turn_no == 2:
+            both[1].relay()
+            both[4].begin()
             mine[1].finish()
             theirs[0].relay()
-            mine[2].finish()
-        if turn_no == 2:
+        if turn_no == 3:
+            both[2].relay()
             theirs[0].finish()
-            both[0].relay()
-    both[1].relay()
-    theirs[1].relay()
-    both[0].finish()
-    both[2].relay()
-    theirs[1].finish()
+            both[0].finish()
+            theirs[1].relay()
+            both[3].relay()
     for made in ctx_made:
         made.wait()
     theirs[0].done()
@@ -984,20 +1034,16 @@
 
     each(tok, BAND, open_one, 0)
     lowt_s[...] = turn(low_s[...]).astype(bf16)
+    theirs[1].finish()
     both[1].finish()
+    both[4].relay()
+    both[2].finish()
     theirs[1].done()
     mine[1].done()
     both[0].done()
 
     def up(chunk, carry):
-        bias = jnp.concatenate(
-            [
-                names_s[2 * chunk + side, 8 + row : 9 + row, :].astype(f32)
-                for side in range(2)
-                for row in range(rows_in)
-            ],
-            axis=1,
-        )
+        bias = bias_s[chunk]
         wide_s[...] = dot(low_s[...], weights[1 + chunk].reshape(width, width), 1, 0)
 
         def gelu(at, carry):
@@ -1013,19 +1059,13 @@
         return carry
 
     lax.fori_loop(0, fold, up, 0)
-    both[2].finish()
-    theirs[2].relay()
-    theirs[2].finish()
-    for one in (mine[2], theirs[2], both[1], both[2]):
+    both[3].finish()
+    both[4].finish()
+    for one in both[1:]:
         one.done()
 
-    def back_rows(chunk):
-        return jnp.concatenate(
-            [weights[1 + fold + row, chunk, side] for side in range(2) for row in range(fold)], axis=0
-        )
-
     def join_back(chunk, carry):
-        acc_s[...] += dot(act_s[chunk], back_rows(chunk), 1, 0)
+        acc_s[...] += dot(act_s[chunk], weights[1 + fold + chunk].reshape(width, width), 1, 0)
         return carry
 
     lax.fori_loop(0, fold, join_back, 0)
@@ -1044,29 +1084,6 @@
     sums = each(tok, BAND, close, (zero, zero, zero))
     for row, value in zip((5, 6, 7), sums):
         put_vector(tiny_s, row, settle(value), part)
-
-    def down(chunk, carry):
-        grad = grad_s[...]
-        wide_s[...] = dot(grad, back_rows(chunk), 1, 1)
-        made = dot(turn(act_s[chunk]).astype(bf16), grad, 1, 0).astype(bf16)
-        for side in range(2):
-            for row in range(fold):
-                start = (side * fold + row) * part
-                weights[1 + fold + row, chunk, side] = made[start : start + part]
-
-        def through(at, sums):
-            d_pre = wide_s[at, :] * slope_s[chunk, at, :]
-            act_s[chunk, at, :] = d_pre.astype(bf16)
-            return sums + fold_rows(d_pre)
-
-        total = settle(each(tok, BAND, through, zero))
-        for side in range(2):
-            for row in range(rows_in):
-                start = (side * rows_in + row) * 128
-                tiny_s[2 * chunk + side, 8 + row : 9 + row, :] = total[:, start : start + 128]
-        return carry
-
-    lax.fori_loop(0, fold, down, 0)
 
     picks = [(1 + fold + slot, db_o.at[pl.ds(slot * part, part)]) for slot in range(fold)]
     picks += [(1 + slot, di_o.at[:, pl.ds(slot * width, width)]) for slot in range(fold)]
@@ -1078,33 +1095,43 @@
     lines = [
         Line(w, z, part_s.at[slot], z_land.at[slot], out) for slot, (_, out) in enumerate(picks)
     ]
-    for one in chunks[:AHEAD]:
-        one.meet.start()
-    ticks = 0
-
-    def tick():
-        nonlocal ticks
-        now = ticks
-        ticks += 1
-        if now + AHEAD < count:
-            chunks[now + AHEAD].meet.start()
-        if now < count:
-            chunks[now].first()
-        if 0 <= now - 1 < count:
-            chunks[now - 1].second()
-        if 0 <= now - 2 < count:
-            chunks[now - 2].third(part_s.at[now - 2])
-            lines[now - 2].first()
-        if 0 <= now - LATE < count:
-            lines[now - LATE].second()
-        if 0 <= now - 2 * LATE + 2 < count:
-            lines[now - 2 * LATE + 2].third()
+    left = [op + str(slot) for slot in range(count) for op in "MFSTYZ"]
+
+    def go(plan):
+        for name in plan:
+            left.remove(name)
+            slot = int(name[1:])
+            chunk, line = chunks[slot], lines[slot]
+            if name[0] == "M":
+                chunk.meet.start()
+            elif name[0] == "F":
+                chunk.first()
+            elif name[0] == "S":
+                chunk.second()
+            elif name[0] == "T":
+                chunk.third(part_s.at[slot])
+                line.first()
+            elif name[0] == "Y":
+                line.second()
+            else:
+                line.third()
 
     for chunk in range(fold):
-        d_low = act_s[chunk]
-        acc_s[...] += dot(d_low, weights[1 + chunk].reshape(width, width), 1, 1)
-        weights[1 + chunk] = dot(lowt_s[...], d_low, 1, 0).astype(bf16).reshape(CHIPS, 2, part, width)
-        tick()
+        grad = grad_s[...]
+        wide_s[...] = dot(grad, weights[1 + fold + chunk].reshape(width, width), 1, 1)
+        weights[1 + fold + chunk] = (
+            dot(turn(act_s[chunk]).astype(bf16), grad, 1, 0).astype(bf16).reshape(CHIPS, 2, part, width)
+        )
+        go(("M" + str(chunk),))
+
+        def through(at, sums):
+            d_pre = wide_s[at, :] * slope_s[chunk, at, :]
+            act_s[chunk, at, :] = d_pre.astype(bf16)
+            return sums + fold_rows(d_pre)
+
+        put_vector(tiny_s, 8 + chunk, settle(each(tok, BAND, through, zero)), part)
+        acc_s[...] += dot(act_s[chunk], weights[1 + chunk].reshape(width, width), 1, 1)
+        go(PLAN_DOWN[chunk])
 
     def finish(at, sums):
         unit = unit_s[at, :]
@@ -1122,10 +1149,14 @@
         for chip, who in ((w.cx, w.xn), (w.cy, w.yn), (w.cd, w.dn))
     ]
     dctx_s[w.chip] = ctx_s[w.chip]
+    go(PLAN_OPEN)
+    for chunk in range(fold):
+        weights[1 + chunk] = dot(lowt_s[...], act_s[chunk], 1, 0).astype(bf16).reshape(CHIPS, 2, part, width)
+        go(PLAN_IN[chunk])
     weights[0] = dot(ctxt[...].reshape(width, tok), grad, 1, 0).astype(bf16).reshape(CHIPS, 2, part, width)
     for row, value in zip((2, 3, 4), sums):
         put_vector(tiny_s, row, settle(value), part)
-    tick()
+    go(PLAN_IN[fold])
 
     dq_s = slope_s.at[:, 0:wide, 0:tok]
     dkv_a[...] = jnp.zeros_like(dkv_a)
@@ -1141,7 +1172,7 @@
         dq_s[index] = attend_back(
             qt[index], dt, log[index], delta, kv_s, kt, segk, segq[2 * index + core], dkv_a, 0, steps, hd
         )
-        tick()
+        go(PLAN_BACK[turn_no])
 
     dkv_s = hid_s.at[:, 0, :, 0 : 2 * wide]
     dkv_land = hid_s.at[:, 1, :, 0 : 2 * wide]
@@ -1153,7 +1184,7 @@
 
     lax.fori_loop(0, CHIPS, away, 0)
     meet = w.start(dkv_s, dkv_land, w.mate)
-    tick()
+    go(PLAN_MEET)
     meet.wait_recv()
 
     def join(index, sums):
@@ -1169,6 +1200,7 @@
         total = sum(dot(hidt[index, at, :], dqkv_s[index], 1, 0) for index in range(CHIPS))
         gq_s[2 * half : 2 * half + 2] = total.astype(bf16).reshape(2, 2, part, 3 * wide)
     q_meet = w.start(gq_s.at[:, 1 - core], q_pair, w.mate)
+    go(PLAN_GRAD)
     for side in range(2):
         slot = 2 * w.chip + side
         tiny_s[slot, 0:1, :part] = sums[:, 2 * wide + side * part : 2 * wide + (side + 1) * part]
@@ -1188,10 +1220,15 @@
         for chip, who in ((w.cx, w.xn), (w.cy, w.yn), (w.cd, w.dn))
     ]
     q_all[w.chip] = q_pair[w.chip]
+    halves = [pl.ds(0, part // 2), pl.ds(part // 2, part // 2)]
     q_lines = [
-        Line(w, z, q_all.at[chip], zq_land.at[chip], dq_o.at[chip]) for chip in (w.chip, w.cx, w.cy, w.cd)
+        Line(w, z, q_all.at[chip, rows], zq_land.at[chip, :, rows], dq_o.at[chip, rows])
+        for chip in (w.chip, w.cx, w.cy, w.cd)
+        for rows in halves
     ]
     q_lines[0].first()
+    q_lines[1].first()
+    go(PLAN_SENT)
 
     def input_grad(index, carry):
         dh_s[index] = dot(dqkv_s[index], wq_a[...].reshape(width, 3 * wide), 1, 1).astype(bf16)
@@ -1199,27 +1236,32 @@
 
     lax.fori_loop(0, CHIPS, input_grad, 0)
     hidden.first()
-    tick()
     for one in tinies:
         one.wait_recv()
     s_sum[...] = jnp.sum(s_land[...], axis=0)
     s_line = Line(w, z, s_sum, zs_land, small_o)
     s_line.first()
+    go(PLAN_END[0])
     for slot in (1, 2, 3):
         q_made[slot - 1].wait_recv()
-        q_lines[slot].first()
-        q_lines[slot - 1].second()
+        for half in range(2):
+            q_lines[2 * slot + half].first()
+        for half in range(2):
+            q_lines[2 * slot - 2 + half].second()
         if slot > 1:
-            q_lines[slot - 2].third()
-    tick()
+            for half in range(2):
+                q_lines[2 * slot - 4 + half].third()
+        go(PLAN_END[slot])
     s_line.second()
-    q_lines[3].second()
-    q_lines[2].third()
+    q_lines[4].third()
+    q_lines[6].second()
+    q_lines[5].third()
+    q_lines[7].second()
     hidden.second()
-    while ticks < count + 2 * LATE - 2:
-        tick()
+    go(tuple(left))
     s_line.third()
-    q_lines[3].third()
+    q_lines[6].third()
+    q_lines[7].third()
     hidden.third(dh_o)
     for one in [q_mate, q_x, q_y, q_d] + q_on + smalls + tinies + q_made + [q_meet, meet] + dctx_made:
         one.wait_send()
@@ -1270,6 +1312,7 @@
         VMEM(heads_block, bf16),
         VMEM(heads_block, bf16),
         VMEM((tok, width), f32),
+        VMEM((fold, 1, width), f32),
         VMEM((tok, width), f32),
         VMEM((tok, 128), f32),
         VMEM((tok, width), bf16),
@@ -1301,7 +1344,7 @@
         out_shape=outs,
         in_specs=[pl.BlockSpec(memory_space=space) for space in (VMEM, VMEM, VMEM, ANY, ANY, ANY, VMEM)],
         out_specs=[pl.BlockSpec(memory_space=VMEM)] * 7,
-        scratch_shapes=scratch + dma_sems(count * 10 + 170) + [pltpu.SemaphoreType.DMA((count,))],
+        scratch_shapes=scratch + dma_sems(count * 10 + 190) + [pltpu.SemaphoreType.DMA((count,))],
         compiler_params=pltpu.CompilerParams(
             collective_id=1, has_side_effects=True, vmem_limit_bytes=67043328
         ),
@@ -1330,15 +1373,18 @@
     for one in made[1:]:
         one.wait()
     db_o[...] = db[...].astype(f32)
-    di_o[...] = di[...].astype(f32)
+    fold = di.shape[1] // width
+    for chunk in range(fold):
+        for shard in range(PLANE):
+            to, start = (shard * fold + chunk) * part, chunk * width + shard * part
+            di_o[:, to : to + part] = di[:, start : start + part].astype(f32)
     do_o[...] = do[...].astype(f32)
     dh_o[...] = dh[...]
     out_o[...] = out[...]
     qv_o[...] = tiny[0:2, :part]
     for row, one in enumerate(vectors):
         one[...] = tiny[2 + row : 3 + row, :part]
-    lines = bi_o.shape[1] // 128
-    bi_o[...] = jnp.concatenate([tiny[8 + row : 9 + row, :] for row in range(lines)], axis=1)
+    bi_o[...] = jnp.concatenate([tiny[8 + row : 9 + row, :part] for row in range(fold)], axis=1)
 
 
 def finish_all(dq, db, di, do, dh, out, tiny):

time: 187 us -> 174 us (0.930)
  Pallas kernels: 182 us -> 169 us
    pallas_call x1, Pallas kernels: 177 us -> 165 us  [layer_all(): pl.pallas_call(functools.partial(layer_kernel, hd=hd), out_shape=outs, in...]
where the time goes in v4:
time: 174 us
  Pallas kernels  169 us (97%)
  other arithmetic  3.28 us (2%)
    pallas_call x1, Pallas kernels, layer_all(): pl.pallas_call(functools.partial(layer_kernel, hd=hd), out_shape=outs, in...  165 us
    pallas_call x1, Pallas kernels, finish_all(): pl.pallas_call(finish_kernel, out_shape=outs, in_specs=[pl.BlockSpec(memo...  4.12 us

profile of v4, /device:TPU:0, one launch (start us, length us, event | category | flops | bytes accessed | tf_op | source)
XLA Modules:
  0.0 174.0 jit_solution(16996105185567601182)
XLA Ops:
  0.6 0.7 convert_bitcast_fusion
  1.3 0.1 pad.8.clone
  1.4 0.8 concatenate.6
  2.2 1.3 fusion.3.small
  3.5 165.1 %layer_all.1 = (bf16[256,768]{1,0:T(8,128)(2,1)}, bf16[4,96,576]{2,1,0:T(8,128)(2,1)}, bf16[384,768]{1,0:T(8,128)(2,1)}, bf16[96,3072]{1,0:T(8,128)(2,1)}, bf16[...) custom-call(bf16[256,768]{1,0:T(8,128)(2,1)} %hid.1, bf16[96,2304]{1,0:T(8,128)(2,1)} %wq.1, ...), custom_call_target="tpu_custom_call" | custom-call | tf_op jit(solution)/shard_map/layer_all/pallas_call | solution.py:1342
  168.6 4.1 %finish_all.1 = (f32[96,2304]{1,0:T(8,128)}, f32[384,768]{1,0:T(8,128)}, f32[96,3072]{1,0:T(8,128)}, f32[96,768]{1,0:T(8,128)}, f32[256,768]{1,0:T(8,128)}, /*in...) custom-call(bf16[4,96,576]{2,1,0:T(8,128)(2,1)} %get-tuple-element.3, ...), custom_call_target="tpu_custom_call" | custom-call | tf_op jit(solution)/shard_map/finish_all/pallas_call | solution.py:1397
  172.7 1.3 reduce
  (1 shorter events, 0.0 us)

commit v5 on v4

--- a/solution.py
+++ b/solution.py
@@ -502,20 +502,20 @@
 
 SPAN = 512
 PLAN_DOWN = ((), ("F0",), ("F1",), ("S0", "F2"))
-PLAN_OPEN = ("S1", "T0")
-PLAN_IN = (("M4",), ("M5", "F3"), ("M6", "S2", "T1"), ("M7",), ("M8", "Y0"))
+PLAN_OPEN = ()
+PLAN_IN = (("M4",), ("M5", "S1"), ("M6", "F3"), ("M7", "S2", "T0"), ("M8", "F4"))
 PLAN_BACK = (
-    ("F4", "S3", "T2", "Y1", "Z0"),
-    ("F5", "S4", "T3", "Y2", "Z1"),
-    ("F6", "S5", "T4", "Y3", "Z2"),
-    ("F7", "S6", "T5", "Y4", "Z3"),
+    ("S3", "F5", "T1", "Y0"),
+    ("S4", "F6", "T2", "Y1", "Z0"),
+    ("S5", "F7", "T3", "Y2", "Z1"),
+    ("S6", "F8", "T4", "Y3", "Z2"),
 )
-PLAN_MEET = ("F8", "S7", "T6", "Y5", "Z4")
-PLAN_GRAD = ("S8", "T7", "Y6", "Z5")
-PLAN_SENT = ("Z6",)
-PLAN_END = (("T8", "Y7"), ("Z7",), ("Y8",), ("Z8",))
-PAIRED = ((0, 2), (1, 3))
-COMMON = (4, 5, 6, 7, 8)
+PLAN_MEET = ("S7", "T5", "Y4", "Z3")
+PLAN_GRAD = ("S8", "T6", "Y5", "Z4")
+PLAN_SENT = ("T7", "Y6", "Z5")
+PLAN_END = (("T8", "Y7", "Z6"), ("Z7",), ("Y8",), ("Z8",))
+PAIRED = ((0, 2), (1, 3), (5, 6))
+COMMON = (4, 7, 8)
 BAND = 32
 
 
@@ -767,7 +767,15 @@
 def layer_kernel(
     hid,
     wq,
-    small,
+    b_qv,
+    vec2,
+    vec3,
+    vec4,
+    vec5,
+    vec6,
+    vec7,
+    b_in,
+    ids_in,
     wo,
     wi,
     wb,
@@ -879,24 +887,19 @@
             start = section * width + chip * wide
             wq_s[chip, :, place * wide : (place + 1) * wide] = wq[:, start : start + wide]
 
-    @pl.when(edge)
-    def _():
-        pl.semaphore_wait(barrier, PLANE)
-
-    @pl.when(jnp.logical_not(edge))
-    def _():
-        pl.semaphore_wait(barrier, PLANE + 1)
-
-    names_s[me] = small[...]
-    smalls = [w.start(small, names_s.at[me], (me + step) % PLANE) for step in range(1, PLANE)]
+    s_sum[...] = jnp.zeros_like(s_sum)
+    s_sum[0:2, :part] = b_qv[...].astype(f32)
+    for row, one in enumerate((vec2, vec3, vec4, vec5, vec6, vec7)):
+        s_sum[2 + row : 3 + row, :part] = one[...].astype(f32).reshape(1, part)
+    flat = b_in[...].astype(f32).reshape(1, rows_in * 128)
+    for row in range(rows_in):
+        s_sum[8 + row : 9 + row, :] = flat[:, row * 128 : (row + 1) * 128]
+    flat = ids_in[...].astype(f32).reshape(1, tok)
+    for row in range(tok // 128):
+        s_sum[seg_row + row : seg_row + row + 1, :] = flat[:, row * 128 : (row + 1) * 128]
+    names_s[me] = s_sum[...].astype(bf16)
     wq_a[me] = wq_s[w.chip]
-    q_mate = w.start(wq_s.at[w.chip], wq_a.at[me], w.mate)
-    q_d = w.start(wq_s.at[w.cd], wq_a.at[me], w.dn)
-    q_x = w.start(wq_s.at[w.cx], wq_a.at[me], w.xn)
-    q_y = w.start(wq_s.at[w.cy], wq_a.at[me], w.yn)
     hid_s[w.chip, core] = hid[...]
-    first = Gather(w, hid_s, hid)
-    first.begin()
     for one in loads:
         one.wait()
     per = PLANE // fold
@@ -909,11 +912,30 @@
             ],
             axis=1,
         )
+
+    @pl.when(edge)
+    def _():
+        pl.semaphore_wait(barrier, PLANE)
+
+    @pl.when(jnp.logical_not(edge))
+    def _():
+        pl.semaphore_wait(barrier, PLANE + 1)
+
+    smalls = [
+        w.start(names_s.at[me], names_s.at[me], (me + step) % PLANE) for step in range(1, PLANE)
+    ]
+    q_mate = w.start(wq_s.at[w.chip], wq_a.at[me], w.mate)
+    q_d = w.start(wq_s.at[w.cd], wq_a.at[me], w.dn)
+    q_x = w.start(wq_s.at[w.cx], wq_a.at[me], w.xn)
+    q_y = w.start(wq_s.at[w.cy], wq_a.at[me], w.yn)
     own_ids = [even + odd * (uneven - even) for even, uneven in PAIRED]
     far_ids = [uneven + odd * (even - uneven) for even, uneven in PAIRED]
     mine = [Gather(w, weights.at[one], far=far) for one in own_ids]
     theirs = [Passed(w, weights.at[one], source) for one, source in zip(far_ids, mine)]
     both = [Gather(w, weights.at[one]) for one in COMMON]
+    first = Gather(w, hid_s)
+    mine[0].begin()
+    first.begin()
     q_on = []
     for came, source in ((q_x, w.xn), (q_y, w.yn), (q_d, w.dn)):
         came.wait_recv()
@@ -971,19 +993,21 @@
 
     first.took("to_mate")
     lax.fori_loop(0, 1, project, 0)
+    mine[0].relay()
     first.relay()
-    for one in mine + theirs:
+    for one in mine[1:] + theirs:
         one.begin()
     both[0].begin()
     first.took("x_mate", "y_mate")
     lax.fori_loop(1, 3, project, 0)
     first.finish()
-    mine[0].relay()
+    mine[0].finish()
+    mine[1].relay()
     first.took("d_low", "d_high")
     lax.fori_loop(3, 4, project, 0)
     first.done()
     both[1].begin()
-    mine[1].relay()
+    mine[2].relay()
     ctx_made = []
     for turn_no, (index, who) in enumerate(
         ((w.cd, w.dn), (w.cx, w.xn), (w.cy, w.yn), (w.chip, None))
@@ -997,22 +1021,20 @@
             ctx_s[index] = context.astype(bf16)
             ctx_made.append(w.start(ctx_s.at[index], ctxt.at[w.chip], who))
         if turn_no == 0:
+            mine[1].finish()
+            both[0].relay()
             both[2].begin()
         if turn_no == 1:
-            both[0].relay()
-            both[3].begin()
-            mine[0].finish()
+            theirs[0].relay()
+            mine[2].finish()
+            both[1].relay()
         if turn_no == 2:
-            both[1].relay()
-            both[4].begin()
-            mine[1].finish()
-            theirs[0].relay()
-        if turn_no == 3:
-            both[2].relay()
             theirs[0].finish()
             both[0].finish()
             theirs[1].relay()
-            both[3].relay()
+        if turn_no == 3:
+            both[2].relay()
+            both[1].finish()
     for made in ctx_made:
         made.wait()
     theirs[0].done()
@@ -1035,9 +1057,6 @@
     each(tok, BAND, open_one, 0)
     lowt_s[...] = turn(low_s[...]).astype(bf16)
     theirs[1].finish()
-    both[1].finish()
-    both[4].relay()
-    both[2].finish()
     theirs[1].done()
     mine[1].done()
     both[0].done()
@@ -1059,9 +1078,10 @@
         return carry
 
     lax.fori_loop(0, fold, up, 0)
-    both[3].finish()
-    both[4].finish()
-    for one in both[1:]:
+    theirs[2].relay()
+    both[2].finish()
+    theirs[2].finish()
+    for one in (mine[2], theirs[2], both[1], both[2]):
         one.done()
 
     def join_back(chunk, carry):
@@ -1272,7 +1292,7 @@
     dh_o[...] = (resid_s[...] + dh_o[...].astype(f32)).astype(dh_o.dtype)
 
 
-def layer_all(hid, wq, small, wo, wi, wb, cot, hd):
+def layer_all(hid, wq, vectors, wo, wi, wb, cot, hd):
     tok, width = hid.shape
     wide = width // CHIPS
     part = wq.shape[0]
@@ -1342,14 +1362,14 @@
     return pl.pallas_call(
         functools.partial(layer_kernel, hd=hd),
         out_shape=outs,
-        in_specs=[pl.BlockSpec(memory_space=space) for space in (VMEM, VMEM, VMEM, ANY, ANY, ANY, VMEM)],
+        in_specs=[pl.BlockSpec(memory_space=space) for space in [VMEM] * 11 + [ANY] * 3 + [VMEM]],
         out_specs=[pl.BlockSpec(memory_space=VMEM)] * 7,
         scratch_shapes=scratch + dma_sems(count * 10 + 190) + [pltpu.SemaphoreType.DMA((count,))],
         compiler_params=pltpu.CompilerParams(
             collective_id=1, has_side_effects=True, vmem_limit_bytes=67043328
         ),
         name="layer_all",
-    )(hid, wq, small, wo, wi, wb, cot)
+    )(hid, wq, *vectors, wo, wi, wb, cot)
 
 
 def finish_kernel(*refs):
@@ -1426,26 +1446,14 @@
     hd = width // HEADS
     part = w_qkv.shape[0]
     ff = w_in.shape[1]
-    lines = b_in.shape[0] // 128
-    narrow = jnp.concatenate(
-        [b_qv] + [one[None] for one in (b_out, gain1, shift1, b_back, gain2, shift2)], axis=0
-    )
-    small = jnp.concatenate(
-        [
-            jnp.pad(narrow, ((0, 0), (0, 128 - part))),
-            b_in.reshape(lines, 128),
-            segment_ids.astype(bf16).reshape(tok // 128, 128),
-            jnp.zeros((8 - lines - tok // 128, 128), bf16),
-        ],
-        axis=0,
-    )
+    vectors = (b_qv, b_out, gain1, shift1, b_back, gain2, shift2, b_in, segment_ids)
     output, dq, db, di, do, dh, tiny = layer_all(
-        hidden, w_qkv, small, w_out, w_in, w_back, cotangent, hd
-    )
-    g_qkv, g_back, g_in, g_out, d_hidden, output, g_qv, g_bin, *vectors = finish_all(
+        hidden, w_qkv, vectors, w_out, w_in, w_back, cotangent, hd
+    )
+    g_qkv, g_back, g_in, g_out, d_hidden, output, g_qv, g_bin, *sums = finish_all(
         dq, db, di, do, dh, output, tiny
     )
-    g_bout, g_gain1, g_shift1, g_bback, g_gain2, g_shift2 = (one.reshape(part) for one in vectors)
+    g_bout, g_gain1, g_shift1, g_bback, g_gain2, g_shift2 = (one.reshape(part) for one in sums)
     return (
         output,
         d_hidden,

time: 174 us -> 167 us (0.960)
  Pallas kernels: 169 us -> 165 us
  other arithmetic: 3.28 us -> 1.25 us
    pallas_call x1, Pallas kernels: 165 us -> 161 us  [layer_all(): pl.pallas_call(functools.partial(layer_kernel, hd=hd), out_shape=outs, in...]
where the time goes in v5:
time: 167 us
  Pallas kernels  165 us (99%)
    pallas_call x1, Pallas kernels, layer_all(): pl.pallas_call(functools.partial(layer_kernel, hd=hd), out_shape=outs, in...  161 us
    pallas_call x1, Pallas kernels, finish_all(): pl.pallas_call(finish_kernel, out_shape=outs, in_specs=[pl.BlockSpec(memo...  4.12 us

profile of v5, /device:TPU:0, one launch (start us, length us, event | category | flops | bytes accessed | tf_op | source)
XLA Modules:
  0.0 167.0 jit_solution(17810789602833899141)
XLA Ops:
  0.7 161.0 %layer_all.1 = (bf16[256,768]{1,0:T(8,128)(2,1)}, bf16[4,96,576]{2,1,0:T(8,128)(2,1)}, bf16[384,768]{1,0:T(8,128)(2,1)}, bf16[96,3072]{1,0:T(8,128)(2,1)}, bf16[...) custom-call(bf16[256,768]{1,0:T(8,128)(2,1)} %hid.1, bf16[96,2304]{1,0:T(8,128)(2,1)} %wq.1, ...), custom_call_target="tpu_custom_call" | custom-call | tf_op jit(solution)/shard_map/layer_all/pallas_call | solution.py:1362
  161.6 4.1 %finish_all.1 = (f32[96,2304]{1,0:T(8,128)}, f32[384,768]{1,0:T(8,128)}, f32[96,3072]{1,0:T(8,128)}, f32[96,768]{1,0:T(8,128)}, f32[256,768]{1,0:T(8,128)}, /*in...) custom-call(bf16[4,96,576]{2,1,0:T(8,128)(2,1)} %get-tuple-element.3, ...), custom_call_target="tpu_custom_call" | custom-call | tf_op jit(solution)/shard_map/finish_all/pallas_call | solution.py:1417
  165.8 1.3 reduce
